TPU v7x, 32 devices: a whole 2x2x4 slice. The times are simulated.
32 devices in a mesh: dp: 8 (over z, y), tensor: 4 (over x, core).
Axes of the slice: x: 2, y: 2, z: 4, core: 2. Of those that a mesh axis runs over, the one named last changes fastest.
Arguments:
- hidden_in: bfloat16 [24576, 768], P('dp'), may hold values from -6 to 6
- box_coords: int32 [4, 24576], P(None, 'dp'), may hold values from 0 to 1000
- page_lengths: int32 [48], P('dp'), may hold values from 40 to 512, as said below
- query_weight: bfloat16 [768, 768], P(None, 'tensor'), may hold values from -0.21875 to 0.21875
- query_bias: float32 [768], P('tensor'), may hold values from -3 to 3
- key_weight: bfloat16 [768, 768], P(None, 'tensor'), may hold values from -0.21875 to 0.21875
- value_weight: bfloat16 [768, 768], P(None, 'tensor'), may hold values from -0.21875 to 0.21875
- value_bias: float32 [768], P('tensor'), may hold values from -3 to 3
- box_weight: bfloat16 [768, 1536], P(None, 'tensor'), may hold values from -0.21875 to 0.21875
- box_bias: float32 [1536], P('tensor'), may hold values from -3 to 3
- output_weight: bfloat16 [768, 768], P('tensor'), may hold values from -0.875 to 0.875
- output_bias: float32 [768], replicated, may hold values from -3 to 3
- first_gain: float32 [768], replicated, may hold values from 0.25 to 1.75
- first_shift: float32 [768], replicated, may hold values from -3 to 3
- up_weight: bfloat16 [768, 3072], P(None, 'tensor'), may hold values from -0.21875 to 0.21875
- up_bias: float32 [3072], P('tensor'), may hold values from -3 to 3
- down_weight: bfloat16 [3072, 768], P('tensor'), may hold values from -0.109375 to 0.109375
- down_bias: float32 [768], replicated, may hold values from -3 to 3
- second_gain: float32 [768], replicated, may hold values from 0.25 to 1.75
- second_shift: float32 [768], replicated, may hold values from -3 to 3
- output_grad: bfloat16 [24576, 768], P(('dp', 'tensor')), may hold values from -6 to 6
Outputs:
- layer_out: bfloat16 [24576, 768], P(('dp', 'tensor'))
- input_grad: float32 [24576, 768], P(('dp', 'tensor'))
- query_weight_grad: float32 [768, 768], P(None, 'tensor')
- query_bias_grad: float32 [768], P('tensor')
- key_weight_grad: float32 [768, 768], P(None, 'tensor')
- value_weight_grad: float32 [768, 768], P(None, 'tensor')
- value_bias_grad: float32 [768], P('tensor')
- box_weight_grad: float32 [768, 1536], P(None, 'tensor')
- box_bias_grad: float32 [1536], P('tensor')
- output_weight_grad: float32 [768, 768], P('tensor')
- output_bias_grad: float32 [768], P('tensor')
- first_gain_grad: float32 [768], P('tensor')
- first_shift_grad: float32 [768], P('tensor')
- up_weight_grad: float32 [768, 3072], P(None, 'tensor')
- up_bias_grad: float32 [3072], P('tensor')
- down_weight_grad: float32 [3072, 768], P('tensor')
- down_bias_grad: float32 [768], P('tensor')
- second_gain_grad: float32 [768], P('tensor')
- second_shift_grad: float32 [768], P('tensor')
Inputs may be any that keep to these rules, and one draw needn't show every extreme that they name: Page p holds real tokens in its first page_lengths[p] slots; every draw has a page of 512 real tokens.
All inputs are finite; a program needn't handle non-finite values.
Results may differ from a plain program's by a relative error of at most 0.02.
Values may be sent and summed in bfloat16 or wider, within the bound.
A program may use at most 192 MiB of HBM per device.

v0:
```python
from functools import partial
import math

import jax
import jax.numpy as jnp
from jax import lax
from jax.sharding import PartitionSpec as P

HEAD = 64
FREQ = 16
POS = 128
PAGE = 512


EPS = 1e-05


def features(box_coords):
    rates = jnp.power(1000.0, -jnp.arange(FREQ, dtype=jnp.float32) / FREQ)
    angles = box_coords.astype(jnp.float32)[:, :, None] * rates[None, None, :]
    angles = jnp.transpose(angles, (1, 0, 2)).reshape(box_coords.shape[1], 4 * FREQ)
    return jnp.concatenate([jnp.cos(angles), jnp.sin(angles)], axis=1)


def mix_position(box_coeff, geometry):
    middle = POS // 2
    first_half = box_coeff[..., :middle]
    second_half = box_coeff[..., middle:]
    cosine = geometry[:, None, :middle]
    sine_part = geometry[:, None, middle:]
    return jnp.concatenate(
        [
            first_half * cosine + second_half * sine_part,
            first_half * sine_part - second_half * cosine,
        ],
        axis=-1,
    )


def masked(scores, page_length):
    is_valid = jnp.arange(PAGE, dtype=jnp.int32) < page_length
    return jnp.where(is_valid[None, None, :], scores, -1000000000.0)


def score_page(query_states, key_states, box_query, geometry, page_length):
    raw_scores = jnp.einsum(
        "qhd,khd->hqk", query_states, key_states, preferred_element_type=jnp.float32
    )
    raw_scores = raw_scores + jnp.einsum(
        "qhp,kp->hqk", box_query, geometry, preferred_element_type=jnp.float32
    )
    return masked(raw_scores * (1.0 / math.sqrt(HEAD)), page_length)


def page_forward(page_block):
    query_states, key_states, value_states, box_query, geometry, page_length = page_block
    scores = score_page(query_states, key_states, box_query, geometry, page_length)
    maxima = jnp.max(scores, axis=-1, keepdims=True)
    exponent = jnp.exp(scores - maxima)
    totals = jnp.sum(exponent, axis=-1, keepdims=True)
    weights = (exponent / totals).astype(jnp.bfloat16)
    context = jnp.einsum(
        "hqk,khd->qhd", weights, value_states, preferred_element_type=jnp.float32
    ).astype(jnp.bfloat16)
    return (context, maxima[..., 0] + jnp.log(totals[..., 0]))


def page_backward(page_block):
    (
        query_states,
        key_states,
        value_states,
        box_query,
        geometry,
        page_length,
        log_total,
        context_grad,
    ) = page_block
    scores = score_page(query_states, key_states, box_query, geometry, page_length)
    probability = jnp.exp(scores - log_total[..., None])
    value_grad = jnp.einsum(
        "hqk,qhd->khd",
        probability.astype(jnp.bfloat16),
        context_grad,
        preferred_element_type=jnp.float32,
    )
    prob_grad = jnp.einsum(
        "qhd,khd->hqk", context_grad, value_states, preferred_element_type=jnp.float32
    )
    score_grad = (
        probability * (prob_grad - jnp.sum(probability * prob_grad, axis=-1, keepdims=True))
    ).astype(jnp.bfloat16)
    factor = 1.0 / math.sqrt(HEAD)
    query_grad = (
        jnp.einsum("hqk,khd->qhd", score_grad, key_states, preferred_element_type=jnp.float32)
        * factor
    )
    key_grad = (
        jnp.einsum("hqk,qhd->khd", score_grad, query_states, preferred_element_type=jnp.float32)
        * factor
    )
    box_grad = (
        jnp.einsum("hqk,kp->qhp", score_grad, geometry, preferred_element_type=jnp.float32) * factor
    )
    return (
        query_grad.astype(jnp.bfloat16),
        key_grad.astype(jnp.bfloat16),
        value_grad.astype(jnp.bfloat16),
        box_grad,
    )


def position_back(box_grad, geometry):
    middle = POS // 2
    first_grad = box_grad[..., :middle]
    second_grad = box_grad[..., middle:]
    cosine = geometry[:, None, :middle]
    sine_part = geometry[:, None, middle:]
    return jnp.concatenate(
        [
            first_grad * cosine + second_grad * sine_part,
            first_grad * sine_part - second_grad * cosine,
        ],
        axis=-1,
    )


def normalize(total, gain, shift):
    row_mean = jnp.mean(total, axis=-1, keepdims=True)
    centred = total - row_mean
    inverse = lax.rsqrt(jnp.mean(centred * centred, axis=-1, keepdims=True) + EPS)
    scaled = centred * inverse
    return (scaled * gain + shift, scaled, inverse)


def norm_back(gradient, scaled, inverse, gain):
    weighted = gradient * gain
    result = inverse * (
        weighted
        - jnp.mean(weighted, axis=-1, keepdims=True)
        - scaled * jnp.mean(weighted * scaled, axis=-1, keepdims=True)
    )
    return (result, jnp.sum(gradient * scaled, axis=0), jnp.sum(gradient, axis=0))


def body(
    hidden_in,
    box_coords,
    page_lengths,
    query_weight,
    query_bias,
    key_weight,
    value_weight,
    value_bias,
    box_weight,
    box_bias,
    output_weight,
    output_bias,
    first_gain,
    first_shift,
    up_weight,
    up_bias,
    down_weight,
    down_bias,
    second_gain,
    second_shift,
    output_grad,
):
    tensor_ways = lax.axis_size("tensor")
    all_rows = hidden_in.shape[0]
    share_rows = all_rows // tensor_ways
    row_offset = lax.axis_index("tensor") * share_rows
    page_count = page_lengths.shape[0]
    local_heads = query_weight.shape[1] // HEAD
    geometry = features(box_coords).astype(jnp.bfloat16)
    geo_wide = geometry.astype(jnp.float32)
    query_states = (
        jnp.dot(hidden_in, query_weight, preferred_element_type=jnp.float32) + query_bias
    ).astype(jnp.bfloat16)
    key_states = jnp.dot(hidden_in, key_weight, preferred_element_type=jnp.float32).astype(
        jnp.bfloat16
    )
    value_states = (
        jnp.dot(hidden_in, value_weight, preferred_element_type=jnp.float32) + value_bias
    ).astype(jnp.bfloat16)
    box_coeff = (
        jnp.dot(hidden_in, box_weight, preferred_element_type=jnp.float32) + box_bias
    ).reshape(all_rows, local_heads, POS)
    box_query = mix_position(box_coeff, geo_wide).astype(jnp.bfloat16)

    def by_page(array, width):
        return array.reshape(page_count, PAGE, local_heads, width)

    page_blocks = (
        by_page(query_states, HEAD),
        by_page(key_states, HEAD),
        by_page(value_states, HEAD),
        by_page(box_query, POS),
        geometry.reshape(page_count, PAGE, POS),
        page_lengths,
    )
    context, log_total = lax.map(page_forward, page_blocks)
    context = context.reshape(all_rows, local_heads * HEAD)
    attn_whole = lax.psum(
        jnp.dot(context, output_weight, preferred_element_type=jnp.float32).astype(jnp.bfloat16),
        "tensor",
    ).astype(jnp.float32)
    first_whole, scaled_whole, inverse_whole = normalize(
        attn_whole + output_bias + hidden_in.astype(jnp.float32), first_gain, first_shift
    )
    first_full = first_whole.astype(jnp.bfloat16)
    first_share = lax.dynamic_slice_in_dim(first_whole, row_offset, share_rows, 0)
    first_scaled = lax.dynamic_slice_in_dim(scaled_whole, row_offset, share_rows, 0)
    first_inverse = lax.dynamic_slice_in_dim(inverse_whole, row_offset, share_rows, 0)
    pre_active = jnp.dot(first_full, up_weight, preferred_element_type=jnp.float32) + up_bias
    activated = jax.nn.gelu(pre_active, approximate=False).astype(jnp.bfloat16)
    ffn_whole = lax.psum(
        jnp.dot(activated, down_weight, preferred_element_type=jnp.float32).astype(jnp.bfloat16),
        "tensor",
    ).astype(jnp.float32)
    ffn_share = lax.dynamic_slice_in_dim(ffn_whole, row_offset, share_rows, 0)
    second, second_scaled, second_inverse = normalize(
        ffn_share + down_bias + first_share, second_gain, second_shift
    )
    layer_out = second.astype(jnp.bfloat16)
    second_grad, second_gain_grad, second_shift_grad = norm_back(
        output_grad.astype(jnp.float32), second_scaled, second_inverse, second_gain
    )
    down_bias_grad = jnp.sum(second_grad, axis=0)
    second_low = lax.all_gather(second_grad.astype(jnp.bfloat16), "tensor", axis=0, tiled=True)
    down_weight_grad = jnp.einsum(
        "tf,td->fd", activated, second_low, preferred_element_type=jnp.float32
    )
    active_grad = jnp.einsum(
        "td,fd->tf", second_low, down_weight, preferred_element_type=jnp.float32
    )
    gelu_back = jax.vjp(partial(jax.nn.gelu, approximate=False), pre_active)[1]
    upper_grad = gelu_back(active_grad)[0].astype(jnp.bfloat16)
    up_bias_grad = jnp.sum(upper_grad.astype(jnp.float32), axis=0)
    up_weight_grad = jnp.einsum(
        "td,tf->df", first_full, upper_grad, preferred_element_type=jnp.float32
    )
    first_grad = (
        lax.psum_scatter(
            jnp.einsum(
                "tf,df->td", upper_grad, up_weight, preferred_element_type=jnp.float32
            ).astype(jnp.bfloat16),
            "tensor",
            scatter_dimension=0,
            tiled=True,
        ).astype(jnp.float32)
        + second_grad
    )
    attn_grad, first_gain_grad, first_shift_grad = norm_back(
        first_grad, first_scaled, first_inverse, first_gain
    )
    output_bias_grad = jnp.sum(attn_grad, axis=0)
    attn_low = lax.all_gather(attn_grad.astype(jnp.bfloat16), "tensor", axis=0, tiled=True)
    output_weight_grad = jnp.einsum(
        "tc,td->cd", context, attn_low, preferred_element_type=jnp.float32
    )
    context_grad = jnp.einsum(
        "td,cd->tc", attn_low, output_weight, preferred_element_type=jnp.float32
    ).astype(jnp.bfloat16)
    query_grad, key_grad, value_grad, box_grad = lax.map(
        page_backward, page_blocks + (log_total, by_page(context_grad, HEAD))
    )
    query_grad = query_grad.reshape(all_rows, local_heads * HEAD)
    key_grad = key_grad.reshape(all_rows, local_heads * HEAD)
    value_grad = value_grad.reshape(all_rows, local_heads * HEAD)
    coeff_grad = (
        position_back(box_grad.reshape(all_rows, local_heads, POS), geo_wide)
        .reshape(all_rows, local_heads * POS)
        .astype(jnp.bfloat16)
    )
    query_weight_grad = jnp.einsum(
        "td,tc->dc", hidden_in, query_grad, preferred_element_type=jnp.float32
    )
    query_bias_grad = jnp.sum(query_grad.astype(jnp.float32), axis=0)
    key_weight_grad = jnp.einsum(
        "td,tc->dc", hidden_in, key_grad, preferred_element_type=jnp.float32
    )
    value_weight_grad = jnp.einsum(
        "td,tc->dc", hidden_in, value_grad, preferred_element_type=jnp.float32
    )
    value_bias_grad = jnp.sum(value_grad.astype(jnp.float32), axis=0)
    box_weight_grad = jnp.einsum(
        "td,tc->dc", hidden_in, coeff_grad, preferred_element_type=jnp.float32
    )
    box_bias_grad = jnp.sum(coeff_grad.astype(jnp.float32), axis=0)

    def slice_times(gradient, weight):
        return jnp.einsum("tc,dc->td", gradient, weight, preferred_element_type=jnp.float32)

    input_grad = (
        lax.psum_scatter(
            (
                slice_times(query_grad, query_weight)
                + slice_times(key_grad, key_weight)
                + slice_times(value_grad, value_weight)
                + slice_times(coeff_grad, box_weight)
            ).astype(jnp.bfloat16),
            "tensor",
            scatter_dimension=0,
            tiled=True,
        ).astype(jnp.float32)
        + attn_grad
    )
    norm_stack = jnp.stack(
        [
            output_bias_grad,
            first_gain_grad,
            first_shift_grad,
            down_bias_grad,
            second_gain_grad,
            second_shift_grad,
        ]
    )
    norm_share = lax.psum_scatter(norm_stack, "tensor", scatter_dimension=1, tiled=True)
    (
        query_weight_grad,
        query_bias_grad,
        key_weight_grad,
        value_weight_grad,
        value_bias_grad,
        box_weight_grad,
        box_bias_grad,
        output_weight_grad,
        up_weight_grad,
        up_bias_grad,
        down_weight_grad,
        norm_share,
    ) = lax.psum(
        (
            query_weight_grad,
            query_bias_grad,
            key_weight_grad,
            value_weight_grad,
            value_bias_grad,
            box_weight_grad,
            box_bias_grad,
            output_weight_grad,
            up_weight_grad,
            up_bias_grad,
            down_weight_grad,
            norm_share,
        ),
        "dp",
    )
    return (
        layer_out,
        input_grad,
        query_weight_grad,
        query_bias_grad,
        key_weight_grad,
        value_weight_grad,
        value_bias_grad,
        box_weight_grad,
        box_bias_grad,
        output_weight_grad,
        norm_share[0],
        norm_share[1],
        norm_share[2],
        up_weight_grad,
        up_bias_grad,
        down_weight_grad,
        norm_share[3],
        norm_share[4],
        norm_share[5],
    )


def solution(mesh):
    in_specs = (
        P("dp", None),
        P(None, "dp"),
        P("dp"),
        P(None, "tensor"),
        P("tensor"),
        P(None, "tensor"),
        P(None, "tensor"),
        P("tensor"),
        P(None, "tensor"),
        P("tensor"),
        P("tensor", None),
        P(),
        P(),
        P(),
        P(None, "tensor"),
        P("tensor"),
        P("tensor", None),
        P(),
        P(),
        P(),
        P(("dp", "tensor"), None),
    )
    out_specs = (
        P(("dp", "tensor"), None),
        P(("dp", "tensor"), None),
        P(None, "tensor"),
        P("tensor"),
        P(None, "tensor"),
        P(None, "tensor"),
        P("tensor"),
        P(None, "tensor"),
        P("tensor"),
        P("tensor", None),
        P("tensor"),
        P("tensor"),
        P("tensor"),
        P(None, "tensor"),
        P("tensor"),
        P("tensor", None),
        P("tensor"),
        P("tensor"),
        P("tensor"),
    )
    return jax.shard_map(body, mesh=mesh, in_specs=in_specs, out_specs=out_specs, check_vma=False)
```

profile of v0, /device:TPU:0, one launch (start us, length us, event | category | flops | bytes accessed | tf_op | source)
XLA Modules:
  0.0 1082.0 jit_solution(2508991166688201813)
XLA Ops:
  8.3 3.1 fusion.94
  15.8 4.6 convolution_add_fusion
  23.2 5.0 copy.158
  28.1 4.9 copy.159
  33.1 6.2 add_convert_fusion.2
  39.3 4.8 copy.152
  44.1 3.1 copy.153
  47.2 4.1 pad_maximum_fusion
  51.4 3.6 copy.131
  59.3 5.0 cosine_convert_fusion
  68.0 5.1 fusion.79
  73.1 3.9 reshape.199
  79.8 5.1 fusion.80
  84.8 3.7 reshape.200
  88.6 2.9 copy.128
  91.4 5.1 convolution_convert_fusion.4
  96.5 3.8 reshape.201
  104.2 46.6 %while.28 = (s32[]{:T(128)}, bf16[6,512,3,64]{1,3,2,0:T(8,128)(2,1)}, f32[6,3,512]{2,1,0:T(4,128)}, bf16[6,512,3,64]{1,3,2,0:T(8,128)(2,1)}, s32[6]{0:T(128)S(1)...) while((s32[]{:T(128)}, ...), condition=%wide.region_3.4_spmd, body=%wide.region_0.3_spmd.sunk | while | flops 409828352 | bytes 17095284 | solution.py:202
  155.1 3.6 convolution_convert_fusion.2
  158.8 96.8 %all-reduce.6.cloned.1.call-done = bf16[3072,768]{1,0:T(8,128)(2,1)} async-done(((bf16[3072,768]{1,0:T(8,128)(2,1)}), bf16[3072,768]{1,0:T(8,128)(2,1)}) %all-reduce.6.cloned.1.call-update) | async-done | bytes 4718608 | tf_op jit(solution)/shard_map/psum | solution.py:204
  255.7 5.5 fusion.78
  261.3 5.5 multiply_reduce_fusion.1
  266.8 5.1 multiply_add_fusion
  271.9 25.2 %multiply_convert_fusion.1 = (bf16[3072,768]{1,0:T(8,128)(2,1)S(1)}, f32[3072,768]{1,0:T(8,128)}, f32[3072,768]{1,0:T(8,128)}) fusion(f32[768]{0:T(1024)S(1)} %copy-done.44, bf16[768,768]{1,0:T(8,128)(2,1)S(1)} %copy-done, f32[3072,768]{1,0:T(8,128)S(1)} %get-tuple-element.384), kind=kOutput, calls=%fused_computation.85 | convolution fusion | flops 3781951488 | bytes 34212864 | tf_op jit(solution)/shard_map/dot_general | solution.py:215
  299.2 5.4 convolution_convert_fusion.1
  304.8 94.2 %all-reduce.8.cloned.1.call-done = bf16[3072,768]{1,0:T(8,128)(2,1)} async-done(((bf16[3072,768]{1,0:T(8,128)(2,1)}), bf16[3072,768]{1,0:T(8,128)(2,1)}) %all-reduce.8.cloned.1.call-update) | async-done | bytes 4718608 | tf_op jit(solution)/shard_map/psum | solution.py:217
  405.7 37.7 %all-gather.3.cloned.1.call-done = bf16[3072,768]{1,0:T(8,128)(2,1)} async-done(((bf16[768,768]{1,0:T(8,128)(2,1)}), bf16[3072,768]{1,0:T(8,128)(2,1)}) %all-gather.3.cloned.1.call-update) | async-done | bytes 4718608 | tf_op jit(solution)/shard_map/all_gather | solution.py:230
  443.5 13.8 %convert_reduce_fusion = (f32[768]{0:T(1024)}, bf16[3072,768]{1,0:T(8,128)(2,1)S(1)}) fusion(f32[3072,768]{1,0:T(8,128)} %get-tuple-element.383, f32[3072,768]{1,0:T(8,128)} %get-tuple-element.409, f32[768]{0:T(1024)} %param.40, bf16[3072,768]{1,0:T(8,128)(2,1)} %all-gather.3.cloned.1.call-done, bf16[768,768]{1,0:T(8,128)(2,1)} %param.41), kind=kOutput, calls=%fused_computation.82 | convolution fusion | flops 3663985920 | bytes 29497344 | tf_op jit(solution)/shard_map/td,fd->tf/dot_general | solution.py:234
  459.4 5.5 convolution_convert_fusion
  465.1 47.8 %reduce-scatter.6.cloned.1.call-done = bf16[768,768]{1,0:T(8,128)(2,1)} async-done(((bf16[3072,768]{1,0:T(8,128)(2,1)}), bf16[768,768]{1,0:T(8,128)(2,1)}) %reduce-scatter.6.cloned.1.call-update) | async-done | bytes 1179664 | tf_op jit(solution)/shard_map/reduce_scatter | solution.py:244
  513.0 3.0 multiply_reduce_fusion.2
  521.5 9.3 fusion.110
  530.8 7.7 fusion.88
  539.8 18.7 %all-gather.5.cloned.1.call-done = bf16[3072,768]{1,0:T(8,128)(2,1)} async-done(((bf16[768,768]{1,0:T(8,128)(2,1)}), bf16[3072,768]{1,0:T(8,128)(2,1)}) %all-gather.5.cloned.1.call-update) | async-done | bytes 4718608 | tf_op jit(solution)/shard_map/all_gather | solution.py:258
  558.6 4.0 convolution_convert_fusion.3
  568.8 145.0 %while.29 = (s32[]{:T(128)}, bf16[6,512,3,64]{1,3,2,0:T(8,128)(2,1)}, bf16[6,512,3,64]{1,3,2,0:T(8,128)(2,1)}, bf16[6,512,3,64]{1,3,2,0:T(8,128)(2,1)}, f32[6,51...) while((s32[]{:T(128)}, ...), condition=%wide.region_17.18_spmd, body=%wide.region_15.17_spmd.sunk | while | flops 914521088 | bytes 38049944 | solution.py:265
  633.8 2.8 fusion.201
  713.8 5.4 multiply_add_fusion.1
  719.3 2.9 convert_reduce_fusion.1
  722.1 3.0 copy.143
  725.2 6.2 convolution_bitcast_fusion
  747.6 5.6 fusion.107
  753.2 5.4 fusion.108
  758.6 9.7 add_convert_fusion
  772.7 39.5 %all-reduce = (f32[192]{0:T(256)}, f32[192]{0:T(256)}, f32[384]{0:T(512)}, f32[6,192]{1,0:T(8,128)S(1)}, f32[768]{0:T(1024)}) all-reduce(f32[192]{0:T(256)S(1)} %reduce_sum.195, f32[192]{0:T(256)S(1)} %reduce_sum.197, f32[384]{0:T(512)S(1)} %bitcast.292, f32[6,192]{1,0:T(8,128)S(1)} %copy.155, ...), channel_id=1, replica_groups=mesh['dp'=8,'tensor'=4] {'dp'}, use_global_device_ids=true, to_apply=%region_21.22 | all-reduce | flops 2688 | bytes 21504 | tf_op jit(solution)/shard_map/psum | solution.py:333
  812.8 203.4 %all-reduce.10.cloned.1.call-done = (f32[768,192]{0,1:T(8,128)}, f32[768,192]{0,1:T(8,128)}, f32[768,192]{0,1:T(8,128)}, f32[768,384]{0,1:T(8,128)}, f32[192,768...) async-done(((f32[768,192]{0,1:T(8,128)}, f32[768,192]{0,1:T(8,128)}, f32[768,192]{0,1:T(8,128)}, f32[768,384]{0,1:T(8,128)}, f32[192,768]{1,0:T(8,128)}, ...) | async-done | bytes 8257552 | tf_op jit(solution)/shard_map/psum | solution.py:333
  1018.9 46.7 %reduce-scatter.8.cloned.1.call-done = bf16[768,768]{1,0:T(8,128)(2,1)} async-done(((bf16[3072,768]{1,0:T(8,128)(2,1)}), bf16[768,768]{1,0:T(8,128)(2,1)}) %reduce-scatter.8.cloned.1.call-update) | async-done | bytes 1179664 | tf_op jit(solution)/shard_map/reduce_scatter | solution.py:296
  1065.7 3.0 convert_add_fusion.1
  (331 shorter events, 269.6 us)
Async XLA Ops:
  7.2 264.7 %copy-start = (bf16[768,768]{1,0:T(8,128)(2,1)S(1)}, bf16[768,768]{1,0:T(8,128)(2,1)}, u32[]{:S(2)}) copy-start(bf16[768,768]{1,0:T(8,128)(2,1)} %param.39) | copy-start | bytes 3538948
  7.2 248.5 %all-reduce.6.cloned.1.call-start = ((), (), s32[]{:S(2)}) async-start(), calls=%async_computation.3 | async-start | bytes 9437184 | tf_op jit(solution)/shard_map/psum | solution.py:204
  8.2 4.4 copy-start.27
  14.2 18.9 %copy-start.9 = (f32[3072,64]{1,0:T(8,128)}, f32[3072,64]{1,0:T(8,128)S(1)}, u32[]{:S(2)}) copy-start(f32[3072,64]{1,0:T(8,128)S(1)} %copy.122) | copy-start | bytes 2359300
  39.3 4.8 copy-start.14
  59.3 8.7 copy-start.46
  73.0 6.7 copy-start.47
  96.5 7.7 copy-start.48
  150.8 7.9 copy-start.6
  150.8 4.3 copy-start.29
  158.8 96.9 %copy-start.33 = (f32[768]{0:T(1024)S(1)}, f32[768]{0:T(1024)}, u32[]{:S(2)}) copy-start(f32[768]{0:T(1024)} %param.36) | copy-start | bytes 9220
  158.8 240.3 %all-reduce.8.cloned.1.call-start = ((), (), s32[]{:S(2)}) async-start(), calls=%async_computation.4 | async-start | bytes 9437184 | tf_op jit(solution)/shard_map/psum | solution.py:217
  255.7 5.5 copy-start.3
  261.2 5.6 slice-start
  261.2 5.6 slice-start.1
  261.2 5.5 copy-start.34
  261.2 5.5 copy-start.39
  266.8 5.1 copy-start.44
  271.9 25.2 %copy-start.2 = (f32[3072,768]{1,0:T(8,128)}, f32[3072,768]{1,0:T(8,128)S(1)}, u32[]{:S(2)}) copy-start(f32[3072,768]{1,0:T(8,128)S(1)} %get-tuple-element.384) | copy-start | bytes 28311556
  271.9 27.3 %copy-start.43 = (bf16[768,768]{1,0:T(8,128)(2,1)S(1)}, bf16[768,768]{1,0:T(8,128)(2,1)}, u32[]{:S(2)}) copy-start(bf16[768,768]{1,0:T(8,128)(2,1)} %param.41) | copy-start | bytes 3538948
  304.7 94.4 %copy-start.40 = (f32[768]{0:T(1024)S(1)}, f32[768]{0:T(1024)}, u32[]{:S(2)}) copy-start(f32[768]{0:T(1024)} %param.42) | copy-start | bytes 9220
  304.7 138.8 %all-gather.3.cloned.1.call-start = ((), (), s32[]{:S(2)}) async-start(), calls=%async_computation.5 | async-start | bytes 5898240 | tf_op jit(solution)/shard_map/all_gather | solution.py:230
  304.8 97.1 %copy-start.15 = (bf16[768,768]{1,0:T(8,128)(2,1)S(1)}, bf16[768,768]{1,0:T(8,128)(2,1)}, u32[]{:S(2)}) copy-start(bf16[768,768]{1,0:T(8,128)(2,1)} %param.45) | copy-start | bytes 3538948
  304.8 97.1 %copy-start.36 = (f32[768]{0:T(1024)S(1)}, f32[768]{0:T(1024)}, u32[]{:S(2)}) copy-start(f32[768]{0:T(1024)} %param.43) | copy-start | bytes 9220
  405.7 107.3 %reduce-scatter.6.cloned.1.call-start = ((), (), s32[]{:S(2)}) async-start(), calls=%async_computation.6 | async-start | bytes 5898240 | tf_op jit(solution)/shard_map/reduce_scatter | solution.py:244
  464.9 48.0 %copy-start.35 = (f32[768]{0:T(1024)S(1)}, f32[768]{0:T(1024)}, u32[]{:S(2)}) copy-start(f32[768]{0:T(1024)} %param.37) | copy-start | bytes 9220
  465.0 93.6 %all-gather.5.cloned.1.call-start = ((), (), s32[]{:S(2)}) async-start(), calls=%async_computation.7 | async-start | bytes 5898240 | tf_op jit(solution)/shard_map/all_gather | solution.py:258
  519.8 11.0 %slice-start.4 = ((s8[9437184]{0:T(1024)(128)(4,1)}), s8[1048576]{0:T(1024)(128)(4,1)S(1)}, s32[]{:S(2)}) async-start(s8[9437184]{0:T(1024)(128)(4,1)} %bitcast.268), calls=%async_computation.15 | async-start | bytes 2097152
  520.9 247.4 %reduce-scatter.10.cloned.1.call-start = ((), (), s32[]{:S(2)}) async-start(), calls=%async_computation.9 | async-start | bytes 491520
  521.5 9.3 slice-start.5
  521.5 9.3 slice-start.6
  530.8 27.8 %copy-start.30 = (bf16[192,768]{1,0:T(8,128)(2,1)S(1)}, bf16[192,768]{1,0:T(8,128)(2,1)}, u32[]{:S(2)}) copy-start(bf16[192,768]{1,0:T(8,128)(2,1)} %param.35) | copy-start | bytes 884740
  539.6 476.7 %all-reduce.10.cloned.1.call-start = ((), (), s32[]{:S(2)}) async-start(), calls=%async_computation.10 | async-start | bytes 16515072 | tf_op jit(solution)/shard_map/psum | solution.py:333
  564.0 4.8 copy-start.49
  719.3 14.6 %slice-start.2 = ((s8[4718592]{0:T(1024)(128)(4,1)}), s8[524288]{0:T(1024)(128)(4,1)S(1)}, s32[]{:S(2)}) async-start(s8[4718592]{0:T(1024)(128)(4,1)} %bitcast.266), calls=%async_computation.13 | async-start | bytes 1048576
  725.2 6.2 copy-start.12
  725.2 8.7 slice-start.3
  737.0 6.3 slice-start.7
  745.2 320.5 %reduce-scatter.8.cloned.1.call-start = ((), (), s32[]{:S(2)}) async-start(), calls=%async_computation.8 | async-start | bytes 5898240 | tf_op jit(solution)/shard_map/reduce_scatter | solution.py:296
  747.6 5.6 copy-start.13
  747.6 5.6 copy-start.22
  753.2 5.4 copy-start.11
  753.2 5.4 copy-start.28
  768.3 4.4 copy-start.42
  768.3 297.3 %copy-start.5 = (f32[768,768]{1,0:T(8,128)S(1)}, f32[768,768]{1,0:T(8,128)}, u32[]{:S(2)}) copy-start(f32[768,768]{1,0:T(8,128)} %copy-done.4) | copy-start | bytes 7077892
  1018.9 50.5 %copy-start.25 = (f32[768,192]{0,1:T(8,128)S(1)}, f32[768,192]{0,1:T(8,128)}, u32[]{:S(2)}) copy-start(f32[768,192]{0,1:T(8,128)} %get-tuple-element.630) | copy-start | bytes 1769476
  1018.9 51.3 %copy-start.24 = (f32[768,192]{0,1:T(8,128)S(1)}, f32[768,192]{0,1:T(8,128)}, u32[]{:S(2)}) copy-start(f32[768,192]{0,1:T(8,128)} %get-tuple-element.631) | copy-start | bytes 1769476
  1068.6 3.3 copy-start.21
  (20 other events, 45.5 us)
Sparse Core Ops, SparseCore 0:
  158.9 96.7 all-reduce.5
  304.8 94.1 all-reduce.7
  405.8 37.6 all-gather.2
  465.1 47.8 reduce-scatter.5
  521.0 37.4 all-gather.4
  561.1 20.8 reduce-scatter.9
  745.3 270.9 all-reduce.9
  1018.8 46.8 reduce-scatter.7
where the time goes:
time: 1090 us; the launch traced here: 1080 us
  waiting for transfers between devices  546 us (50%)
  matrix products  258 us (24%)
  local copies, waits for them, and re-layouts  132 us (12%)
  other arithmetic  90.1 us (8%)
  blocking collectives  39.5 us (4%)
  between operations  15.3 us (1%)
    psum x1, waiting for transfers between devices, body(): lax.psum((query_weight_grad, query_bias_grad, key_weight_grad, value_weig...  203 us
    psum x1, waiting for transfers between devices, body(): lax.psum(jnp.dot(context, output_weight, preferred_element_type=jnp.float...  96.8 us
    psum x1, waiting for transfers between devices, body(): lax.psum(jnp.dot(activated, down_weight, preferred_element_type=jnp.float...  94.2 us
    reduce_scatter x1, waiting for transfers between devices, body(): lax.psum_scatter(jnp.einsum('tf,df->td', upper_grad, up_weight, preferred...  47.8 us
    reduce_scatter x1, waiting for transfers between devices, body(): lax.psum_scatter((slice_times(query_grad, query_weight) + slice_times(key...  46.7 us
    psum x1, blocking collectives, body(): lax.psum((query_weight_grad, query_bias_grad, key_weight_grad, value_weig...  39.5 us
    all_gather x1, waiting for transfers between devices, body(): lax.all_gather(second_grad.astype(jnp.bfloat16), 'tensor', axis=0, tiled=...  37.7 us
    unnamed x135, local copies, waits for them, and re-layouts  30.4 us
  transfers between devices with their start and end apart: 8, of which 7 were waited for; matrix products, arithmetic and copies ran while one was open for 22% of the time, Pallas kernels for 0%

commit v1 on v0

v1 whole, which is shorter than its diff:
```python
import math
from functools import partial
import jax, jax.numpy as jnp
from jax import lax
from jax.experimental import pallas as pl
from jax.experimental.pallas import tpu as pltpu
HEAD=64; POS=128; PAGE=512
F32=jnp.float32; BF=jnp.bfloat16
LOG2E=1.4426950408889634

def mm(a,b): return jnp.dot(a,b,preferred_element_type=F32)
def mm_nt(a,b): return lax.dot_general(a,b,(((1,),(1,)),((),())),preferred_element_type=F32)
def mm_tn(a,b): return lax.dot_general(a,b,(((0,),(0,)),((),())),preferred_element_type=F32)

def mixing(geo):
    half=POS//2
    c=geo[:,:half]; s=geo[:,half:]
    return jnp.concatenate([c,-c],axis=1), jnp.concatenate([s,s],axis=1)

def mix(coeff, cos_sign, sin_twice):
    return coeff*cos_sign + pltpu.roll(coeff, POS//2, 1)*sin_twice

def attend_forward(base_ref, len_ref, h_ref, geo_ref, wq_ref, wk_ref, wv_ref, wb_ref, qb_ref, vb_ref, bb_ref, ctx_ref, q_ref, k_ref, v_ref, p_ref, cat_q, cat_k, *, rows):
    heads=q_ref.shape[1]//HEAD
    length=len_ref[base_ref[0]+pl.program_id(0)]
    h=h_ref[...]
    geo=geo_ref[...]
    q_ref[...]=(mm(h,wq_ref[...])+qb_ref[...]).astype(BF)
    k_ref[...]=mm(h,wk_ref[...]).astype(BF)
    v_ref[...]=(mm(h,wv_ref[...])+vb_ref[...]).astype(BF)
    cs,ss=mixing(geo.astype(F32))
    for head in range(heads):
        coeff=mm(h,wb_ref[:,head*POS:(head+1)*POS])+bb_ref[:,head*POS:(head+1)*POS]
        cat_q[head,:,:POS]=mix(coeff,cs,ss).astype(BF)
        cat_q[head,:,POS:]=q_ref[:,head*HEAD:(head+1)*HEAD]
        cat_k[head,:,:POS]=geo
        cat_k[head,:,POS:]=k_ref[:,head*HEAD:(head+1)*HEAD]
    valid=lax.broadcasted_iota(jnp.int32,(1,PAGE),1)<length
    scale=LOG2E/math.sqrt(HEAD)
    for head in range(heads):
        keys=cat_k[head]
        values=v_ref[:,head*HEAD:(head+1)*HEAD]
        for r in range(0,PAGE,rows):
            s=mm_nt(cat_q[head,r:r+rows,:],keys)
            s=jnp.where(valid,s,-1e30)
            top=jnp.max(s,axis=1,keepdims=True)
            e=jnp.exp2((s-top)*scale)
            total=jnp.sum(e,axis=1,keepdims=True)
            p=(e*(1.0/total)).astype(BF)
            p_ref[head,r:r+rows,:]=p
            ctx_ref[r:r+rows,head*HEAD:(head+1)*HEAD]=mm(p,values).astype(BF)

def run_forward(base, lengths, hidden, geo, wq, wk, wv, wb, qb, vb, bb, pages, rows=256):
    cols=wq.shape[1]; heads=cols//HEAD; d=hidden.shape[1]
    page_in=lambda w: pl.BlockSpec((PAGE,w),lambda i,b,l:(b[0]+i,0))
    page_out=lambda w: pl.BlockSpec((PAGE,w),lambda i,b,l:(i,0))
    whole=lambda a: pl.BlockSpec(a.shape,lambda i,b,l:(0,0),pipeline_mode=pl.Buffered(1))
    rows_out=pages*PAGE
    return pl.pallas_call(partial(attend_forward,rows=rows),
        out_shape=[jax.ShapeDtypeStruct((rows_out,cols),BF)]*4+[jax.ShapeDtypeStruct((pages,heads,PAGE,PAGE),BF)],
        grid_spec=pltpu.PrefetchScalarGridSpec(num_scalar_prefetch=2,grid=(pages,),
            in_specs=[page_in(d),page_in(POS)]+[whole(a) for a in (wq,wk,wv,wb,qb,vb,bb)],
            out_specs=[page_out(cols)]*4+[pl.BlockSpec((pl.Squeezed(),heads,PAGE,PAGE),lambda i,b,l:(i,0,0,0))],
            scratch_shapes=[pltpu.VMEM((heads,PAGE,POS+HEAD),BF)]*2),
        compiler_params=pltpu.CompilerParams(vmem_limit_bytes=60<<20),
        name="attend_forward",
    )(base,lengths,hidden,geo,wq,wk,wv,wb,qb,vb,bb)
EPS=1e-05

def normal(z):
    mean=jnp.mean(z,axis=1,keepdims=True)
    centred=z-mean
    inverse=lax.rsqrt(jnp.mean(centred*centred,axis=1,keepdims=True)+EPS)
    return centred*inverse, inverse

def normal_back(inner, scaled, inverse):
    return inverse*(inner-jnp.mean(inner,axis=1,keepdims=True)-scaled*jnp.mean(inner*scaled,axis=1,keepdims=True))

def columns(x): return jnp.sum(x,axis=0,keepdims=True)

def middle(t_ref, hid_any, og_any, ctx_any, w0, w1, w2, w3, w4, w5, w6, w7, w8, w9, w10, w11, ub_ref, vec_ref,
           out_any, ag_any, dctx_any, act_any, ug_any, fl_any, sl_any, al_any, vg_ref, ubg_ref,
           hid, og, ctx, wo, wu, wd, act, ug, fl, sl, al, lo, ag, first, scaled1, inv1, ffn, dctx, sem_in, sem_w, sem_out, *, tile):
    rows,d=hid.shape
    groups=wu.shape[0]
    weights=(w0,w1,w2,w3,w4,w5,w6,w7,w8,w9,w10,w11)
    head_loads=[pltpu.make_async_copy(hid_any.at[pl.ds(t_ref[0]*rows,rows)],hid,sem_in.at[0]),
           pltpu.make_async_copy(og_any,og,sem_in.at[1]),
           pltpu.make_async_copy(ctx_any,ctx,sem_in.at[2])]
    loads=[[pltpu.make_async_copy(weights[3*g+k],(wo,wu,wd)[k].at[g],sem_w.at[k,g]) for g in range(groups)] for k in range(3)]
    for c in head_loads: c.start()
    for k in range(3):
        for c in loads[k]: c.start()
    for c in head_loads: c.wait()
    for c in loads[0]: c.wait()
    ob,g1,s1,db,g2,s2=(vec_ref[i:i+1,:] for i in range(6))
    vg_ref[...]=jnp.zeros_like(vg_ref)
    ubg_ref[...]=jnp.zeros_like(ubg_ref)
    for c in loads[1]: c.wait()
    for c in loads[2]: c.wait()
    def step(i,_):
        r=pl.ds(pl.multiple_of(i*tile,tile),tile)
        attn=mm(ctx[0,r],wo[0])
        for g in range(1,groups): attn=attn+mm(ctx[g,r],wo[g])
        scaled,inverse=normal(attn+ob+hid[r].astype(F32))
        f=scaled*g1+s1
        first[...]=f
        scaled1[...]=scaled
        inv1[...]=inverse
        fl[r]=f.astype(BF)
        ffn[...]=jnp.zeros_like(ffn)
        def up(g,_):
            x=mm(fl[r],wu[g])+ub_ref[g]
            half=0.5+0.5*lax.erf(x*0.7071067811865476)
            a=(x*half).astype(BF)
            act[g,r]=a
            ug[g,r]=(half+x*jnp.exp(-0.5*x*x)*0.3989422804014327).astype(BF)
            ffn[...]+=mm(a,wd[g])
            return 0
        lax.fori_loop(0,groups,up,0)
        scaled,inverse=normal(ffn[...]+db+first[...])
        lo[r]=(scaled*g2+s2).astype(BF)
        o=og[r].astype(F32)
        second=normal_back(o*g2,scaled,inverse)
        vg_ref[3:4,:]+=columns(second)
        vg_ref[4:5,:]+=columns(o*scaled)
        vg_ref[5:6,:]+=columns(o)
        sl[r]=second.astype(BF)
        ffn[...]=second
        def down(g,_):
            u=(mm_nt(sl[r],wd[g])*ug[g,r].astype(F32)).astype(BF)
            ug[g,r]=u
            ubg_ref[g]+=columns(u.astype(F32))
            ffn[...]+=mm_nt(u,wu[g])
            return 0
        lax.fori_loop(0,groups,down,0)
        fg=ffn[...]
        scaled=scaled1[...]
        a=normal_back(fg*g1,scaled,inv1[...])
        vg_ref[0:1,:]+=columns(a)
        vg_ref[1:2,:]+=columns(fg*scaled)
        vg_ref[2:3,:]+=columns(fg)
        ag[r]=a
        alow=a.astype(BF)
        al[r]=alow
        for g in range(groups): dctx[g,r]=mm_nt(alow,wo[g]).astype(BF)
        return 0
    lax.fori_loop(0,rows//tile,step,0)
    stores=[pltpu.make_async_copy(a,b,sem_out.at[i]) for i,(a,b) in enumerate(((dctx,dctx_any),(act,act_any),(ug,ug_any),(fl,fl_any),(sl,sl_any),(al,al_any),(lo,out_any),(ag,ag_any)))]
    for c in stores: c.start()
    for c in stores: c.wait()

def run_middle(t, hidden, og, ctx, weights, ub, vec, tile=256):
    rows,d=og.shape; groups=4; q=weights[0].shape[0]; f=weights[1].shape[1]
    anyspec=pl.BlockSpec(memory_space=pl.ANY)
    vm=pl.BlockSpec(memory_space=pltpu.VMEM)
    S=jax.ShapeDtypeStruct
    return pl.pallas_call(partial(middle,tile=tile),
        out_shape=[S((rows,d),BF),S((rows,d),F32),S((groups,rows,q),BF),S((groups,rows,f),BF),S((groups,rows,f),BF),S((rows,d),BF),S((rows,d),BF),S((rows,d),BF),S((8,d),F32),S((groups,1,f),F32)],
        in_specs=[pl.BlockSpec(memory_space=pltpu.SMEM)]+[anyspec]*15+[vm,vm],
        out_specs=[anyspec]*8+[vm,vm],
        scratch_shapes=[pltpu.VMEM((rows,d),BF),pltpu.VMEM((rows,d),BF),pltpu.VMEM((groups,rows,q),BF),
            pltpu.VMEM((groups,q,d),BF),pltpu.VMEM((groups,d,f),BF),pltpu.VMEM((groups,f,d),BF),
            pltpu.VMEM((groups,rows,f),BF),pltpu.VMEM((groups,rows,f),BF),
            pltpu.VMEM((rows,d),BF),pltpu.VMEM((rows,d),BF),pltpu.VMEM((rows,d),BF),pltpu.VMEM((rows,d),BF),pltpu.VMEM((rows,d),F32),
            pltpu.VMEM((tile,d),F32),pltpu.VMEM((tile,d),F32),pltpu.VMEM((tile,1),F32),pltpu.VMEM((tile,d),F32),
            pltpu.VMEM((groups,rows,q),BF),
            pltpu.SemaphoreType.DMA((3,)),pltpu.SemaphoreType.DMA((3,groups)),pltpu.SemaphoreType.DMA((8,))],
        compiler_params=pltpu.CompilerParams(vmem_limit_bytes=62<<20),
        name="middle",
    )(t,hidden,og,ctx,*weights,ub,vec)

def weight_grads(ctx_ref,al_ref,fl_ref,ug_ref,act_ref,sl_ref,extra_ref,g_ref,*,step):
    q=ctx_ref.shape[1]; d=fl_ref.shape[1]; f=ug_ref.shape[1]
    g_ref[0:q]=mm_tn(ctx_ref[...],al_ref[...]).astype(BF)
    g_ref[q:q+d]=mm_tn(fl_ref[...],ug_ref[...]).astype(BF)
    g_ref[q+d:q+d+f]=mm_tn(act_ref[...],sl_ref[...]).astype(BF)
    g_ref[q+d+f:q+d+f+8]=extra_ref[...].astype(BF)
    g_ref[q+d+f+8:]=jnp.zeros((g_ref.shape[0]-(q+d+f+8),d),BF)

def run_weight_grads(ctx,al,fl,ug,act,sl,extra,padded):
    groups,rows,q=ctx.shape; d=fl.shape[1]; f=ug.shape[2]
    order=lambda i:(i%2)*2+i//2
    per=lambda w: pl.BlockSpec((pl.Squeezed(),rows,w),lambda i:(order(i),0,0))
    whole=pl.BlockSpec((rows,d),lambda i:(0,0),pipeline_mode=pl.Buffered(1))
    return pl.pallas_call(partial(weight_grads,step=256),
        out_shape=jax.ShapeDtypeStruct((groups,padded,d),BF),
        grid=(groups,),
        in_specs=[per(q),whole,whole,per(f),per(f),whole,pl.BlockSpec((pl.Squeezed(),8,d),lambda i:(order(i),0,0))],
        out_specs=pl.BlockSpec((pl.Squeezed(),padded,d),lambda i:(i,0,0)),
        compiler_params=pltpu.CompilerParams(vmem_limit_bytes=60<<20),
        name="weight_grads")(ctx,al,fl,ug,act,sl,extra)
def attend_backward(base_ref, h_ref, geo_ref, w_ref, q_ref, k_ref, v_ref, p_ref, dc_ref, *rest, has_start, last):
    if has_start: start_ref,bstart_ref,*rest=rest
    dx_ref,dw_ref,db_ref,total,btotal,mixed=rest
    i=pl.program_id(0)
    cols=q_ref.shape[1]; heads=cols//HEAD
    @pl.when(i==0)
    def _():
        if has_start:
            total[...]=start_ref[...]; btotal[...]=bstart_ref[...]
        else:
            total[...]=jnp.zeros_like(total); btotal[...]=jnp.zeros_like(btotal)
    geo=geo_ref[...]
    cs,ss=mixing(geo.astype(F32))
    factor=1.0/math.sqrt(HEAD)
    for head in range(heads):
        lanes=slice(head*HEAD,(head+1)*HEAD)
        p=p_ref[head]
        dc=dc_ref[:,lanes]
        mixed[:,2*cols+head*HEAD:2*cols+(head+1)*HEAD]=mm_tn(p,dc).astype(BF)
        dp=mm_nt(dc,v_ref[:,lanes])
        pf=p.astype(F32)
        delta=jnp.sum(pf*dp,axis=1,keepdims=True)
        ds=(pf*(dp-delta)).astype(BF)
        both=mm(ds,jnp.concatenate([geo,k_ref[:,lanes]],axis=1))*factor
        mixed[:,lanes]=both[:,POS:].astype(BF)
        mixed[:,3*cols+head*POS:3*cols+(head+1)*POS]=mix(both[:,:POS],cs,ss).astype(BF)
        mixed[:,cols+head*HEAD:cols+(head+1)*HEAD]=(mm_tn(ds,q_ref[:,lanes])*factor).astype(BF)
    total[...]+=mm_tn(h_ref[...],mixed[...])
    btotal[0:1,:]+=jnp.sum(mixed[...].astype(F32),axis=0,keepdims=True)
    dx_ref[...]=mm_nt(mixed[...],w_ref[...]).astype(BF)
    @pl.when(i==pl.num_programs(0)-1)
    def _():
        dw_ref[...]=total[...].astype(dw_ref.dtype); db_ref[...]=btotal[...]

def run_backward(base,hidden,geo,w,q,k,v,p,dc,start=None,last=False):
    pages,heads=p.shape[:2]; cols=q.shape[1]; d=hidden.shape[1]; wide=w.shape[1]
    page_in=lambda n: pl.BlockSpec((PAGE,n),lambda i,b:(b[0]+i,0))
    page=lambda n: pl.BlockSpec((PAGE,n),lambda i,b:(i,0))
    whole=lambda s: pl.BlockSpec(s,lambda i,b:(0,0),pipeline_mode=pl.Buffered(1))
    extra=[] if start is None else list(start)
    S=jax.ShapeDtypeStruct
    return pl.pallas_call(partial(attend_backward,has_start=start is not None,last=last),
        out_shape=[S((pages*PAGE,d),BF),S((d,wide),BF if last else F32),S((8,wide),F32)],
        grid_spec=pltpu.PrefetchScalarGridSpec(num_scalar_prefetch=1,grid=(pages,),
            in_specs=[page_in(d),page_in(POS),whole(w.shape),page(cols),page(cols),page(cols),pl.BlockSpec((pl.Squeezed(),heads,PAGE,PAGE),lambda i,b:(i,0,0,0)),page(cols)]+[whole(a.shape) for a in extra],
            out_specs=[page(d),pl.BlockSpec((d,wide),lambda i,b:(0,0)),pl.BlockSpec((8,wide),lambda i,b:(0,0))],
            scratch_shapes=[pltpu.VMEM((d,wide),F32),pltpu.VMEM((8,wide),F32),pltpu.VMEM((PAGE,wide),BF)]),
        compiler_params=pltpu.CompilerParams(vmem_limit_bytes=60<<20),
        name="attend_backward")(base,hidden,geo,w,q,k,v,p,dc,*extra)

FREQ=16

def features(box_coords):
    rates = jnp.power(1000.0, -jnp.arange(FREQ, dtype=jnp.float32) / FREQ)
    angles = box_coords.astype(jnp.float32)[:, :, None] * rates[None, None, :]
    angles = jnp.transpose(angles, (1, 0, 2)).reshape(box_coords.shape[1], 4 * FREQ)
    return jnp.concatenate([jnp.cos(angles), jnp.sin(angles)], axis=1)

from jax.sharding import PartitionSpec as P

def body(hidden_in, box_coords, page_lengths, query_weight, query_bias, key_weight, value_weight, value_bias,
         box_weight, box_bias, output_weight, output_bias, first_gain, first_shift, up_weight, up_bias,
         down_weight, down_bias, second_gain, second_shift, output_grad):
    ways=lax.axis_size("tensor")
    place=lax.axis_index("tensor")
    core=place%2; chip=place//2
    rows=hidden_in.shape[0]//ways
    pages=page_lengths.shape[0]//2
    def swap(x,by):
        return lax.ppermute(x,"tensor",[(i,i^by) for i in range(ways)])
    def part(x,which):
        return lax.dynamic_slice_in_dim(x,which*rows,rows,0)
    own=(output_weight,up_weight,down_weight)
    far=tuple(swap(x,2) for x in own)
    near=tuple(swap(x,1) for x in own)
    cross=tuple(swap(x,1) for x in far)
    up_rel=jnp.stack([up_bias]+[swap(up_bias,b) for b in (1,2,3)])[:,None,:]
    geo=features(box_coords).astype(BF)
    far_base=((1-chip)*pages).reshape(1).astype(jnp.int32)
    own_base=(chip*pages).reshape(1).astype(jnp.int32)
    proj=(query_weight,key_weight,value_weight,box_weight,query_bias[None],value_bias[None],box_bias[None])
    ctx_f,*saved_f=run_forward(far_base,page_lengths,hidden_in,geo,*proj,pages=pages,rows=PAGE)
    ctx_o,*saved_o=run_forward(own_base,page_lengths,hidden_in,geo,*proj,pages=pages,rows=PAGE)
    ctx=jnp.stack([part(ctx_o,core),swap(part(ctx_o,1-core),1),swap(part(ctx_f,core),2),swap(part(ctx_f,1-core),3)])
    vec=jnp.stack([output_bias,first_gain,first_shift,down_bias,second_gain,second_shift,output_bias,output_bias])
    here=place.reshape(1).astype(jnp.int32)
    layer_out,attn_grad,dctx,act,ug,fl,sl,al,vg,ubg=run_middle(here,hidden_in,output_grad,ctx,own+near+far+cross,up_rel,vec,tile=384)
    d0,d1,d2,d3=(dctx[i] for i in range(4))
    d1=swap(d1,1); d2=swap(d2,2); d3=swap(d3,3)
    order=lambda a,b: jnp.where(core==0,jnp.concatenate([a,b]),jnp.concatenate([b,a]))
    dc_o=order(d0,d1); dc_f=order(d2,d3)
    width=vg.shape[1]//ways
    small=jnp.stack([jnp.concatenate([ubg[g],lax.dynamic_slice_in_dim(vg[:6],(place^g)*width,width,1).reshape(-1,width*ways//2)[:,:].reshape(1,-1)],axis=1) for g in range(ways)])
    small=jnp.pad(small,((0,0),(0,0),(0,8*vg.shape[1]-small.shape[2]))).reshape(ways,8,vg.shape[1])
    size=sum(x.shape[0] for x in own); padded=-(-(size+8)//64)*64
    grads=run_weight_grads(ctx,al,fl,ug,act,sl,small,padded)
    add=lambda a,b: (a.astype(F32)+b.astype(F32)).astype(BF)
    grads=add(grads[:2],swap(grads[2:],1))
    grads=add(grads[0],swap(grads[1],2))
    grads=lax.psum(grads,"dp").astype(F32)
    wide=jnp.concatenate([query_weight,key_weight,value_weight,box_weight],axis=1)
    dx_f,*start=run_backward(far_base,hidden_in,geo,wide,*saved_f,dc_f)
    dx_o,dw,db=run_backward(own_base,hidden_in,geo,wide,*saved_o,dc_o,start=start,last=True)
    half=add(part(dx_f,core),swap(part(dx_f,1-core),1))
    near_half=part(dx_o,core).astype(F32)+swap(part(dx_o,1-core),1).astype(F32)
    input_grad=near_half+swap(half,2).astype(F32)+attn_grad
    dw=lax.psum(dw,"dp").astype(F32)
    db=lax.psum(db[0],"dp")
    h=query_weight.shape[1]
    o=output_weight.shape[0]; f=up_weight.shape[0]
    tail=grads[size:size+8].reshape(-1)
    ubias=tail[:up_bias.shape[0]]
    norms=tail[up_bias.shape[0]:up_bias.shape[0]+6*width].reshape(6,width)
    return (layer_out,input_grad,dw[:,:h],db[:h],dw[:,h:2*h],dw[:,2*h:3*h],db[2*h:3*h],dw[:,3*h:],db[3*h:],
            grads[:o],norms[0],norms[1],norms[2],grads[o:o+f],ubias,grads[o+f:size],norms[3],norms[4],norms[5])


def solution(mesh):
    rep=P()
    in_specs=(P("dp",None),P(None,"dp"),P("dp"),P(None,"tensor"),P("tensor"),P(None,"tensor"),P(None,"tensor"),P("tensor"),
        P(None,"tensor"),P("tensor"),P("tensor",None),rep,rep,rep,P(None,"tensor"),P("tensor"),P("tensor",None),rep,rep,rep,P(("dp","tensor"),None))
    out_specs=(P(("dp","tensor"),None),P(("dp","tensor"),None),P(None,"tensor"),P("tensor"),P(None,"tensor"),P(None,"tensor"),P("tensor"),
        P(None,"tensor"),P("tensor"),P("tensor",None),P("tensor"),P("tensor"),P("tensor"),P(None,"tensor"),P("tensor"),P("tensor",None),P("tensor"),P("tensor"),P("tensor"))
    return jax.shard_map(body,mesh=mesh,in_specs=in_specs,out_specs=out_specs,check_vma=False)
```

time: 1090 us -> 507 us (0.47)
  waiting for transfers between devices: 546 us -> 259 us
  matrix products: 258 us -> 0 us
  Pallas kernels: 0 us -> 125 us
  local copies, waits for them, and re-layouts: 132 us -> 35.2 us
  other arithmetic: 90.1 us -> 35 us
  blocking collectives: 39.5 us -> 23.1 us
  starting transfers between devices: 0.97 us -> 13.8 us
    psum x3 -> x1, waiting for transfers between devices: 395 us -> 122 us  [body(): dw = lax.psum(dw, 'dp').astype(F32)]
    dot_general x81 -> x0, matrix products: 258 us -> none  [the longest x1 25.2 us: body(): jnp.dot(first_full, up_weight, preferred_element_type=jnp.float32) + up_bias]
    ppermute x0 -> x23, waiting for transfers between devices: none -> 137 us  [swap(): return lax.ppermute(x, 'tensor', [(i, i ^ by) for i in range(ways)])]
    pallas_call x0 -> x6, Pallas kernels: none -> 125 us  [the longest x1 41.6 us: run_middle(): pl.pallas_call(partial(middle, tile=tile), out_shape=[S((rows, d), BF), S...]
    reduce_scatter x2 -> x0, waiting for transfers between devices: 94.6 us -> none  [the longest x1 47.8 us: body(): lax.psum_scatter(jnp.einsum('tf,df->td', upper_grad, up_weight, preferred...]
    all_gather x2 -> x0, waiting for transfers between devices: 56.5 us -> none  [the longest x1 37.7 us: body(): lax.all_gather(second_grad.astype(jnp.bfloat16), 'tensor', axis=0, tiled=...]
    reduce_sum x16 -> x0, other arithmetic: 29.3 us -> none  [the longest x2 7.88 us: normalize(): row_mean = jnp.mean(total, axis=-1, keepdims=True)]
    dynamic_update_slice x12 -> x0, local copies, waits for them, and re-layouts: 26.3 us -> none  [body(): lax.map(page_backward, page_blocks + (log_total, by_page(context_grad, HE...]
  transfers between devices with their start and end apart: 8 -> 24, of which waited for: 7 -> 10; matrix products, arithmetic and copies ran while one was open for 22% -> 7% of each run, Pallas kernels for 0% -> 14%
where the time goes in v1:
time: 507 us; the launch traced here: 506 us
  waiting for transfers between devices  259 us (51%)
  Pallas kernels  125 us (25%)
  local copies, waits for them, and re-layouts  35.2 us (7%)
  other arithmetic  35 us (7%)
  blocking collectives  23.1 us (5%)
  between operations  14.5 us (3%)
  starting transfers between devices  13.8 us (3%)
    ppermute x23, waiting for transfers between devices, swap(): return lax.ppermute(x, 'tensor', [(i, i ^ by) for i in range(ways)])  137 us
    psum x1, waiting for transfers between devices, body(): dw = lax.psum(dw, 'dp').astype(F32)  122 us
    pallas_call x1, Pallas kernels, run_middle(): pl.pallas_call(partial(middle, tile=tile), out_shape=[S((rows, d), BF), S...  41.6 us
    pallas_call x2, Pallas kernels, run_backward(): pl.pallas_call(partial(attend_backward, has_start=start is not None, last...  40.9 us
    pallas_call x2, Pallas kernels, run_forward(): pl.pallas_call(partial(attend_forward, rows=rows), out_shape=[jax.ShapeDt...  28.2 us
    psum x1, blocking collectives, body(): db = lax.psum(db[0], 'dp')  23.1 us
    pallas_call x1, Pallas kernels, run_weight_grads(): pl.pallas_call(partial(weight_grads, step=256), out_shape=jax.ShapeDtypeS...  14.4 us
    ppermute x23, starting transfers between devices, swap(): return lax.ppermute(x, 'tensor', [(i, i ^ by) for i in range(ways)])  13.7 us
  transfers between devices with their start and end apart: 24, of which 10 were waited for; matrix products, arithmetic and copies ran while one was open for 7% of the time, Pallas kernels for 14%

profile of v1, /device:TPU:0, one launch (start us, length us, event | category | flops | bytes accessed | tf_op | source)
XLA Modules:
  0.0 506.2 jit_solution(7438657938408307768)
XLA Ops:
  7.2 3.0 collective-permute-start.7
  13.0 0.9 copy.69.wk_ref
  14.0 0.9 copy.70.wv_ref
  15.4 5.7 %cosine_convert_fusion = (bf16[3072,64]{1,0:T(8,128)(2,1)S(1)}, bf16[3072,64]{1,0:T(8,128)(2,1)S(1)}) fusion(f32[3072,64]{1,0:T(8,128)S(1)} %copy.66, f32[64]{0:T(128)S(1)} %mul.58), kind=kLoop, calls=%fused_computation.10 | loop fusion | flops 589824 | bytes 1573120 | tf_op jit(solution)/shard_map/convert.1
  21.2 1.4 pad_maximum_fusion.2.geo_ref
  22.5 14.1 %attend_forward.3 = (bf16[1536,192]{1,0:T(8,128)(2,1)}, bf16[1536,192]{1,0:T(8,128)(2,1)}, bf16[1536,192]{1,0:T(8,128)(2,1)}, bf16[1536,192]{1,0:T(8,128)(2,1)}, bf16[3,3,512,512]{3,2,1,0:T(8,128)(2,1)}) custom-call(s32[1]{0:T(128)} %bitcast.8.base_ref, s32[6]{0:T(128)} %len_ref.3, bf16[3072,768]{1,0:T(8,128)(2,1)} %h_ref.7, ...), custom_call_target="tpu_custom_call" | custom-call | tf_op jit(solution)/shard_map/attend_forward/pallas_call | solution.py:59
  36.6 1.9 constant_dynamic-slice_fusion.7
  39.4 1.2 collective-permute-start.1
  40.5 1.4 collective-permute-start.14
  42.0 35.9 %collective-permute-done.14 = f32[768]{0:T(1024)S(1)} collective-permute-done((f32[768]{0:T(1024)S(1)}, f32[768]{0:T(1024)S(1)}, u32[]{:S(2)}, u32[]{:S(2)}) %collective-permute-start.14) | collective-permute-done | bytes 3104 | tf_op jit(solution)/shard_map/ppermute | solution.py:262
  77.9 1.3 collective-permute-start.13
  79.2 14.1 %attend_forward.2 = (bf16[1536,192]{1,0:T(8,128)(2,1)}, bf16[1536,192]{1,0:T(8,128)(2,1)}, bf16[1536,192]{1,0:T(8,128)(2,1)}, bf16[1536,192]{1,0:T(8,128)(2,1)}, bf16[3,3,512,512]{3,2,1,0:T(8,128)(2,1)}) custom-call(s32[1]{0:T(128)} %bitcast.1.base_ref, s32[6]{0:T(128)} %len_ref.3, bf16[3072,768]{1,0:T(8,128)(2,1)} %h_ref.7, ...), custom_call_target="tpu_custom_call" | custom-call | tf_op jit(solution)/shard_map/attend_forward/pallas_call | solution.py:59
  93.5 1.0 collective-permute-start.12
  94.5 1.2 dynamic-slice_bitcast_fusion
  97.6 4.1 collective-permute-done.3.w3
  101.9 8.9 %collective-permute-done.6.w6 = bf16[192,768]{1,0:T(8,128)(2,1)} collective-permute-done((bf16[192,768]{1,0:T(8,128)(2,1)S(1)}, bf16[192,768]{1,0:T(8,128)(2,1)}, u32[]{:S(2)}, u32[]{:S(2)}) %collective-permute-start.6) | collective-permute-done | bytes 294944 | tf_op jit(solution)/shard_map/ppermute | solution.py:262
  112.2 1.5 pad_maximum_fusion.ctx_any.ctx_ref
  114.5 41.6 %middle.1 = (bf16[768,768]{1,0:T(8,128)(2,1)}, f32[768,768]{1,0:T(8,128)}, bf16[4,768,192]{2,1,0:T(8,128)(2,1)}, bf16[4,768,768]{2,1,0:T(8,128)(2,1)}, bf16[4,76...) custom-call(s32[1]{0:T(128)} %bitcast.t_ref, ...), custom_call_target="tpu_custom_call" | custom-call | tf_op jit(solution)/shard_map/middle/pallas_call | solution.py:158
  158.7 14.4 %weight_grads.1 = bf16[4,1792,768]{2,1,0:T(8,128)(2,1)} custom-call(bf16[4,768,192]{2,1,0:T(8,128)(2,1)} %pad_maximum_fusion.ctx_any.ctx_ref, bf16[768,768]{1,0:T(8,128)(2,1)} %get-tuple-element.64.al_ref, bf16[768,768]{1,0:T(8,128)(2,1)} %get-tuple-element.65.fl_ref, bf16[4,768,768]{2,1,0:T(8,128)(2,1)} %get-tuple-element.66.ug_ref, ...), custom_call_target="tpu_custom_call" | custom-call | tf_op jit(solution)/shard_map/weight_grads/pallas_call | solution.py:186
  173.1 3.1 slice.154
  176.8 8.8 %collective-permute-done.21 = bf16[2,1792,768]{2,1,0:T(8,128)(2,1)} collective-permute-done((bf16[2,1792,768]{2,1,0:T(8,128)(2,1)S(1)}, bf16[2,1792,768]{2,1,0:T(8,128)(2,1)}, u32[]{:S(2)}, u32[]{:S(2)}) %collective-permute-start.21) | collective-permute-done | bytes 5505056 | tf_op jit(solution)/shard_map/ppermute | solution.py:262
  185.5 6.3 %add_convert_fusion = bf16[2,1792,768]{2,1,0:T(8,128)(2,1)} fusion(bf16[2,1792,768]{2,1,0:T(8,128)(2,1)} %collective-permute-done.21, bf16[4,1792,768]{2,1,0:T(8,128)(2,1)S(1)} %copy-done), kind=kLoop, calls=%fused_computation | loop fusion | flops 11010048 | bytes 16515072 | tf_op jit(solution)/shard_map/convert_element_type | solution.py:289
  191.9 3.6 slice_bitcast_fusion
  195.7 1.0 slice_bitcast_fusion.5
  196.7 1.4 collective-permute-start.17
  198.6 1.9 pad_maximum_fusion.1.w_ref
  200.5 65.0 %collective-permute-done.17 = bf16[768,192]{1,0:T(8,128)(2,1)} collective-permute-done((bf16[768,192]{1,0:T(8,128)(2,1)}, bf16[768,192]{1,0:T(8,128)(2,1)}, u32[]{:S(2)}, u32[]{:S(2)}) %collective-permute-start.17) | collective-permute-done | bytes 294944 | tf_op jit(solution)/shard_map/ppermute | solution.py:262
  265.5 9.0 %collective-permute-done.16 = bf16[768,192]{1,0:T(8,128)(2,1)} collective-permute-done((bf16[768,192]{1,0:T(8,128)(2,1)}, bf16[768,192]{1,0:T(8,128)(2,1)}, u32[]{:S(2)}, u32[]{:S(2)}) %collective-permute-start.16) | collective-permute-done | bytes 294944 | tf_op jit(solution)/shard_map/ppermute | solution.py:262
  274.5 2.5 maximum_select_fusion.1.dc_ref
  277.0 20.4 %attend_backward.2 = (bf16[1536,768]{1,0:T(8,128)(2,1)}, f32[768,960]{1,0:T(8,128)}, f32[8,960]{1,0:T(8,128)}) custom-call(s32[1]{0:T(128)} %bitcast.8.base_ref, bf16[3072,768]{1,0:T(8,128)(2,1)} %h_ref.7, bf16[3072,128]{1,0:T(8,128)(2,1)} %pad_maximum_fusion.2.geo_ref, bf16[768,960]{1,0:T(8,128)(2,1)} %pad_maximum_fusion.1.w_ref, ...), custom_call_target="tpu_custom_call" | custom-call | tf_op jit(solution)/shard_map/attend_backward/pallas_call | solution.py:234
  297.4 2.4 maximum_select_fusion.dc_ref
  299.8 20.5 %attend_backward.3 = (bf16[1536,768]{1,0:T(8,128)(2,1)}, bf16[768,960]{1,0:T(8,128)(2,1)}, f32[8,960]{1,0:T(8,128)}) custom-call(s32[1]{0:T(128)} %bitcast.1.base_ref, bf16[3072,768]{1,0:T(8,128)(2,1)} %h_ref.7, bf16[3072,128]{1,0:T(8,128)(2,1)} %pad_maximum_fusion.2.geo_ref, bf16[768,960]{1,0:T(8,128)(2,1)} %pad_maximum_fusion.1.w_ref, ...), custom_call_target="tpu_custom_call" | custom-call | tf_op jit(solution)/shard_map/attend_backward/pallas_call | solution.py:234
  320.3 4.1 fusion
  324.4 1.5 constant_dynamic-slice_fusion.4
  326.6 2.2 collective-permute-done.19
  328.8 1.3 add_convert_fusion.1
  331.2 23.1 %psum.22 = f32[960]{0:T(1024)S(1)} all-reduce(f32[960]{0:T(1024)S(1)} %bitcast.59), channel_id=1, replica_groups=mesh['dp'=8,'tensor'=4] {'dp'}, use_global_device_ids=true, to_apply=%region_1.2 | all-reduce | flops 960 | bytes 7680 | tf_op jit(solution)/shard_map/psum | solution.py:300
  355.6 2.9 collective-permute-done.20
  358.5 4.2 add_add_fusion
  362.7 122.0 %all-reduce.4.cloned.1.call-done = (bf16[768,960]{1,0:T(8,128)(2,1)}, bf16[1792,768]{1,0:T(8,128)(2,1)}) async-done(((bf16[768,960]{1,0:T(8,128)(2,1)}, bf16[1792,768]{1,0:T(8,128)(2,1)}), (bf16[768,960]{1,0:T(8,128)(2,1)}, bf16[1792,768]{1,0:T(8,128)(2,1)})) %all-reduce.4.cloned.1.call-update) | async-done | bytes 4227088 | tf_op jit(solution)/shard_map/psum | solution.py:299
  484.7 1.7 fusion.2
  486.6 1.3 slice.152
  488.7 2.5 fusion.1
  491.3 2.8 convert_element_type.66
  494.1 1.1 copy.77
  495.2 1.1 copy.78
  496.2 1.1 copy.79
  498.0 1.3 slice_reduce_fusion
  (123 shorter events, 17.1 us)
Async XLA Ops:
  7.2 477.6 %all-reduce.4.cloned.1.call-start = ((), (), s32[]{:S(2)}) async-start(), calls=%async_computation | async-start | bytes 8650752 | tf_op jit(solution)/shard_map/psum | solution.py:299
  7.2 89.1 %collective-permute-start.7 = (bf16[768,768]{1,0:T(8,128)(2,1)}, bf16[768,768]{1,0:T(8,128)(2,1)}, u32[]{:S(2)}, u32[]{:S(2)}) collective-permute-start(bf16[768,768]{1,0:T(8,128)(2,1)} %w1.1), channel_id=1, source_target_pairs={{0,2},{1,3},{2,0},{3,1},{4,6},{5,7},{6,4},{7,5},{8,10},{9,11},{10,... | collective-permute-start | bytes 3538952 | tf_op jit(solution)/shard_map/ppermute | solution.py:262
  10.2 86.5 %collective-permute-start.8 = (bf16[768,768]{1,0:T(8,128)(2,1)}, bf16[768,768]{1,0:T(8,128)(2,1)}, u32[]{:S(2)}, u32[]{:S(2)}) collective-permute-start(bf16[768,768]{1,0:T(8,128)(2,1)} %w2.1), channel_id=1, source_target_pairs={{0,2},{1,3},{2,0},{3,1},{4,6},{5,7},{6,4},{7,5},{8,10},{9,11},{10,... | collective-permute-start | bytes 3538952 | tf_op jit(solution)/shard_map/ppermute | solution.py:262
  11.1 1.0 copy-start.11
  11.2 1.8 copy-start.12
  11.2 2.7 copy-start.13
  11.7 3.2 copy-start.24
  36.6 3.9 copy-start.17
  38.6 57.3 %collective-permute-start.2 = (bf16[768,192]{1,0:T(8,128)(2,1)}, bf16[768,192]{1,0:T(8,128)(2,1)S(1)}, u32[]{:S(2)}, u32[]{:S(2)}) collective-permute-start(bf16[768,192]{1,0:T(8,128)(2,1)} %get-tuple-element.144), channel_id=1, source_target_pairs={{0,3},{1,2},{2,1},{3,0},{4,7},{5,6},{6,5},{7,4},{8,11},{9,10},{10,... | collective-permute-start | bytes 884744 | tf_op jit(solution)/shard_map/ppermute | solution.py:262
  39.4 56.8 %collective-permute-start.1 = (bf16[768,192]{1,0:T(8,128)(2,1)S(1)}, bf16[768,192]{1,0:T(8,128)(2,1)S(1)}, u32[]{:S(2)}, u32[]{:S(2)}) collective-permute-start(bf16[768,192]{1,0:T(8,128)(2,1)S(1)} %get-tuple-element.143), channel_id=1, source_target_pairs={{0,2},{1,3},{2,0},{3,1},{4,6},{5,7},{6,4},{7,5},{8,10},{9,11},{10,... | collective-permute-start | bytes 884744 | tf_op jit(solution)/shard_map/ppermute | solution.py:262
  40.5 37.3 %collective-permute-start.14 = (f32[768]{0:T(1024)S(1)}, f32[768]{0:T(1024)S(1)}, u32[]{:S(2)}, u32[]{:S(2)}) collective-permute-start(f32[768]{0:T(1024)S(1)} %copy-done.17), channel_id=1, source_target_pairs={{0,3},{1,2},{2,1},{3,0},{4,7},{5,6},{6,5},{7,4},{8,11},{9,10},{10,... | collective-permute-start | bytes 9224 | tf_op jit(solution)/shard_map/ppermute | solution.py:262
  77.9 15.5 %collective-permute-start.13 = (f32[768]{0:T(1024)S(1)}, f32[768]{0:T(1024)S(1)}, u32[]{:S(2)}, u32[]{:S(2)}) collective-permute-start(f32[768]{0:T(1024)S(1)} %copy-done.17), channel_id=1, source_target_pairs={{0,2},{1,3},{2,0},{3,1},{4,6},{5,7},{6,4},{7,5},{8,10},{9,11},{10,... | collective-permute-start | bytes 9224 | tf_op jit(solution)/shard_map/ppermute | solution.py:262
  93.3 2.5 copy-start.10
  93.4 4.1 copy-start.14
  93.4 17.4 %copy-start.18 = (f32[768]{0:T(1024)S(1)}, f32[768]{0:T(1024)}, u32[]{:S(2)}) copy-start(f32[768]{0:T(1024)} %param.32) | copy-start | bytes 9220
  93.4 17.5 %copy-start.19 = (f32[768]{0:T(1024)S(1)}, f32[768]{0:T(1024)}, u32[]{:S(2)}) copy-start(f32[768]{0:T(1024)} %param.33) | copy-start | bytes 9220
  93.4 17.5 %copy-start.20 = (f32[768]{0:T(1024)S(1)}, f32[768]{0:T(1024)}, u32[]{:S(2)}) copy-start(f32[768]{0:T(1024)} %param.34) | copy-start | bytes 9220
  93.4 17.5 %copy-start.21 = (f32[768]{0:T(1024)S(1)}, f32[768]{0:T(1024)}, u32[]{:S(2)}) copy-start(f32[768]{0:T(1024)} %param.38) | copy-start | bytes 9220
  93.4 17.5 %copy-start.22 = (f32[768]{0:T(1024)S(1)}, f32[768]{0:T(1024)}, u32[]{:S(2)}) copy-start(f32[768]{0:T(1024)} %param.39) | copy-start | bytes 9220
  93.4 17.5 %copy-start.23 = (f32[768]{0:T(1024)S(1)}, f32[768]{0:T(1024)}, u32[]{:S(2)}) copy-start(f32[768]{0:T(1024)} %param.40) | copy-start | bytes 9220
  93.5 2.2 collective-permute-start.12
  95.6 1.8 collective-permute-start
  95.8 18.0 %collective-permute-start.4 = (bf16[768,768]{1,0:T(8,128)(2,1)S(1)}, bf16[768,768]{1,0:T(8,128)(2,1)}, u32[]{:S(2)}, u32[]{:S(2)}) collective-permute-start(bf16[768,768]{1,0:T(8,128)(2,1)S(1)} %copy-done.10), channel_id=1, source_target_pairs={{0,1},{1,0},{2,3},{3,2},{4,5},{5,4},{6,7},{7,6},{8,9},{9,8},{10,11... | collective-permute-start | bytes 3538952 | tf_op jit(solution)/shard_map/ppermute | solution.py:262
  96.2 18.3 %collective-permute-start.5 = (bf16[768,768]{1,0:T(8,128)(2,1)}, bf16[768,768]{1,0:T(8,128)(2,1)}, u32[]{:S(2)}, u32[]{:S(2)}) collective-permute-start(bf16[768,768]{1,0:T(8,128)(2,1)} %w2.1), channel_id=1, source_target_pairs={{0,1},{1,0},{2,3},{3,2},{4,5},{5,4},{6,7},{7,6},{8,9},{9,8},{10,11... | collective-permute-start | bytes 3538952 | tf_op jit(solution)/shard_map/ppermute | solution.py:262
  96.3 18.1 %collective-permute-start.10 = (bf16[768,768]{1,0:T(8,128)(2,1)}, bf16[768,768]{1,0:T(8,128)(2,1)}, u32[]{:S(2)}, u32[]{:S(2)}) collective-permute-start(bf16[768,768]{1,0:T(8,128)(2,1)} %collective-permute-done.7.w7), channel_id=1, source_target_pairs={{0,1},{1,0},{2,3},{3,2},{4,5},{5,4},{6,7},{7,6},{8,9},{9,8},{10,11... | collective-permute-start | bytes 3538952 | tf_op jit(solution)/shard_map/ppermute | solution.py:262
  96.7 17.8 %collective-permute-start.11 = (bf16[768,768]{1,0:T(8,128)(2,1)}, bf16[768,768]{1,0:T(8,128)(2,1)}, u32[]{:S(2)}, u32[]{:S(2)}) collective-permute-start(bf16[768,768]{1,0:T(8,128)(2,1)} %collective-permute-done.8.w8), channel_id=1, source_target_pairs={{0,1},{1,0},{2,3},{3,2},{4,5},{5,4},{6,7},{7,6},{8,9},{9,8},{10,11... | collective-permute-start | bytes 3538952 | tf_op jit(solution)/shard_map/ppermute | solution.py:262
  97.4 4.2 collective-permute-start.3
  101.6 12.1 %copy-start.15 = (bf16[192,768]{1,0:T(8,128)(2,1)}, bf16[192,768]{1,0:T(8,128)(2,1)S(1)}, u32[]{:S(2)}) copy-start(bf16[192,768]{1,0:T(8,128)(2,1)S(1)} %collective-permute-done.3.w3) | copy-start | bytes 884740
  101.6 9.2 %collective-permute-start.6 = (bf16[192,768]{1,0:T(8,128)(2,1)S(1)}, bf16[192,768]{1,0:T(8,128)(2,1)}, u32[]{:S(2)}, u32[]{:S(2)}) collective-permute-start(bf16[192,768]{1,0:T(8,128)(2,1)S(1)} %copy-done.14), channel_id=1, source_target_pairs={{0,2},{1,3},{2,0},{3,1},{4,6},{5,7},{6,4},{7,5},{8,10},{9,11},{10,... | collective-permute-start | bytes 884744 | tf_op jit(solution)/shard_map/ppermute | solution.py:262
  110.8 3.0 collective-permute-start.9
  173.1 12.4 %copy-start = (bf16[4,1792,768]{2,1,0:T(8,128)(2,1)S(1)}, bf16[4,1792,768]{2,1,0:T(8,128)(2,1)}, u32[]{:S(2)}) copy-start(bf16[4,1792,768]{2,1,0:T(8,128)(2,1)} %weight_grads.1) | copy-start | bytes 33030148
  176.2 9.4 %collective-permute-start.21 = (bf16[2,1792,768]{2,1,0:T(8,128)(2,1)S(1)}, bf16[2,1792,768]{2,1,0:T(8,128)(2,1)}, u32[]{:S(2)}, u32[]{:S(2)}) collective-permute-start(bf16[2,1792,768]{2,1,0:T(8,128)(2,1)S(1)} %slice.154), channel_id=1, source_target_pairs={{0,1},{1,0},{2,3},{3,2},{4,5},{5,4},{6,7},{7,6},{8,9},{9,8},{10,11... | collective-permute-start | bytes 16515080 | tf_op jit(solution)/shard_map/ppermute | solution.py:262
  191.8 3.9 copy-start.9
  195.4 124.9 %collective-permute-start.22 = (bf16[1792,768]{1,0:T(8,128)(2,1)}, bf16[1792,768]{1,0:T(8,128)(2,1)S(1)}, u32[]{:S(2)}, u32[]{:S(2)}) collective-permute-start(bf16[1792,768]{1,0:T(8,128)(2,1)} %slice_bitcast_fusion), channel_id=1, source_target_pairs={{0,2},{1,3},{2,0},{3,1},{4,6},{5,7},{6,4},{7,5},{8,10},{9,11},{10,... | collective-permute-start | bytes 8257544 | tf_op jit(solution)/shard_map/ppermute | solution.py:262
  195.7 2.9 copy-start.3
  195.7 2.9 copy-start.4
  195.7 2.9 copy-start.5
  195.7 2.9 copy-start.6
  196.7 68.8 %collective-permute-start.17 = (bf16[768,192]{1,0:T(8,128)(2,1)}, bf16[768,192]{1,0:T(8,128)(2,1)}, u32[]{:S(2)}, u32[]{:S(2)}) collective-permute-start(bf16[768,192]{1,0:T(8,128)(2,1)} %get-tuple-element.138), channel_id=1, source_target_pairs={{0,3},{1,2},{2,1},{3,0},{4,7},{5,6},{6,5},{7,4},{8,11},{9,10},{10,... | collective-permute-start | bytes 884744 | tf_op jit(solution)/shard_map/ppermute | solution.py:262
  198.1 76.4 %collective-permute-start.16 = (bf16[768,192]{1,0:T(8,128)(2,1)}, bf16[768,192]{1,0:T(8,128)(2,1)}, u32[]{:S(2)}, u32[]{:S(2)}) collective-permute-start(bf16[768,192]{1,0:T(8,128)(2,1)} %get-tuple-element.139), channel_id=1, source_target_pairs={{0,2},{1,3},{2,0},{3,1},{4,6},{5,7},{6,4},{7,5},{8,10},{9,11},{10,... | collective-permute-start | bytes 884744 | tf_op jit(solution)/shard_map/ppermute | solution.py:262
  198.5 98.9 %collective-permute-start.15 = (bf16[768,192]{1,0:T(8,128)(2,1)S(1)}, bf16[768,192]{1,0:T(8,128)(2,1)}, u32[]{:S(2)}, u32[]{:S(2)}) collective-permute-start(bf16[768,192]{1,0:T(8,128)(2,1)S(1)} %get-tuple-element.140), channel_id=1, source_target_pairs={{0,1},{1,0},{2,3},{3,2},{4,5},{5,4},{6,7},{7,6},{8,9},{9,8},{10,11... | collective-permute-start | bytes 884744 | tf_op jit(solution)/shard_map/ppermute | solution.py:262
  324.4 2.0 copy-start.7
  325.9 2.9 copy-start.8
  325.9 2.9 collective-permute-start.19
  326.5 29.1 %collective-permute-start.18 = (bf16[768,768]{1,0:T(8,128)(2,1)S(1)}, bf16[768,768]{1,0:T(8,128)(2,1)}, u32[]{:S(2)}, u32[]{:S(2)}) collective-permute-start(bf16[768,768]{1,0:T(8,128)(2,1)S(1)} %constant_dynamic-slice_fusion.5), channel_id=1, source_target_pairs={{0,1},{1,0},{2,3},{3,2},{4,5},{5,4},{6,7},{7,6},{8,9},{9,8},{10,11... | collective-permute-start | bytes 3538952 | tf_op jit(solution)/shard_map/ppermute | solution.py:262
  330.2 28.3 %collective-permute-start.20 = (bf16[768,768]{1,0:T(8,128)(2,1)}, bf16[768,768]{1,0:T(8,128)(2,1)}, u32[]{:S(2)}, u32[]{:S(2)}) collective-permute-start(bf16[768,768]{1,0:T(8,128)(2,1)} %add_convert_fusion.1), channel_id=1, source_target_pairs={{0,2},{1,3},{2,0},{3,1},{4,6},{5,7},{6,4},{7,5},{8,10},{9,11},{10,... | collective-permute-start | bytes 3538952 | tf_op jit(solution)/shard_map/ppermute | solution.py:262
  484.7 1.8 copy-start.2
  484.7 3.1 copy-start.1
  (1 other events, 0.7 us)
Sparse Core Ops, SparseCore 0:
  324.5 160.1 all-reduce.3

commit v2 on v1

v2 whole, which is shorter than its diff:
```python
import math
from functools import partial
import jax, jax.numpy as jnp
from jax import lax
from jax.experimental import pallas as pl
from jax.experimental.pallas import tpu as pltpu
from jax.sharding import PartitionSpec as P
HEAD=64; POS=128; PAGE=512
F32=jnp.float32; BF=jnp.bfloat16
LOG2E=1.4426950408889634

def mm(a,b): return jnp.dot(a,b,preferred_element_type=F32)
def mm_nt(a,b): return lax.dot_general(a,b,(((1,),(1,)),((),())),preferred_element_type=F32)
def mm_tn(a,b): return lax.dot_general(a,b,(((0,),(0,)),((),())),preferred_element_type=F32)

def mixing(geo):
    half=POS//2
    c=geo[:,:half]; s=geo[:,half:]
    return jnp.concatenate([c,-c],axis=1), jnp.concatenate([s,s],axis=1)

def mix(coeff, cos_sign, sin_twice):
    return coeff*cos_sign + pltpu.roll(coeff, POS//2, 1)*sin_twice

EPS=1e-05

def normal(z):
    mean=jnp.mean(z,axis=1,keepdims=True)
    centred=z-mean
    inverse=lax.rsqrt(jnp.mean(centred*centred,axis=1,keepdims=True)+EPS)
    return centred*inverse, inverse

def normal_back(inner, scaled, inverse):
    return inverse*(inner-jnp.mean(inner,axis=1,keepdims=True)-scaled*jnp.mean(inner*scaled,axis=1,keepdims=True))

def columns(x): return jnp.sum(x,axis=0,keepdims=True)

def middle(t_ref, hid_any, og_any, ctx_any, w0, w1, w2, w3, w4, w5, w6, w7, w8, w9, w10, w11, ub_ref, vec_ref,
           out_any, ag_any, dctx_any, act_any, ug_any, fl_any, sl_any, al_any, small_ref,
           hid, og, ctx, wo, wu, wd, act, ug, fl, sl, al, lo, ag, first, scaled1, inv1, ffn, dctx, vg_ref, sem_in, sem_w, sem_out, *, tile):
    rows,d=hid.shape
    groups=wu.shape[0]
    weights=(w0,w1,w2,w3,w4,w5,w6,w7,w8,w9,w10,w11)
    head_loads=[pltpu.make_async_copy(hid_any.at[pl.ds(t_ref[0]*rows,rows)],hid,sem_in.at[0]),
           pltpu.make_async_copy(og_any,og,sem_in.at[1]),
           pltpu.make_async_copy(ctx_any,ctx,sem_in.at[2])]
    loads=[[pltpu.make_async_copy(weights[3*g+k],(wo,wu,wd)[k].at[g],sem_w.at[k,g]) for g in range(groups)] for k in range(3)]
    for c in head_loads: c.start()
    for k in range(3):
        for c in loads[k]: c.start()
    for c in head_loads: c.wait()
    for c in loads[0]: c.wait()
    ob,g1,s1,db,g2,s2=(vec_ref[i:i+1,:] for i in range(6))
    vg_ref[...]=jnp.zeros_like(vg_ref)
    small_ref[...]=jnp.zeros_like(small_ref)
    for c in loads[1]: c.wait()
    for c in loads[2]: c.wait()
    def step(i,_):
        r=pl.ds(pl.multiple_of(i*tile,tile),tile)
        attn=mm(ctx[0,r],wo[0])
        for g in range(1,groups): attn=attn+mm(ctx[g,r],wo[g])
        scaled,inverse=normal(attn+ob+hid[r].astype(F32))
        f=scaled*g1+s1
        first[...]=f
        scaled1[...]=scaled
        inv1[...]=inverse
        fl[r]=f.astype(BF)
        ffn[...]=jnp.zeros_like(ffn)
        def up(g,_):
            x=mm(fl[r],wu[g])+ub_ref[g]
            half=0.5+0.5*lax.erf(x*0.7071067811865476)
            a=(x*half).astype(BF)
            act[g,r]=a
            ug[g,r]=(half+x*jnp.exp(-0.5*x*x)*0.3989422804014327).astype(BF)
            ffn[...]+=mm(a,wd[g])
            return 0
        lax.fori_loop(0,groups,up,0)
        scaled,inverse=normal(ffn[...]+db+first[...])
        lo[r]=(scaled*g2+s2).astype(BF)
        o=og[r].astype(F32)
        second=normal_back(o*g2,scaled,inverse)
        vg_ref[3:4,:]+=columns(second)
        vg_ref[4:5,:]+=columns(o*scaled)
        vg_ref[5:6,:]+=columns(o)
        sl[r]=second.astype(BF)
        ffn[...]=second
        def down(g,_):
            u=(mm_nt(sl[r],wd[g])*ug[g,r].astype(F32)).astype(BF)
            ug[g,r]=u
            small_ref[g,0:1,:]+=columns(u.astype(F32))
            ffn[...]+=mm_nt(u,wu[g])
            return 0
        lax.fori_loop(0,groups,down,0)
        fg=ffn[...]
        scaled=scaled1[...]
        a=normal_back(fg*g1,scaled,inv1[...])
        vg_ref[0:1,:]+=columns(a)
        vg_ref[1:2,:]+=columns(fg*scaled)
        vg_ref[2:3,:]+=columns(fg)
        ag[r]=a
        alow=a.astype(BF)
        al[r]=alow
        for g in range(groups): dctx[g,r]=mm_nt(alow,wo[g]).astype(BF)
        return 0
    lax.fori_loop(0,rows//tile,step,0)
    width=d//groups
    for a in range(groups):
        small_ref[a^t_ref[0],1:7,:width]=vg_ref[0:6,a*width:(a+1)*width]
    stores=[pltpu.make_async_copy(a,b,sem_out.at[i]) for i,(a,b) in enumerate(((dctx,dctx_any),(act,act_any),(ug,ug_any),(fl,fl_any),(sl,sl_any),(al,al_any),(lo,out_any),(ag,ag_any)))]
    for c in stores: c.start()
    for c in stores: c.wait()

def run_middle(t, hidden, og, ctx, weights, ub, vec, tile=256):
    rows,d=og.shape; groups=4; q=weights[0].shape[0]; f=weights[1].shape[1]
    anyspec=pl.BlockSpec(memory_space=pl.ANY)
    vm=pl.BlockSpec(memory_space=pltpu.VMEM)
    S=jax.ShapeDtypeStruct
    return pl.pallas_call(partial(middle,tile=tile),
        out_shape=[S((rows,d),BF),S((rows,d),F32),S((groups,rows,q),BF),S((groups,rows,f),BF),S((groups,rows,f),BF),S((rows,d),BF),S((rows,d),BF),S((rows,d),BF),S((groups,8,d),F32)],
        in_specs=[pl.BlockSpec(memory_space=pltpu.SMEM)]+[anyspec]*15+[vm,vm],
        out_specs=[anyspec]*8+[vm],
        scratch_shapes=[pltpu.VMEM((rows,d),BF),pltpu.VMEM((rows,d),BF),pltpu.VMEM((groups,rows,q),BF),
            pltpu.VMEM((groups,q,d),BF),pltpu.VMEM((groups,d,f),BF),pltpu.VMEM((groups,f,d),BF),
            pltpu.VMEM((groups,rows,f),BF),pltpu.VMEM((groups,rows,f),BF),
            pltpu.VMEM((rows,d),BF),pltpu.VMEM((rows,d),BF),pltpu.VMEM((rows,d),BF),pltpu.VMEM((rows,d),BF),pltpu.VMEM((rows,d),F32),
            pltpu.VMEM((tile,d),F32),pltpu.VMEM((tile,d),F32),pltpu.VMEM((tile,1),F32),pltpu.VMEM((tile,d),F32),
            pltpu.VMEM((groups,rows,q),BF),pltpu.VMEM((8,d),F32),
            pltpu.SemaphoreType.DMA((3,)),pltpu.SemaphoreType.DMA((3,groups)),pltpu.SemaphoreType.DMA((8,))],
        compiler_params=pltpu.CompilerParams(vmem_limit_bytes=62<<20),
        name="middle",
    )(t,hidden,og,ctx,*weights,ub,vec)


MESH=pl.DeviceIdType.MESH

def remote(src,dst,sent,got,device):
    return pltpu.make_async_remote_copy(src_ref=src,dst_ref=dst,send_sem=sent,recv_sem=got,device_id=device,device_id_type=MESH)

def seats():
    group=lax.axis_index("dp"); place=lax.axis_index("tensor")
    core=lax.rem(place,2); chip=place//2
    near=place+1-2*core
    far=place+2-4*chip
    cross=far+1-2*core
    return group,place,core,chip,near,far,cross

def greet(devices):
    barrier=pltpu.get_barrier_semaphore()
    for device in devices:
        pl.semaphore_signal(barrier,inc=1,device_id=device,device_id_type=MESH)
    pl.semaphore_wait(barrier,len(devices))

def page_of(i,pages):
    chip=lax.axis_index("tensor")//2
    return jnp.where(i<pages,(1-chip)*pages+i,chip*pages+i-pages)

PART=192

def forward_kernel(len_ref, h_ref, geo_ref, w_ref, qb_ref, vb_ref, bb_ref, wo_any, wu_any, wd_any, ub_any,
                   q_ref, k_ref, v_ref, p_ref, ctx_any, no_any, nu_any, nd_any, fo_any, fu_any, fd_any, co_any, cu_any, cd_any, ua_any,
                   cat_q, cat_k, cpage, x_s, x_r, y_s, y_r, n_s, n_r, c_s, c_r, u_s, u_r, t_s, t_r, *, pages):
    i=pl.program_id(0)
    heads=q_ref.shape[1]//HEAD; cols=q_ref.shape[1]
    group,place,core,chip,near,far,cross=seats()
    side=lax.rem(group,2)
    beside=group+1-2*side
    own=(wo_any,wu_any,wd_any); nears=(no_any,nu_any,nd_any); fars=(fo_any,fu_any,fd_any); crosses=(co_any,cu_any,cd_any)
    chunks=[]
    for a,w in enumerate(own):
        half=w.shape[0]//2; step=min(PART,half)
        chunks+=[(a,s,step) for s in range(0,half,step)]
    def rows(c,other):
        a,s,n=chunks[c]
        half=own[a].shape[0]//2
        return a,pl.ds(pl.multiple_of(half*(1-side if other else side)+s,16),n)
    def x_copy(c):
        a,r=rows(c,False)
        return remote(own[a].at[r],fars[a].at[r],x_s.at[c],x_r.at[c],(group,far))
    def y_copy(c):
        a,r=rows(c,False)
        return remote(fars[a].at[r],fars[a].at[r],y_s.at[c],y_r.at[c],(beside,place))
    def y_got(c):
        a,r=rows(c,True)
        return remote(fars[a].at[r],fars[a].at[r],y_s.at[c],y_r.at[c],(beside,place))
    def c_copy(c,other):
        a,r=rows(c,other)
        k=1 if other else 0
        return remote(fars[a].at[r],crosses[a].at[r],c_s.at[k,c],c_r.at[k,c],(group,near))
    n_copies=[remote(own[a],nears[a],n_s.at[a],n_r.at[a],(group,near)) for a in range(3)]
    u_copies=[remote(ub_any,ua_any.at[g],u_s.at[g-1],u_r.at[g-1],(group,d)) for g,d in ((1,near),(2,far),(3,cross))]
    u_local=pltpu.make_async_copy(ub_any,ua_any.at[0],u_s.at[3])
    @pl.when(i==0)
    def _():
        greet([(group,near),(group,far),(group,cross),(beside,place)])
        for c in range(len(chunks)): x_copy(c).start()
        for n in n_copies: n.start()
        for u in u_copies: u.start()
        u_local.start()
    length=len_ref[page_of(i,pages)]
    h=h_ref[...]
    geo=geo_ref[...]
    q_ref[...]=(mm(h,w_ref[:,:cols])+qb_ref[...]).astype(BF)
    k_ref[...]=mm(h,w_ref[:,cols:2*cols]).astype(BF)
    v_ref[...]=(mm(h,w_ref[:,2*cols:3*cols])+vb_ref[...]).astype(BF)
    cs,ss=mixing(geo.astype(F32))
    for head in range(heads):
        coeff=mm(h,w_ref[:,3*cols+head*POS:3*cols+(head+1)*POS])+bb_ref[:,head*POS:(head+1)*POS]
        cat_q[head,:,:POS]=mix(coeff,cs,ss).astype(BF)
        cat_q[head,:,POS:]=q_ref[:,head*HEAD:(head+1)*HEAD]
        cat_k[head,:,:POS]=geo
        cat_k[head,:,POS:]=k_ref[:,head*HEAD:(head+1)*HEAD]
    valid=lax.broadcasted_iota(jnp.int32,(1,PAGE),1)<length
    scale=LOG2E/math.sqrt(HEAD)
    half=PAGE//2
    for head in range(heads):
        s=mm_nt(cat_q[head],cat_k[head])
        s=jnp.where(valid,s,-1e30)
        top=jnp.max(s,axis=1,keepdims=True)
        e=jnp.exp2((s-top)*scale)
        total=jnp.sum(e,axis=1,keepdims=True)
        p=(e*(1.0/total)).astype(BF)
        p_ref[head]=p
        c=mm(p,v_ref[:,head*HEAD:(head+1)*HEAD]).astype(BF)
        for k in range(2): cpage[2*i+k,:,head*HEAD:(head+1)*HEAD]=c[k*half:(k+1)*half]
    def context_copy(k):
        piece=2*lax.rem(i,pages)+k
        oc=piece//pages
        slot=lax.rem(piece,pages)
        return piece,oc,slot
    for k in range(2):
        piece,oc,slot=context_copy(k)
        mine=oc==core
        @pl.when(i<pages)
        def _():
            g=jnp.where(mine,2,3)
            remote(cpage.at[2*i+k],ctx_any.at[g,slot],t_s.at[2*i+k],t_r.at[g,slot],(group,2*(1-chip)+oc)).start()
        @pl.when((i>=pages) & jnp.logical_not(mine))
        def _():
            remote(cpage.at[2*i+k],ctx_any.at[1,slot],t_s.at[2*i+k],t_r.at[1,slot],(group,near)).start()
        @pl.when((i>=pages) & mine)
        def _():
            pltpu.make_async_copy(cpage.at[2*i+k],ctx_any.at[0,slot],t_r.at[0,slot]).start()
    count=2*pages
    plan={0:[0],1:[1],3:[2],4:[3],5:[4]}
    left=[c for c in range(len(chunks)) if not any(c in v for v in plan.values())]
    for at,todo in plan.items():
        @pl.when(i==at)
        def _():
            for c in todo:
                x_copy(c).wait_recv()
                y_copy(c).start()
                c_copy(c,False).start()
    @pl.when(i==count-1)
    def _():
        for c in left:
            x_copy(c).wait_recv()
            y_copy(c).start()
            c_copy(c,False).start()
        for c in range(len(chunks)):
            y_got(c).wait_recv()
            c_copy(c,True).start()
        for n in n_copies: n.wait()
        for u in u_copies: u.wait()
        u_local.wait()
        for slot in range(pages):
            pltpu.make_async_copy(ctx_any.at[0,slot],ctx_any.at[0,slot],t_r.at[0,slot]).wait()
            for g in (1,2,3):
                pltpu.make_async_copy(ctx_any.at[g,slot],ctx_any.at[g,slot],t_r.at[g,slot]).wait()
        for j in range(2*count):
            if j<count:
                pltpu.make_async_copy(cpage.at[j],cpage.at[j],t_s.at[j]).wait()
            else:
                @pl.when((j-count)//pages!=core)
                def _():
                    pltpu.make_async_copy(cpage.at[j],cpage.at[j],t_s.at[j]).wait()
        for c in range(len(chunks)):
            x_copy(c).wait_send()
            y_copy(c).wait_send()
            c_copy(c,False).wait()
            c_copy(c,True).wait()

def run_forward(lengths, hidden, geo, w, qb, vb, bb, wo, wu, wd, ub):
    cols=qb.shape[1]; heads=cols//HEAD; d=hidden.shape[1]
    pages=lengths.shape[0]//2
    page_in=lambda n: pl.BlockSpec((PAGE,n),lambda i:(page_of(i,pages),0))
    page_out=lambda n: pl.BlockSpec((PAGE,n),lambda i:(i,0))
    whole=lambda a: pl.BlockSpec(a.shape,lambda i:(0,0),pipeline_mode=pl.Buffered(1))
    anyspec=pl.BlockSpec(memory_space=pl.ANY)
    S=jax.ShapeDtypeStruct
    half=PAGE//2
    own=(wo,wu,wd)
    n=sum((x.shape[0]//2)//min(PART,x.shape[0]//2) for x in own)
    D=pltpu.SemaphoreType.DMA
    return pl.pallas_call(partial(forward_kernel,pages=pages),
        out_shape=[S((2*pages*PAGE,cols),BF)]*3+[S((2*pages,heads,PAGE,PAGE),BF),S((4,pages,half,cols),BF)]+[S(x.shape,BF) for x in own]*3+[S((4,)+ub.shape,F32)],
        grid=(2*pages,),
        in_specs=[pl.BlockSpec(memory_space=pltpu.SMEM),page_in(d),page_in(POS)]+[whole(a) for a in (w,qb,vb,bb)]+[anyspec]*4,
        out_specs=[page_out(cols)]*3+[pl.BlockSpec((pl.Squeezed(),heads,PAGE,PAGE),lambda i:(i,0,0,0))]+[anyspec]*11,
        scratch_shapes=[pltpu.VMEM((heads,PAGE,POS+HEAD),BF)]*2+[pltpu.VMEM((4*pages,half,cols),BF),
            D((n,)),D((n,)),D((n,)),D((n,)),D((3,)),D((3,)),D((2,n)),D((2,n)),D((4,)),D((3,)),D((4*pages,)),D((4,pages))],
        compiler_params=pltpu.CompilerParams(vmem_limit_bytes=56<<20,collective_id=0,has_side_effects=True),
        name="forward",
    )(lengths,hidden,geo,w,qb,vb,bb,wo,wu,wd,ub)

BLOCK=256

def cube(x,pr): return x.reshape(x.shape[0]//pr,pr,x.shape[1])

class Reduce:
    def __init__(self,main,yrecv,zrecv,final,out,sems,group,place,m):
        self.main,self.yrecv,self.zrecv,self.final,self.out=main,yrecv,zrecv,final,out
        self.sems=sems; self.m=m; self.place=place
        self.side=lax.rem(group,2); self.z=group//2
        self.beside=group+1-2*self.side
    def half(self,j,s): return pl.ds((2*j+s)*self.m,self.m)
    def y_copy(self,j):
        return remote(self.main.at[self.half(j,1-self.side)],self.yrecv.at[j],self.sems.at[0,j],self.sems.at[1,j],(self.beside,self.place))
    def y_add(self,j):
        self.y_copy(j).wait_recv()
        def one(k,_):
            at=(2*j+self.side)*self.m+k
            self.main[at]=(self.main[at].astype(F32)+self.yrecv[j,k].astype(F32)).astype(BF)
            return 0
        lax.fori_loop(0,self.m,one,0)
        def send(k,_):
            z=lax.rem(self.z+k,self.m)
            remote(self.main.at[(2*j+self.side)*self.m+z],self.zrecv.at[j,self.m-k-1],self.sems.at[2,j],self.sems.at[3,j],(2*z+self.side,self.place)).start()
            return 0
        lax.fori_loop(1,self.m,send,0)
    def z_add(self,j):
        pltpu.make_async_copy(self.zrecv.at[j],self.zrecv.at[j],self.sems.at[3,j]).wait()
        def one(k,acc): return acc+self.zrecv[j,k].astype(F32)
        acc=lax.fori_loop(0,self.m-1,one,self.main[(2*j+self.side)*self.m+self.z].astype(F32))
        self.final[j]=acc.astype(BF)
        at=(2*j+self.side)*self.m+self.z
        pltpu.make_async_copy(self.final.at[j],self.out.at[at],self.sems.at[8,j]).start()
        def send(k,_):
            z=lax.rem(self.z+k,self.m)
            remote(self.final.at[j],self.out.at[at],self.sems.at[4,j],self.sems.at[5,j],(2*z+self.side,self.place)).start()
            return 0
        lax.fori_loop(1,self.m,send,0)
    def g_copy(self,j):
        here=self.half(j,self.side)
        return remote(self.out.at[here],self.out.at[here],self.sems.at[6,j],self.sems.at[7,j],(self.beside,self.place))
    def g_send(self,j):
        pltpu.make_async_copy(self.zrecv.at[j],self.zrecv.at[j],self.sems.at[5,j]).wait()
        pltpu.make_async_copy(self.final.at[j],self.final.at[j],self.sems.at[8,j]).wait()
        self.g_copy(j).start()
    def finish(self,j):
        self.g_copy(j).wait()
        self.y_copy(j).wait_send()
        pltpu.make_async_copy(self.zrecv.at[j],self.zrecv.at[j],self.sems.at[2,j]).wait()
        pltpu.make_async_copy(self.zrecv.at[j],self.zrecv.at[j],self.sems.at[4,j]).wait()

def backward_kernel(h_ref, geo_ref, w_ref, q_ref, k_ref, v_ref, p_ref, small_ref, dctx_any, act_any, ug_any, fl_any, sl_any, al_any, ctx_any, ag_any,
                    fin_any, afin_any, ig_any,
                    act, ug, fl, sl, ctx, cs, crecv, gx, xrecv, main, yrecv, zrecv, final,
                    amain, ayrecv, azrecv, afinal, dc, dcp, total, btotal, mixed, keep, give, drecv, dxrecv, ag,
                    l_sem, c_s, c_r, x_s, x_r, r_sem, a_sem, e_s, e_r, d_s, d_r, f_s, f_r, o_sem, *, pages, m, blocks, per):
    i=pl.program_id(0)
    count=2*pages
    group,place,core,chip,near,far,cross=seats()
    cols=q_ref.shape[1]; heads=cols//HEAD; d=h_ref.shape[1]
    pr=main.shape[1]; pb=BLOCK//pr
    f=act.shape[2]; qc=ctx.shape[2]
    chunks=blocks//per; achunks=amain.shape[0]//(2*m)
    ffn=Reduce(main,yrecv,zrecv,final,fin_any,r_sem,group,place,m)
    att=Reduce(amain,ayrecv,azrecv,afinal,afin_any,a_sem,group,place,m)
    loads=[pltpu.make_async_copy(a,b,l_sem.at[n]) for n,(a,b) in enumerate(((sl_any,sl),(act_any,act),(fl_any,fl),(ug_any,ug),(al_any,act.at[0]),(ctx_any,ctx)))]
    e_copies=[remote(dctx_any.at[g],dc.at[g],e_s.at[g-1],e_r.at[g-1],(group,t)) for g,t in ((2,far),(3,cross),(1,near))]
    e_local=pltpu.make_async_copy(dctx_any.at[0],dc.at[0],e_s.at[3])
    ag_loads=[pltpu.make_async_copy(ag_any.at[pl.ds(k*BLOCK,BLOCK)],ag.at[k],l_sem.at[6+k]) for k in range(pages)]
    def c_copy(b,slot): return remote(cs.at[slot],crecv.at[b],c_s.at[b],c_r.at[b],(group,near))
    def x_copy(b): return remote(gx.at[b],xrecv.at[b],x_s.at[b],x_r.at[b],(group,far))
    def span(b): return pl.ds(b*pb,pb)
    def put(b,g,value):
        value=cube(value.astype(BF),pr)
        if g==0: main[span(b)]=value
        elif g==2: gx[b]=value
        else: cs[lax.rem(b,2),g//2]=value
    def c_add(b):
        c_copy(b,lax.rem(b,2)).wait_recv()
        def one(k,_):
            at=b*pb+k
            main[at]=(main[at].astype(F32)+crecv[b,0,k].astype(F32)).astype(BF)
            gx[b,k]=(gx[b,k].astype(F32)+crecv[b,1,k].astype(F32)).astype(BF)
            return 0
        lax.fori_loop(0,pb,one,0)
        x_copy(b).start()
    def x_add(b):
        x_copy(b).wait_recv()
        def one(k,_):
            at=b*pb+k
            main[at]=(main[at].astype(F32)+xrecv[b,k].astype(F32)).astype(BF)
            return 0
        lax.fori_loop(0,pb,one,0)

    @pl.when(i==0)
    def _():
        peers=[(group,near),(group,far),(group,cross),(ffn.beside,place)]
        barrier=pltpu.get_barrier_semaphore()
        for device in peers:
            pl.semaphore_signal(barrier,inc=1,device_id=device,device_id_type=MESH)
        def call(k,_):
            z=lax.rem(ffn.z+k,m)
            pl.semaphore_signal(barrier,inc=1,device_id=(2*z+ffn.side,place),device_id_type=MESH)
            return 0
        lax.fori_loop(1,m,call,0)
        for n in (0,1,2,3,5): loads[n].start()
        for c in ag_loads: c.start()
        pl.semaphore_wait(barrier,len(peers)+m-1)
        for c in e_copies: c.start()
        e_local.start()
        def block(b,kind):
            slot=lax.rem(b,2)
            @pl.when(b>=2)
            def _(): c_copy(b-2,slot).wait_send()
            if kind=="down":
                r=pl.ds(pl.multiple_of(b*BLOCK,BLOCK),BLOCK)
                for g in range(4): put(b,g,mm_tn(act[g,:,r],sl[...]))
            elif kind=="up":
                r=pl.ds(pl.multiple_of((b-f//BLOCK)*BLOCK,BLOCK),BLOCK)
                for g in range(4): put(b,g,mm_tn(fl[:,r],ug[g]))
            elif kind=="out":
                for g in range(4):
                    top=mm_tn(ctx[g],act[0])
                    pad=jnp.concatenate([top,small_ref[g],jnp.zeros((BLOCK-qc-small_ref.shape[1],d),F32)],axis=0)
                    put(b,g,pad)
            else:
                for g in range(4): put(b,g,jnp.zeros((BLOCK,d),F32))
            c_copy(b,slot).start()
            @pl.when(b>=1)
            def _(): c_add(b-1)
        loads[0].wait(); loads[1].wait()
        lax.fori_loop(0,f//BLOCK,lambda b,_: (block(b,"down"),0)[1],0)
        loads[4].start()
        loads[2].wait(); loads[3].wait()
        lax.fori_loop(f//BLOCK,(f+d)//BLOCK,lambda b,_: (block(b,"up"),0)[1],0)
        loads[4].wait(); loads[5].wait()
        block((f+d)//BLOCK,"out")
        for b in range((f+d)//BLOCK+1,blocks): block(b,"zero")
        c_add(blocks-1)
        for b in (blocks-2,blocks-1): c_copy(b,b%2).wait_send()
        total[...]=jnp.zeros_like(total); btotal[...]=jnp.zeros_like(btotal)
        for c in e_copies: c.wait_recv()
        e_local.wait()

    half=PAGE//2
    for k in range(2):
        piece=2*lax.rem(i,pages)+k
        g=jnp.where(piece//pages==core,0,1)+jnp.where(i<pages,2,0)
        dcp[k*half:(k+1)*half,:]=dc[g,lax.rem(piece,pages)]
    geo=geo_ref[...]
    co,si=mixing(geo.astype(F32))
    factor=1.0/math.sqrt(HEAD)
    for head in range(heads):
        lanes=slice(head*HEAD,(head+1)*HEAD)
        p=p_ref[head]
        dcl=dcp[:,lanes]
        mixed[:,2*cols+head*HEAD:2*cols+(head+1)*HEAD]=mm_tn(p,dcl).astype(BF)
        dp=mm_nt(dcl,v_ref[:,lanes])
        pf=p.astype(F32)
        delta=jnp.sum(pf*dp,axis=1,keepdims=True)
        ds=(pf*(dp-delta)).astype(BF)
        both=mm(ds,jnp.concatenate([geo,k_ref[:,lanes]],axis=1))*factor
        mixed[:,lanes]=both[:,POS:].astype(BF)
        mixed[:,3*cols+head*POS:3*cols+(head+1)*POS]=mix(both[:,:POS],co,si).astype(BF)
        mixed[:,cols+head*HEAD:cols+(head+1)*HEAD]=(mm_tn(ds,q_ref[:,lanes])*factor).astype(BF)
    total[...]+=mm_tn(h_ref[...],mixed[...])
    btotal[0:1,:]+=jnp.sum(mixed[...].astype(F32),axis=0,keepdims=True)
    def d_copy(kind,slot): return remote(give.at[kind,slot],drecv.at[kind,slot],d_s.at[kind,slot],d_r.at[kind,slot],(group,near))
    def f_copy(slot): return remote(keep.at[0,slot],dxrecv.at[slot],f_s.at[slot],f_r.at[slot],(group,far))
    kind=jnp.where(i<pages,0,1)
    for k in range(2):
        piece=2*lax.rem(i,pages)+k
        slot=lax.rem(piece,pages)
        value=mm_nt(mixed[k*half:(k+1)*half,:],w_ref[...]).astype(BF)
        mine=piece//pages==core
        @pl.when(mine)
        def _(): keep[kind,slot]=value
        @pl.when(jnp.logical_not(mine))
        def _():
            give[kind,slot]=value
            d_copy(kind,slot).start()
    @pl.when(i==pages)
    def _():
        for slot in range(pages):
            d_copy(0,slot).wait_recv()
            keep[0,slot]=(keep[0,slot].astype(F32)+drecv[0,slot].astype(F32)).astype(BF)
            f_copy(slot).start()

    def advance(s):
        b=s
        @pl.when((b>=0)&(b<blocks))
        def _():
            x_add(b)
            @pl.when(b==(f+d)//BLOCK)
            def _():
                at=b*pb+qc//pr
                bias=btotal[0:1,:]
                row=jnp.concatenate([bias[:,:cols],bias[:,2*cols:]],axis=1)
                sub=qc%pr
                eight=jnp.where(lax.broadcasted_iota(jnp.int32,(16,d),0)==7,row,0.0)
                main[at,sub:sub+16,:]=(main[at,sub:sub+16,:].astype(F32)+eight).astype(BF)
            @pl.when(lax.rem(b+1,per)==0)
            def _(): ffn.y_copy(b//per).start()
        c=s-per
        ready=lambda c: (c>=0)&(c<blocks)&(lax.rem(c+1,per)==0)
        @pl.when(ready(s-1))
        def _(): ffn.y_add((s-1)//per)
        @pl.when(ready(s-2))
        def _(): ffn.z_add((s-2)//per)
        @pl.when(ready(s-3))
        def _(): ffn.g_send((s-3)//per)
    @pl.when((i>=1)&(i<count-1))
    def _(): advance(i-1)

    @pl.when(i==count-1)
    def _():
        rows=amain.shape[0]*pr
        for b in range(rows//BLOCK):
            if b*BLOCK<d: amain[span(b)]=cube(total[b*BLOCK:(b+1)*BLOCK,:].astype(BF),pr)
            else: amain[span(b)]=jnp.zeros((pb,pr,total.shape[1]),BF)
        for j in range(achunks): att.y_copy(j).start()
        advance(count-2)
        for j in range(achunks): att.y_add(j)
        advance(count-1)
        for j in range(achunks): att.z_add(j)
        advance(count)
        for j in range(achunks): att.g_send(j)
        lax.fori_loop(count+1,blocks+3,lambda s,_: (advance(s),0)[1],0)
        for slot in range(pages):
            d_copy(1,slot).wait_recv()
            f_copy(slot).wait_recv()
            ag_loads[slot].wait()
            ag[slot]=ag[slot]+keep[1,slot].astype(F32)+drecv[1,slot].astype(F32)+dxrecv[slot].astype(F32)
            pltpu.make_async_copy(ag.at[slot],ig_any.at[pl.ds(slot*BLOCK,BLOCK)],o_sem.at[slot]).start()
        for slot in range(pages):
            pltpu.make_async_copy(ag.at[slot],ig_any.at[pl.ds(slot*BLOCK,BLOCK)],o_sem.at[slot]).wait()
            f_copy(slot).wait_send()
            d_copy(0,slot).wait_send()
            d_copy(1,slot).wait_send()
        for j in range(achunks): att.finish(j)
        lax.fori_loop(0,chunks,lambda j,_: (ffn.finish(j),0)[1],0)
        lax.fori_loop(0,blocks,lambda b,_: (x_copy(b).wait_send(),0)[1],0)
        for c in e_copies: c.wait_send()

def run_backward(hidden,geo,w,q,k,v,p,small,dctx,act,ug,fl,sl,al,ctx,ag):
    count,heads=p.shape[:2]; pages=count//2; cols=q.shape[1]; d=hidden.shape[1]; wide=w.shape[1]
    f=act.shape[2]; rows=fl.shape[0]
    ways=lax.axis_size("dp"); m=ways//2
    chunk=max(BLOCK,16*ways); per=chunk//BLOCK; pr=chunk//ways; pb=BLOCK//pr
    blocks=-(-((f+d)//BLOCK+1)//per)*per
    ablocks=-(-(d//BLOCK)//per)*per
    chunks=blocks//per; achunks=ablocks//per
    page_in=lambda n: pl.BlockSpec((PAGE,n),lambda i:(page_of(i,pages),0))
    page=lambda n: pl.BlockSpec((PAGE,n),lambda i:(i,0))
    whole=lambda s: pl.BlockSpec(s,lambda i:(0,)*len(s),pipeline_mode=pl.Buffered(1))
    anyspec=pl.BlockSpec(memory_space=pl.ANY)
    S=jax.ShapeDtypeStruct; V=pltpu.VMEM; D=pltpu.SemaphoreType.DMA
    half=PAGE//2
    dctx=dctx.reshape(4,pages,half,cols)
    return pl.pallas_call(partial(backward_kernel,pages=pages,m=m,blocks=blocks,per=per),
        out_shape=[S((blocks*pb,pr,d),BF),S((ablocks*pb,pr,wide),BF),S((rows,d),F32)],
        grid=(count,),
        in_specs=[page_in(d),page_in(POS),whole(w.shape),page(cols),page(cols),page(cols),pl.BlockSpec((pl.Squeezed(),heads,PAGE,PAGE),lambda i:(i,0,0,0)),whole(small.shape)]+[anyspec]*8,
        out_specs=[anyspec]*3,
        scratch_shapes=[V(act.shape,BF),V(ug.shape,BF),V(fl.shape,BF),V(sl.shape,BF),V(ctx.shape,BF),
            V((2,2,pb,pr,d),BF),V((blocks,2,pb,pr,d),BF),V((blocks,pb,pr,d),BF),V((blocks,pb,pr,d),BF),V((blocks*pb,pr,d),BF),
            V((chunks,m,pr,d),BF),V((chunks,m-1,pr,d),BF),V((chunks,pr,d),BF),
            V((ablocks*pb,pr,wide),BF),V((achunks,m,pr,wide),BF),V((achunks,m-1,pr,wide),BF),V((achunks,pr,wide),BF),
            V((4,pages,half,cols),BF),V((PAGE,cols),BF),V((d,wide),F32),V((8,wide),F32),V((PAGE,wide),BF),
            V((2,pages,half,d),BF),V((2,pages,half,d),BF),V((2,pages,half,d),BF),V((pages,half,d),BF),V((pages,half,d),F32),
            D((6+pages,)),D((blocks,)),D((blocks,)),D((blocks,)),D((blocks,)),D((9,chunks)),D((9,achunks)),D((4,)),D((3,)),
            D((2,pages)),D((2,pages)),D((pages,)),D((pages,)),D((pages,))],
        compiler_params=pltpu.CompilerParams(vmem_limit_bytes=67043328,collective_id=1,has_side_effects=True),
        name="backward")(hidden,geo,w,q,k,v,p,small,dctx,act,ug,fl,sl,al,ctx,ag)

FREQ=16

def features(box_coords):
    rates = jnp.power(1000.0, -jnp.arange(FREQ, dtype=jnp.float32) / FREQ)
    angles = box_coords.astype(jnp.float32)[:, :, None] * rates[None, None, :]
    angles = jnp.transpose(angles, (1, 0, 2)).reshape(box_coords.shape[1], 4 * FREQ)
    return jnp.concatenate([jnp.cos(angles), jnp.sin(angles)], axis=1)

def body(hidden_in, box_coords, page_lengths, query_weight, query_bias, key_weight, value_weight, value_bias,
         box_weight, box_bias, output_weight, output_bias, first_gain, first_shift, up_weight, up_bias,
         down_weight, down_bias, second_gain, second_shift, output_grad):
    place=lax.axis_index("tensor")
    geo=features(box_coords).astype(BF)
    wide=jnp.concatenate([query_weight,key_weight,value_weight,box_weight],axis=1)
    vec=jnp.stack([output_bias,first_gain,first_shift,down_bias,second_gain,second_shift,output_bias,output_bias])
    q,k,v,p,ctx,*gathered=run_forward(page_lengths,hidden_in,geo,wide,query_bias[None],value_bias[None],box_bias[None],
        output_weight,up_weight,down_weight,up_bias[None])
    ups=gathered.pop()
    rows=output_grad.shape[0]
    ctx=ctx.reshape(ctx.shape[0],rows,ctx.shape[3])
    here=place.reshape(1).astype(jnp.int32)
    layer_out,attn_grad,dctx,act,ug,fl,sl,al,small=run_middle(here,hidden_in,output_grad,ctx,(output_weight,up_weight,down_weight,*gathered),ups,vec,tile=384)
    fin,afin,input_grad=run_backward(hidden_in,geo,wide,q,k,v,p,small,dctx,act,ug,fl,sl,al,ctx,attn_grad)
    d=fin.shape[2]; h=query_weight.shape[1]; o=output_weight.shape[0]; f=up_weight.shape[1]
    fin=fin.reshape(-1,d); afin=afin.reshape(-1,afin.shape[2])[:d]
    down=fin[:f].astype(F32); up=fin[f:f+d].astype(F32); out=fin[f+d:f+d+o].astype(F32)
    tail=fin[f+d+o:f+d+o+8].astype(F32)
    width=d//4
    part=lambda a,b: afin[:,a:b].astype(F32)
    bias=tail[7]
    return (layer_out,input_grad,part(0,h),bias[:h],part(h,2*h),part(2*h,3*h),bias[h:2*h],part(3*h,afin.shape[1]),bias[2*h:],
            out,tail[1,:width],tail[2,:width],tail[3,:width],up,tail[0],down,tail[4,:width],tail[5,:width],tail[6,:width])


def solution(mesh):
    rep=P()
    in_specs=(P("dp",None),P(None,"dp"),P("dp"),P(None,"tensor"),P("tensor"),P(None,"tensor"),P(None,"tensor"),P("tensor"),
        P(None,"tensor"),P("tensor"),P("tensor",None),rep,rep,rep,P(None,"tensor"),P("tensor"),P("tensor",None),rep,rep,rep,P(("dp","tensor"),None))
    out_specs=(P(("dp","tensor"),None),P(("dp","tensor"),None),P(None,"tensor"),P("tensor"),P(None,"tensor"),P(None,"tensor"),P("tensor"),
        P(None,"tensor"),P("tensor"),P("tensor",None),P("tensor"),P("tensor"),P("tensor"),P(None,"tensor"),P("tensor"),P("tensor",None),P("tensor"),P("tensor"),P("tensor"))
    return jax.shard_map(body,mesh=mesh,in_specs=in_specs,out_specs=out_specs,check_vma=False)
```

time: 507 us -> 285 us (0.56)
  waiting for transfers between devices: 259 us -> 0 us
  Pallas kernels: 125 us -> 245 us
  blocking collectives: 23.1 us -> 0 us
  other arithmetic: 35 us -> 16.8 us
  starting transfers between devices: 13.8 us -> 0 us
  between operations: 14.5 us -> 0.79 us
  local copies, waits for them, and re-layouts: 35.2 us -> 22 us
    ppermute x23 -> x0, waiting for transfers between devices: 137 us -> none  [swap(): return lax.ppermute(x, 'tensor', [(i, i ^ by) for i in range(ways)])]
    psum x1 -> x0, waiting for transfers between devices: 122 us -> none  [body(): dw = lax.psum(dw, 'dp').astype(F32)]
    pallas_call x5 -> x2, Pallas kernels: 83.5 us -> 203 us  [the longest x1 150 us: run_backward(): pl.pallas_call(partial(backward_kernel, pages=pages, m=m, blocks=blocks,...]
    psum x1 -> x0, blocking collectives: 23.1 us -> none  [body(): db = lax.psum(db[0], 'dp')]
    ppermute x23 -> x0, starting transfers between devices: 13.7 us -> none  [swap(): return lax.ppermute(x, 'tensor', [(i, i ^ by) for i in range(ways)])]
    slice x11 -> x5, local copies, waits for them, and re-layouts: 13.4 us -> 4.72 us  [the longest x1 1.9 us: body(): down = fin[:f].astype(F32)]
    convert_element_type x4 -> x5, other arithmetic: 14.5 us -> 6.98 us  [the longest x2 2.7 us: body(): part = lambda a, b: afin[:, a:b].astype(F32)]
    squeeze x3 -> x0, local copies, waits for them, and re-layouts: 5.23 us -> none  [the longest x1 3.56 us: body(): grads = add(grads[0], swap(grads[1], 2))]
  transfers between devices with their start and end apart: 24 -> 0, of which waited for: 10 -> 0; matrix products, arithmetic and copies ran while one was open for 7% -> 0% of each run, Pallas kernels for 14% -> 0%
where the time goes in v2:
time: 285 us; the launch traced here: 284 us
  Pallas kernels  245 us (86%)
  local copies, waits for them, and re-layouts  22 us (8%)
  other arithmetic  16.8 us (6%)
    pallas_call x1, Pallas kernels, run_backward(): pl.pallas_call(partial(backward_kernel, pages=pages, m=m, blocks=blocks,...  150 us
    pallas_call x1, Pallas kernels, run_forward(): pl.pallas_call(partial(forward_kernel, pages=pages), out_shape=[S((2 * pa...  53.1 us
    pallas_call x1, Pallas kernels, run_middle(): pl.pallas_call(partial(middle, tile=tile), out_shape=[S((rows, d), BF), S...  41.4 us
    unnamed x15, local copies, waits for them, and re-layouts  9.32 us
    another operation x1, other arithmetic  5.74 us

profile of v2, /device:TPU:0, one launch (start us, length us, event | category | flops | bytes accessed | tf_op | source)
XLA Modules:
  0.0 284.2 jit_solution(5200912967227523807)
XLA Ops:
  0.7 0.0 copy-start.2
  0.7 0.0 copy-start.3
  0.7 0.1 mul.27
  0.8 1.3 broadcast_in_dim.16.bb_ref
  2.1 0.7 stack.23
  2.8 0.7 stack.24
  3.5 0.7 stack.25
  4.2 1.3 broadcast_in_dim.17.ub_any
  5.4 0.7 stack.26
  6.1 0.7 stack.27
  6.8 0.7 stack.28
  7.5 0.6 stack.29.vec_ref
  8.1 0.8 convert_bitcast_fusion
  9.0 1.1 copy.56
  10.1 1.1 copy.57
  11.2 0.0 copy-done.3
  11.2 0.2 copy.58
  11.4 0.0 copy-done.2
  11.4 1.9 pad_maximum_fusion.w_ref
  13.3 0.1 mul.24
  13.4 0.5 copy.54
  13.8 5.7 %cosine_convert_fusion = (bf16[3072,64]{1,0:T(8,128)(2,1)S(1)}, bf16[3072,64]{1,0:T(8,128)(2,1)S(1)}) fusion(f32[3072,64]{1,0:T(8,128)S(1)} %copy.54, f32[64]{0:T(128)S(1)} %mul.27), kind=kLoop, calls=%fused_computation.2 | loop fusion | flops 589824 | bytes 1573120 | tf_op jit(solution)/shard_map/convert.3
  19.6 1.3 pad_maximum_fusion.1.geo_ref
  20.9 53.1 %forward.1 = (bf16[3072,192]{1,0:T(8,128)(2,1)}, bf16[3072,192]{1,0:T(8,128)(2,1)}, bf16[3072,192]{1,0:T(8,128)(2,1)}, bf16[6,3,512,512]{3,2,1,0:T(8,128)(2,1)},...) custom-call(s32[6]{0:T(128)} %len_ref.1, ...), custom_call_target="tpu_custom_call" | custom-call | tf_op jit(solution)/shard_map/forward/pallas_call | solution.py:293
  74.0 41.4 %middle.1 = (bf16[768,768]{1,0:T(8,128)(2,1)}, f32[768,768]{1,0:T(8,128)}, bf16[4,768,192]{2,1,0:T(8,128)(2,1)}, bf16[4,768,768]{2,1,0:T(8,128)(2,1)}, bf16[4,76...) custom-call(s32[1]{0:T(128)} %bitcast.t_ref, ...), custom_call_target="tpu_custom_call" | custom-call | tf_op jit(solution)/shard_map/middle/pallas_call | solution.py:117
  115.4 150.2 %backward.1 = (bf16[56,32,768]{2,1,0:T(8,128)(2,1)}, bf16[24,32,960]{2,1,0:T(8,128)(2,1)}, f32[768,768]{1,0:T(8,128)}) custom-call(bf16[3072,768]{1,0:T(8,128)(2,1)} %h_ref.3, bf16[3072,128]{1,0:T(8,128)(2,1)} %pad_maximum_fusion.1.geo_ref, bf16[768,960]{1,0:T(8,128)(2,1)} %pad_maximum_fusion.w_ref, bf16[3072,192]{1,0:T(8,128)(2,1)} %get-tuple-element.58.q_ref, ...), custom_call_target="tpu_custom_call" | custom-call | tf_op jit(solution)/shard_map/backward/pallas_call | solution.py:562
  265.6 0.7 slice_convert_fusion.4
  266.3 0.6 slice_reduce_fusion.1
  266.9 0.6 slice_reduce_fusion
  267.5 0.6 fusion.1
  268.2 1.0 slice.81
  269.1 0.0 copy-start.1
  269.1 1.9 fusion
  271.0 0.9 bitcast_convert_fusion.2
  271.9 0.0 copy-done.1
  271.9 1.3 slice_convert_fusion
  273.2 1.4 slice_convert_fusion.1
  274.6 2.2 copy.61
  276.8 2.2 copy.60
  279.0 1.1 copy.59
  280.1 0.0 copy-start
  280.1 2.7 bitcast_convert_fusion
  282.8 0.0 copy-done
  282.8 1.4 copy.63
  (2 shorter events, 0.0 us)
Async XLA Ops:
  0.7 10.8 %copy-start.2 = (bf16[768,384]{1,0:T(8,128)(2,1)S(1)}, bf16[768,384]{1,0:T(8,128)(2,1)}, u32[]{:S(2)}) copy-start(bf16[768,384]{1,0:T(8,128)(2,1)} %param.29) | copy-start | bytes 1769476
  0.7 10.6 %copy-start.3 = (bf16[768,192]{0,1:T(8,128)(2,1)S(1)}, bf16[768,192]{0,1:T(8,128)(2,1)}, u32[]{:S(2)}) copy-start(bf16[768,192]{0,1:T(8,128)(2,1)} %param.27) | copy-start | bytes 884740
  269.1 2.8 copy-start.1
  280.1 2.7 copy-start

commit v3 on v1

v3 whole, which is shorter than its diff:
```python
from functools import partial
import math
import jax
import jax.numpy as jnp
from jax import lax
from jax.experimental import pallas as pl
from jax.experimental.pallas import tpu as pltpu
from jax.sharding import PartitionSpec as P

HEAD = 64
POS = 128
FREQ = 16
PAGE = 512
HALF = PAGE // 2
BLOCK = 256
PART = 192
EPS = 1e-05
LOG2E = 1.4426950408889634
F32 = jnp.float32
BF = jnp.bfloat16
MESH = pl.DeviceIdType.MESH
V = pltpu.VMEM
D = pltpu.SemaphoreType.DMA
S = jax.ShapeDtypeStruct
ANY = pl.BlockSpec(memory_space=pl.ANY)
WHOLE = pl.BlockSpec(memory_space=pltpu.VMEM)


def mm(a, b):
    return jnp.dot(a, b, preferred_element_type=F32)


def mm_nt(a, b):
    return lax.dot_general(a, b, (((1,), (1,)), ((), ())), preferred_element_type=F32)


def mm_tn(a, b):
    return lax.dot_general(a, b, (((0,), (0,)), ((), ())), preferred_element_type=F32)


def columns(x):
    return jnp.sum(x, axis=0, keepdims=True)


def row(ref):
    return ref[...].reshape(1, ref.shape[0])


def normal(z):
    mean = jnp.mean(z, axis=1, keepdims=True)
    centred = z - mean
    inverse = lax.rsqrt(jnp.mean(centred * centred, axis=1, keepdims=True) + EPS)
    return centred * inverse, inverse


def normal_back(inner, scaled, inverse):
    return inverse * (
        inner
        - jnp.mean(inner, axis=1, keepdims=True)
        - scaled * jnp.mean(inner * scaled, axis=1, keepdims=True)
    )


def geometry_of(coords, rates):
    n = coords.shape[1]
    split = jnp.concatenate([coords // 256, coords % 256], axis=0).astype(F32)
    split = jnp.concatenate([split, jnp.zeros_like(split)], axis=0).astype(BF)
    lane = lax.broadcasted_iota(jnp.int32, (16, POS), 1)
    which = lax.broadcasted_iota(jnp.int32, (16, POS), 0)
    spread = jnp.where((lane % (POS // 2)) // FREQ == which % 4, 1.0, 0.0)
    spread = jnp.where(which < 4, 256.0 * spread, spread).astype(BF)
    angle = mm_tn(split, spread) * rates
    turns = jnp.round(angle * 0.6366197723675814)
    r = ((angle - turns * 1.5703125) - turns * 4.837512969970703125e-4) - turns * 7.54978995489188216e-8
    z = r * r
    sine = r + r * z * (-1.6666654611e-1 + z * (8.3321608736e-3 - z * 1.9515295891e-4))
    cosine = 1.0 - 0.5 * z + z * z * (4.166664568298827e-2 + z * (-1.388731625493765e-3 + z * 2.443315711809948e-5))
    quarter = turns.astype(jnp.int32) + jnp.where(lax.broadcasted_iota(jnp.int32, (n, POS), 1) < POS // 2, 1, 0)
    value = jnp.where((quarter & 1) == 1, cosine, sine)
    return jnp.where((quarter & 2) == 2, -value, value).astype(BF)


def mixing(geo):
    half = POS // 2
    c = geo[:, :half]
    s = geo[:, half:]
    return jnp.concatenate([c, -c], axis=1), jnp.concatenate([s, s], axis=1)


def mix(coeff, cos_sign, sin_twice):
    return coeff * cos_sign + pltpu.roll(coeff, POS // 2, 1) * sin_twice


def remote(src, dst, sent, got, device):
    return pltpu.make_async_remote_copy(
        src_ref=src, dst_ref=dst, send_sem=sent, recv_sem=got, device_id=device, device_id_type=MESH
    )


def arrived(ref, sem):
    pltpu.make_async_copy(ref, ref, sem).wait()


def seats():
    group = lax.axis_index("dp")
    place = lax.axis_index("tensor")
    core = lax.rem(place, 2)
    chip = place // 2
    near = place + 1 - 2 * core
    far = place + 2 - 4 * chip
    cross = far + 1 - 2 * core
    return group, place, core, chip, near, far, cross


def page_of(i, pages):
    chip = lax.axis_index("tensor") // 2
    return jnp.where(i < pages, (1 - chip) * pages + i, chip * pages + i - pages)


def forward_kernel(len_ref, rates_ref, h_ref, coords_ref, wb_ref, qb_ref, vb_ref, bb_ref, ub_ref, wq_any, wk_any, wv_any, wo_any, wu_any, wd_any,
                   q_ref, k_ref, v_ref, geo_ref, p_ref, ctx_any, wt_any, ua_any, no_any, nu_any, nd_any, fo_any, fu_any, fd_any, co_any, cu_any, cd_any,
                   wt, cat_q, cat_k, cpage, ubs, l_s, x_s, x_r, y_s, y_r, n_s, n_r, c_s, c_r, u_s, u_r, t_s, t_r, *, pages):
    i = pl.program_id(0)
    cols = q_ref.shape[1]
    heads = cols // HEAD
    box = heads * POS
    group, place, core, chip, near, far, cross = seats()
    side = lax.rem(group, 2)
    beside = group + 1 - 2 * side
    own = (wo_any, wu_any, wd_any)
    nears = (no_any, nu_any, nd_any)
    fars = (fo_any, fu_any, fd_any)
    crosses = (co_any, cu_any, cd_any)
    chunks = []
    for a, w in enumerate(own):
        half = w.shape[0] // 2
        step = min(PART, half)
        chunks += [(a, s, step) for s in range(0, half, step)]

    def rows(c, other):
        a, s, n = chunks[c]
        half = own[a].shape[0] // 2
        return a, pl.ds(pl.multiple_of(half * (1 - side if other else side) + s, 16), n)

    def x_copy(c):
        a, r = rows(c, False)
        return remote(own[a].at[r], fars[a].at[r], x_s.at[c], x_r.at[c], (group, far))

    def y_copy(c, other=False):
        a, r = rows(c, other)
        return remote(fars[a].at[r], fars[a].at[r], y_s.at[c], y_r.at[c], (beside, place))

    def c_copy(c, other):
        a, r = rows(c, other)
        k = 1 if other else 0
        return remote(fars[a].at[r], crosses[a].at[r], c_s.at[k, c], c_r.at[k, c], (group, near))

    n_copies = [remote(own[a], nears[a], n_s.at[a], n_r.at[a], (group, near)) for a in range(3)]
    u_copies = [remote(ubs.at[0], ubs.at[g], u_s.at[g - 1], u_r.at[g - 1], (group, d)) for g, d in ((1, near), (2, far), (3, cross))]
    loads = [pltpu.make_async_copy(w, wt.at[pl.ds(box + n * cols, cols)], l_s.at[n]) for n, w in enumerate((wq_any, wk_any, wv_any))]
    keep_wt = pltpu.make_async_copy(wt, wt_any, l_s.at[3])

    @pl.when(i == 0)
    def _():
        for c in loads:
            c.start()
        ubs[0] = row(ub_ref)
        barrier = pltpu.get_barrier_semaphore()
        peers = [(group, near), (group, far), (group, cross), (beside, place)]
        for device in peers:
            pl.semaphore_signal(barrier, inc=1, device_id=device, device_id_type=MESH)
        pl.semaphore_wait(barrier, len(peers))
        for c in range(len(chunks)):
            x_copy(c).start()
        for n in n_copies:
            n.start()
        for u in u_copies:
            u.start()
        wt[:box, :] = wb_ref[...].T
        for c in loads:
            c.wait()
        keep_wt.start()

    length = len_ref[page_of(i, pages)]
    geo = geometry_of(coords_ref[...], rates_ref[...])
    geo_ref[...] = geo
    proj = mm_nt(h_ref[...], wt[...])
    q_ref[...] = (proj[:, box : box + cols] + row(qb_ref)).astype(BF)
    k_ref[...] = proj[:, box + cols : box + 2 * cols].astype(BF)
    v_ref[...] = (proj[:, box + 2 * cols :] + row(vb_ref)).astype(BF)
    co, si = mixing(geo.astype(F32))
    bias = row(bb_ref)
    for head in range(heads):
        wide = slice(head * POS, (head + 1) * POS)
        lanes = slice(head * HEAD, (head + 1) * HEAD)
        cat_q[head, :, :POS] = mix(proj[:, wide] + bias[:, wide], co, si).astype(BF)
        cat_q[head, :, POS:] = q_ref[:, lanes]
        cat_k[head, :, :POS] = geo
        cat_k[head, :, POS:] = k_ref[:, lanes]
    valid = lax.broadcasted_iota(jnp.int32, (1, PAGE), 1) < length
    scale = LOG2E / math.sqrt(HEAD)
    for head in range(heads):
        lanes = slice(head * HEAD, (head + 1) * HEAD)
        s = mm_nt(cat_q[head], cat_k[head])
        s = jnp.where(valid, s, -1e30)
        top = jnp.max(s, axis=1, keepdims=True)
        e = jnp.exp2((s - top) * scale)
        total = jnp.sum(e, axis=1, keepdims=True)
        p = (e * (1.0 / total)).astype(BF)
        p_ref[head] = p
        c = mm(p, v_ref[:, lanes]).astype(BF)
        for k in range(2):
            cpage[2 * i + k, :, lanes] = c[k * HALF : (k + 1) * HALF]
    for k in range(2):
        piece = 2 * lax.rem(i, pages) + k
        oc = piece // pages
        slot = lax.rem(piece, pages)
        mine = oc == core

        @pl.when(i < pages)
        def _():
            g = jnp.where(mine, 2, 3)
            remote(cpage.at[2 * i + k], ctx_any.at[g, slot], t_s.at[2 * i + k], t_r.at[g, slot], (group, 2 * (1 - chip) + oc)).start()

        @pl.when((i >= pages) & jnp.logical_not(mine))
        def _():
            remote(cpage.at[2 * i + k], ctx_any.at[1, slot], t_s.at[2 * i + k], t_r.at[1, slot], (group, near)).start()

        @pl.when((i >= pages) & mine)
        def _():
            pltpu.make_async_copy(cpage.at[2 * i + k], ctx_any.at[0, slot], t_r.at[0, slot]).start()

    count = 2 * pages

    def forward_on(c):
        x_copy(c).wait_recv()
        y_copy(c).start()
        c_copy(c, False).start()

    plan = {0: [0], 1: [1], 3: [2], 4: [3], 5: [4]}
    for at, todo in plan.items():

        @pl.when(i == at)
        def _():
            for c in todo:
                forward_on(c)

    @pl.when(i == count - 1)
    def _():
        keep_wt.wait()
        for u in u_copies:
            u.wait()
        keep_ub = pltpu.make_async_copy(ubs, ua_any, u_s.at[3])
        keep_ub.start()
        for c in range(len(chunks)):
            y_copy(c, True).wait_recv()
            c_copy(c, True).start()
        for n in n_copies:
            n.wait()
        keep_ub.wait()
        for slot in range(pages):
            for g in range(4):
                arrived(ctx_any.at[g, slot], t_r.at[g, slot])
        for j in range(2 * count):
            if j < count:
                arrived(cpage.at[j], t_s.at[j])
            else:

                @pl.when((j - count) // pages != core)
                def _():
                    arrived(cpage.at[j], t_s.at[j])

        for c in range(len(chunks)):
            x_copy(c).wait_send()
            y_copy(c).wait_send()
            c_copy(c, False).wait()
            c_copy(c, True).wait()


def run_forward(lengths, rates, hidden, coords, wb, qb, vb, bb, ub, wq, wk, wv, wo, wu, wd):
    cols, d = wq.shape
    heads = cols // HEAD
    pages = lengths.shape[0] // 2
    wide = wb.shape[1] + 3 * cols
    own = (wo, wu, wd)
    n = sum((x.shape[0] // 2) // min(PART, x.shape[0] // 2) for x in own)
    page_out = lambda w: pl.BlockSpec((PAGE, w), lambda i: (i, 0))
    rows = 2 * pages * PAGE
    return pl.pallas_call(
        partial(forward_kernel, pages=pages),
        out_shape=[S((rows, cols), BF)] * 3
        + [S((rows, POS), BF), S((2 * pages, heads, PAGE, PAGE), BF), S((4, pages, HALF, cols), BF), S((wide, d), BF), S((4, 1, ub.shape[0]), F32)]
        + [S(x.shape, BF) for x in own] * 3,
        grid=(2 * pages,),
        in_specs=[
            pl.BlockSpec(memory_space=pltpu.SMEM),
            WHOLE,
            pl.BlockSpec((PAGE, d), lambda i: (page_of(i, pages), 0)),
            pl.BlockSpec((4, PAGE), lambda i: (0, page_of(i, pages))),
        ]
        + [WHOLE] * 5
        + [ANY] * 6,
        out_specs=[page_out(cols)] * 3
        + [page_out(POS), pl.BlockSpec((pl.Squeezed(), heads, PAGE, PAGE), lambda i: (i, 0, 0, 0))]
        + [ANY] * 12,
        scratch_shapes=[V((wide, d), BF), V((heads, PAGE, POS + HEAD), BF), V((heads, PAGE, POS + HEAD), BF), V((4 * pages, HALF, cols), BF), V((4, 1, ub.shape[0]), F32)]
        + [D((4,)), D((n,)), D((n,)), D((n,)), D((n,)), D((3,)), D((3,)), D((2, n)), D((2, n)), D((4,)), D((3,)), D((4 * pages,)), D((4, pages))],
        compiler_params=pltpu.CompilerParams(vmem_limit_bytes=56 << 20, collective_id=0, has_side_effects=True),
        name="forward",
    )(lengths, rates, hidden, coords, wb, qb, vb, bb, ub, wq, wk, wv, wo, wu, wd)


def middle_kernel(hid_any, og_any, ctx_any, w0, w1, w2, w3, w4, w5, w6, w7, w8, w9, w10, w11, ub_ref, ob_ref, g1_ref, s1_ref, db_ref, g2_ref, s2_ref,
                  out_any, act_any, ug_any, fl_any, sl_any, scaled_any, second_any, inv_ref, vg_ref,
                  hid, og, ctx, wo, wu, wd, act, ug, fl, sl, lo, first, scaled1, second2, ffn, sem_in, sem_w, sem_out, *, tile):
    rows, d = og.shape
    groups = wu.shape[0]
    weights = (w0, w1, w2, w3, w4, w5, w6, w7, w8, w9, w10, w11)
    place = lax.axis_index("tensor")
    head_loads = [
        pltpu.make_async_copy(ctx_any, ctx, sem_in.at[0]),
        pltpu.make_async_copy(hid_any.at[pl.ds(place * rows, rows)], hid, sem_in.at[1]),
        pltpu.make_async_copy(og_any, og, sem_in.at[2]),
    ]
    loads = [[pltpu.make_async_copy(weights[3 * g + k], (wo, wu, wd)[k].at[g], sem_w.at[k, g]) for g in range(groups)] for k in range(3)]
    head_loads[0].start()
    for c in loads[0]:
        c.start()
    head_loads[1].start()
    for g in range(groups):
        loads[1][g].start()
        loads[2][g].start()
    head_loads[2].start()
    head_loads[0].wait()
    for c in loads[0]:
        c.wait()
    head_loads[1].wait()
    vg_ref[...] = jnp.zeros_like(vg_ref)
    steps = rows // tile

    def stores(i):
        r = pl.ds(pl.multiple_of(i * tile, tile), tile)
        pairs = ((act.at[:, r], act_any.at[:, r]), (ug.at[:, r], ug_any.at[:, r]), (fl.at[r], fl_any.at[r]), (sl.at[r], sl_any.at[r]),
                 (lo.at[r], out_any.at[r]), (scaled1.at[r], scaled_any.at[r]), (second2.at[r], second_any.at[r]))
        return [pltpu.make_async_copy(a, b, sem_out.at[n, i]) for n, (a, b) in enumerate(pairs)]

    def step(i, _):
        r = pl.ds(pl.multiple_of(i * tile, tile), tile)
        attn = mm(ctx[0, r], wo[0])
        for g in range(1, groups):
            attn = attn + mm(ctx[g, r], wo[g])
        scaled, inverse = normal(attn + row(ob_ref) + hid[r].astype(F32))
        f = scaled * row(g1_ref) + row(s1_ref)
        first[...] = f
        scaled1[r] = scaled
        inv_ref[r] = inverse
        fl[r] = f.astype(BF)
        for g in range(groups):

            @pl.when(i == 0)
            def _():
                loads[1][g].wait()

            x = mm(fl[r], wu[g]) + ub_ref[g]
            half = 0.5 + 0.5 * lax.erf(x * 0.7071067811865476)
            a = (x * half).astype(BF)
            act[g, r] = a
            ug[g, r] = (half + x * jnp.exp(-0.5 * x * x) * 0.3989422804014327).astype(BF)

            @pl.when(i == 0)
            def _():
                loads[2][g].wait()

            part = mm(a, wd[g])
            if g == 0:
                ffn[...] = part
            else:
                ffn[...] += part

        scaled, inverse = normal(ffn[...] + row(db_ref) + first[...])
        lo[r] = (scaled * row(g2_ref) + row(s2_ref)).astype(BF)

        @pl.when(i == 0)
        def _():
            head_loads[2].wait()

        o = og[r].astype(F32)
        second = normal_back(o * row(g2_ref), scaled, inverse)
        vg_ref[3:4, :] += columns(second)
        vg_ref[4:5, :] += columns(o * scaled)
        vg_ref[5:6, :] += columns(o)
        sl[r] = second.astype(BF)
        second2[r] = second
        for c in stores(i):
            c.start()
        return 0

    lax.fori_loop(0, steps, step, 0)
    for i in range(steps):
        for c in stores(i):
            c.wait()


def run_middle(hidden, og, ctx, weights, ub, vectors, tile):
    rows, d = og.shape
    groups = 4
    q = weights[0].shape[0]
    f = weights[1].shape[1]
    return pl.pallas_call(
        partial(middle_kernel, tile=tile),
        out_shape=[S((rows, d), BF), S((groups, rows, f), BF), S((groups, rows, f), BF), S((rows, d), BF), S((rows, d), BF), S((rows, d), F32), S((rows, d), F32), S((rows, 1), F32), S((8, d), F32)],
        in_specs=[ANY] * 15 + [WHOLE] * 7,
        out_specs=[ANY] * 7 + [WHOLE] * 2,
        scratch_shapes=[
            V((rows, d), BF), V((rows, d), BF), V((groups, rows, q), BF), V((groups, q, d), BF), V((groups, d, f), BF), V((groups, f, d), BF),
            V((groups, rows, f), BF), V((groups, rows, f), BF), V((rows, d), BF), V((rows, d), BF), V((rows, d), BF),
            V((tile, d), F32), V((rows, d), F32), V((rows, d), F32), V((tile, d), F32),
            D((3,)), D((3, groups)), D((7, rows // tile)),
        ],
        compiler_params=pltpu.CompilerParams(vmem_limit_bytes=62 << 20),
        name="middle",
    )(hidden, og, ctx, *weights, ub, *vectors)


class Cube:
    def __init__(self, main, recv, out, sems, group, place, rows, levels):
        self.main, self.recv, self.out, self.sems = main, recv, out, sems
        self.group, self.place, self.rows, self.levels = group, place, rows, levels
        self.steps = 2 * levels - 1

    def bit(self, j, s):
        if s > 1:
            return 2**s
        return jnp.where(lax.rem(j, 4) == 3, 2 - s, 1 + s)

    def side(self, j, s):
        return lax.rem(self.group // self.bit(j, s), 2)

    def partner(self, j, s):
        return (self.group + self.bit(j, s) * (1 - 2 * self.side(j, s)), self.place)

    def low(self, j, s):
        at = j * self.rows
        for t in range(s):
            at = at + self.side(j, t) * (self.rows >> (t + 1))
        return at

    def span(self, start, n):
        return pl.ds(pl.multiple_of(start, 16), n)

    def r_copy(self, j, s):
        n = self.rows >> (s + 1)
        src = self.main.at[self.span(self.low(j, s) + (1 - self.side(j, s)) * n, n)]
        dst = self.recv.at[self.span(j * self.rows + self.rows - (self.rows >> s), n)]
        return remote(src, dst, self.sems.at[0, j, s], self.sems.at[1, j, s], self.partner(j, s))

    def g_copy(self, j, s):
        here = self.span(self.low(j, s + 1), self.rows >> (s + 1))
        src = self.main if s == self.levels - 1 else self.out
        return remote(src.at[here], self.out.at[here], self.sems.at[2, j, s], self.sems.at[3, j, s], self.partner(j, s))

    def keep(self, j):
        here = self.span(self.low(j, self.levels), self.rows >> self.levels)
        return pltpu.make_async_copy(self.main.at[here], self.out.at[here], self.sems.at[0, j, self.levels])

    def start(self, j):
        self.r_copy(j, 0).start()

    def step(self, k, j):
        last = self.levels - 1
        if k <= last:
            self.r_copy(j, k).wait_recv()
            n = self.rows >> (k + 1)
            mine = self.span(self.low(j, k + 1), n)
            got = self.span(j * self.rows + self.rows - (self.rows >> k), n)
            self.main[mine] = self.main[mine] + self.recv[got]
            if k < last:
                self.r_copy(j, k + 1).start()
            else:
                self.keep(j).start()
                self.g_copy(j, last).start()
        else:
            s = 2 * self.levels - 2 - k
            self.g_copy(j, s + 1).wait_recv()
            if s + 1 == last:
                self.keep(j).wait()
            self.g_copy(j, s).start()

    def finish(self, j):
        self.g_copy(j, 0).wait_recv()
        for s in range(self.levels):
            self.r_copy(j, s).wait_send()
            self.g_copy(j, s).wait_send()


SLOTS = 3


def backward_kernel(h_ref, wt_ref, q_ref, k_ref, v_ref, geo_ref, p_ref, inv_ref, vgin_ref, g1_ref,
                    act_any, ug_any, fl_any, sl_any, scaled_any, second_any, ctx_any,
                    o0, u0, n0, o1, u1, n1, o2, u2, n2, o3, u3, n3,
                    fin_any, afin_any, ig_any,
                    act, ug, wd, wo, fl, sl, al, ctx, cs, crecv, gx, xrecv, main, mrecv, amain, arecv, dsrc, dc, dcp, total, btotal, mixed, drecv, dxrecv, ag, acc, vg, ubg,
                    l_sem, w_sem, c_s, c_r, free, x_s, x_r, r_sem, a_sem, e_s, e_r, d_s, d_r, f_s, f_r, o_sem, *, pages, ways, blocks, per, arows):
    i = pl.program_id(0)
    count = 2 * pages
    group, place, core, chip, near, far, cross = seats()
    cols = q_ref.shape[1]
    heads = cols // HEAD
    box = heads * POS
    d = h_ref.shape[1]
    levels = ways.bit_length() - 1
    f = act.shape[2]
    qc = ctx.shape[2]
    downs = f // BLOCK
    ups = downs + d // BLOCK
    chunks = blocks // per
    achunks = amain.shape[0] // arows
    ffn = Cube(main, mrecv, fin_any, r_sem, group, place, per * BLOCK, levels)
    att = Cube(amain, arecv, afin_any, a_sem, group, place, arows, levels)
    second = total.at[pl.ds(0, pages * BLOCK), :]
    loads = [pltpu.make_async_copy(a, b, l_sem.at[n]) for n, (a, b) in enumerate(((sl_any, sl), (fl_any, fl), (ug_any, ug), (scaled_any, ag), (second_any, second), (ctx_any, ctx)))]
    act_loads = [pltpu.make_async_copy(act_any.at[g], act.at[g], w_sem.at[3, g]) for g in range(4)]
    wo_loads = [pltpu.make_async_copy(a, wo.at[g], w_sem.at[0, g]) for g, a in enumerate((o0, o1, o2, o3))]
    wu_loads = [pltpu.make_async_copy(a, act.at[g], w_sem.at[1, g]) for g, a in enumerate((u0, u1, u2, u3))]
    wd_loads = [pltpu.make_async_copy(a, wd.at[g], w_sem.at[2, g]) for g, a in enumerate((n0, n1, n2, n3))]
    spare = lambda which, slot: wd.at[which, pl.ds(slot * HALF, HALF)]

    def e_copy(g, slot):
        return remote(dsrc.at[g - 1, slot], dc.at[g, slot], e_s.at[g - 1, slot], e_r.at[g - 1, slot], (group, (near, far, cross)[g - 1]))

    def c_copy(b):
        return remote(cs.at[lax.rem(b, 2)], crecv.at[lax.rem(b, SLOTS)], c_s.at[b], c_r.at[b], (group, near))

    def x_copy(b):
        return remote(gx.at[b], xrecv.at[b], x_s.at[b], x_r.at[b], (group, far))

    def span(b):
        return pl.ds(pl.multiple_of(b * BLOCK, BLOCK), BLOCK)

    def plus(a, b):
        return a + b

    def put(b, g, value):
        value = value.astype(BF)
        if g == 0:
            main[span(b)] = value
        elif g == 2:
            gx[b] = value
        else:
            cs[lax.rem(b, 2), g // 2] = value

    def c_add(b):
        c_copy(b).wait_recv()
        slot = lax.rem(b, SLOTS)

        main[span(b)] = plus(main[span(b)], crecv[slot, 0])
        gx[b] = plus(gx[b], crecv[slot, 1])
        x_copy(b).start()

        @pl.when(b + SLOTS < blocks)
        def _():
            pl.semaphore_signal(free, inc=1, device_id=(group, near), device_id_type=MESH)

    def block(b, kind):
        @pl.when(b >= 2)
        def _():
            c_copy(b - 2).wait_send()

        if kind == "down":
            r = pl.ds(pl.multiple_of(b * BLOCK, BLOCK), BLOCK)
            for g in range(4):

                @pl.when(b == 0)
                def _():
                    act_loads[g].wait()

                put(b, g, mm_tn(act[g, :, r], sl[...]))
        elif kind == "up":
            r = pl.ds(pl.multiple_of((b - downs) * BLOCK, BLOCK), BLOCK)
            for g in range(4):
                put(b, g, mm_tn(fl[:, r], ug[g]))
        elif kind == "out":
            width = d // 4
            for g, place_g in enumerate((place, near, far, cross)):
                norms = vg[0:6, :width]
                for a in range(1, 4):
                    norms = jnp.where(place_g == a, vg[0:6, a * width : (a + 1) * width], norms)
                norms = jnp.concatenate([norms, jnp.zeros((6, d - width), F32)], axis=1)
                extra = jnp.concatenate([ubg[g, 0:1, :], norms, jnp.zeros((BLOCK - qc - 7, d), F32)], axis=0)
                put(b, g, jnp.concatenate([mm_tn(ctx[g], al[...]), extra], axis=0))
        else:
            for g in range(4):
                put(b, g, jnp.zeros((BLOCK, d), F32))

        @pl.when(b >= SLOTS)
        def _():
            pl.semaphore_wait(free, 1)

        c_copy(b).start()

    def x_add(b):
        x_copy(b).wait_recv()

        main[span(b)] = plus(main[span(b)], xrecv[b])

        @pl.when(lax.rem(b + 1, per) == 0)
        def _():
            ffn.start(b // per)

    def tick(u, low, high=blocks):
        half = u // 2
        odd = lax.rem(u, 2)
        if high == blocks:

            @pl.when((odd == 0) & (half >= low) & (half < high))
            def _():
                x_add(half)

        for k in range(ffn.steps):
            b = (u - k - 1) // 2

            @pl.when((lax.rem(u + k, 2) == 1) & (u > k) & (b >= low) & (b < high) & (lax.rem(b + 1, per) == 0))
            def _():
                ffn.step(k, b // per)

    @pl.when(i == 0)
    def _():
        loads[0].start()
        for c in act_loads:
            c.start()
        peers = [(group, near), (group, far), (group, cross)]
        peers += [(group + 2**n * (1 - 2 * lax.rem(group // 2**n, 2)), place) for n in range(levels)]
        barrier = pltpu.get_barrier_semaphore()
        for device in peers:
            pl.semaphore_signal(barrier, inc=1, device_id=device, device_id_type=MESH)

        for c in wd_loads:
            c.start()
        loads[2].start()
        loads[4].start()
        loads[3].start()
        for c in wo_loads:
            c.start()
        loads[1].start()
        loads[5].start()
        pl.semaphore_wait(barrier, len(peers))
        loads[0].wait()

        def down_block(b, _):
            block(b, "down")

            @pl.when(b >= 1)
            def _():
                c_add(b - 1)

            return 0

        lax.fori_loop(0, downs, down_block, 0)
        for c in wu_loads:
            c.start()
        for c in wd_loads:
            c.wait()
        for n in (2, 3, 4):
            loads[n].wait()
        c_add(downs - 1)
        for c in wo_loads:
            c.wait()
        for n in (1, 5):
            loads[n].wait()
        vg[...] = vgin_ref[...]
        ubg[...] = jnp.zeros_like(ubg)

        def tile(t, _):
            r = pl.ds(pl.multiple_of(t * BLOCK, BLOCK), BLOCK)
            acc[...] = total[r, :]
            for g in range(4):
                u = (mm_nt(sl[r], wd[g]) * ug[g, r].astype(F32)).astype(BF)
                ug[g, r] = u
                ubg[g, 0:1, :] += columns(u.astype(F32))

                @pl.when(t == 0)
                def _():
                    wu_loads[g].wait()

                acc[...] += mm_nt(u, act[g])

            @pl.when(t == 1)
            def _():
                tick(0, 0)

            fg = acc[...]
            scaled = ag[r]
            a = normal_back(fg * row(g1_ref), scaled, inv_ref[r])
            vg[0:1, :] += columns(a)
            vg[1:2, :] += columns(fg * scaled)
            vg[2:3, :] += columns(fg)
            ag[r] = a
            low = a.astype(BF)
            al[r] = low
            for g in (2, 3, 1, 0):
                value = mm_nt(low, wo[g]).astype(BF)
                if g == 0:
                    dc[0, t] = value
                else:
                    dsrc[g - 1, t] = value
                    e_copy(g, t).start()

            @pl.when(t == 2)
            def _():
                tick(1, 0)

            return 0

        lax.fori_loop(0, pages, tile, 0)

        def up_block(b, _):
            block(b, "up")

            @pl.when(b > downs)
            def _():
                c_add(b - 1)

            @pl.when(b == downs + 1)
            def _():
                tick(2, 0)

            return 0

        lax.fori_loop(downs, ups, up_block, 0)
        block(ups, "out")
        c_add(ups - 1)
        for b in range(ups + 1, blocks):
            block(b, "zero")
            c_add(b - 1)
        c_add(blocks - 1)
        for b in (blocks - 2, blocks - 1):
            c_copy(b).wait_send()
        total[...] = jnp.zeros_like(total)
        btotal[...] = jnp.zeros_like(btotal)
        tick(3, 0)
        for slot in range(pages):
            e_copy(1, slot).wait_recv()

    @pl.when(i == pages)
    def _():
        for g in (2, 3):
            for slot in range(pages):
                e_copy(g, slot).wait_recv()

    for k in range(2):
        piece = 2 * lax.rem(i, pages) + k
        g = jnp.where(piece // pages == core, 0, 1) + jnp.where(i < pages, 0, 2)
        dcp[k * HALF : (k + 1) * HALF, :] = dc[g, lax.rem(piece, pages)]
    geo = geo_ref[...]
    co, si = mixing(geo.astype(F32))
    factor = 1.0 / math.sqrt(HEAD)
    for head in range(heads):
        lanes = slice(head * HEAD, (head + 1) * HEAD)
        p = p_ref[head]
        dcl = dcp[:, lanes]
        mixed[:, box + 2 * cols + head * HEAD : box + 2 * cols + (head + 1) * HEAD] = mm_tn(p, dcl).astype(BF)
        dp = mm_nt(dcl, v_ref[:, lanes])
        pf = p.astype(F32)
        delta = jnp.sum(pf * dp, axis=1, keepdims=True)
        ds = (pf * (dp - delta)).astype(BF)
        both = mm(ds, jnp.concatenate([geo, k_ref[:, lanes]], axis=1)) * factor
        mixed[:, box + head * HEAD : box + (head + 1) * HEAD] = both[:, POS:].astype(BF)
        mixed[:, head * POS : (head + 1) * POS] = mix(both[:, :POS], co, si).astype(BF)
        mixed[:, box + cols + head * HEAD : box + cols + (head + 1) * HEAD] = (mm_tn(ds, q_ref[:, lanes]) * factor).astype(BF)
        if head == heads // 2:

            @pl.when(i < 2)
            def _():
                tick(4 + i, 0)

    total[...] += mm_tn(mixed[...], h_ref[...])
    btotal[0:1, :] += columns(mixed[...].astype(F32))

    def d_copy(kind, slot):
        return remote(spare(2 + kind, slot), drecv.at[kind, slot], d_s.at[kind, slot], d_r.at[kind, slot], (group, near))

    def f_copy(slot):
        return remote(spare(0, slot), dxrecv.at[slot], f_s.at[slot], f_r.at[slot], (group, far))

    kind = jnp.where(i < pages, 1, 0)
    for k in range(2):
        piece = 2 * lax.rem(i, pages) + k
        slot = lax.rem(piece, pages)
        value = mm(mixed[k * HALF : (k + 1) * HALF, :], wt_ref[...]).astype(BF)
        mine = piece // pages == core
        r = pl.ds(pl.multiple_of(slot * HALF, HALF), HALF)

        @pl.when(mine)
        def _():
            wd[kind, r] = value

        @pl.when(jnp.logical_not(mine))
        def _():
            wd[2 + kind, r] = value
            remote(wd.at[2 + kind, r], drecv.at[kind, slot], d_s.at[kind, slot], d_r.at[kind, slot], (group, near)).start()

    @pl.when(i >= 1)
    def _():
        tick(5 + i, 0)

    @pl.when(i == count - 1)
    def _():
        bias = btotal[0:1, :]
        bias = jnp.concatenate([bias[:, : box + cols], bias[:, box + 2 * cols :]], axis=1)
        wide = total.shape[0]
        for b in range(0, wide, 64):
            amain[b : b + 64, :] = total[b : b + 64, :].astype(BF)
        ending = jnp.where(lax.broadcasted_iota(jnp.int32, (amain.shape[0] - wide, d), 0) == 0, bias, 0.0)
        amain[wide:, :] = ending.astype(BF)
        for j in range(achunks):
            att.start(j)
        for slot in range(pages):
            d_copy(0, slot).wait_recv()
            here = spare(0, slot)
            here[...] = plus(here[...], drecv[0, slot])
            f_copy(slot).start()
        first = 5 + count
        when = [0, 4, 7, 9, 11, 13]
        ticks = 2 * (blocks - 1) + ffn.steps - first + 1
        when += list(range(14, 14 + ticks - len(when)))
        waves = max(achunks + 2 * (att.steps - 1), when[-1] + 1)

        def wave(w, _):
            u = -100
            for n in range(ticks):
                u = jnp.where(w == when[n], first + n, u)
            tick(u, 0)
            for k in range(att.steps):

                @pl.when((w >= 2 * k) & (w - 2 * k < achunks))
                def _():
                    att.step(k, w - 2 * k)

            return 0

        lax.fori_loop(0, waves, wave, 0)
        outs = [pltpu.make_async_copy(ag.at[pl.ds(slot * HALF, HALF)], ig_any.at[pl.ds(slot * HALF, HALF)], o_sem.at[slot]) for slot in range(pages)]
        for slot in range(pages):
            r = pl.ds(slot * HALF, HALF)
            d_copy(1, slot).wait_recv()
            f_copy(slot).wait_recv()
            ag[r] = ag[r] + wd[1, r].astype(F32) + drecv[1, slot].astype(F32) + dxrecv[slot].astype(F32)
            outs[slot].start()
        for slot in range(pages):
            outs[slot].wait()
            f_copy(slot).wait_send()
            d_copy(0, slot).wait_send()
            d_copy(1, slot).wait_send()
            for g in (1, 2, 3):
                e_copy(g, slot).wait_send()
        lax.fori_loop(0, achunks, lambda j, _: (att.finish(j), 0)[1], 0)
        lax.fori_loop(0, chunks, lambda j, _: (ffn.finish(j), 0)[1], 0)
        lax.fori_loop(0, blocks, lambda b, _: (x_copy(b).wait_send(), 0)[1], 0)


def run_backward(hidden, wt, q, k, v, geo, p, inv, vg, g1, act, ug, fl, sl, scaled, second, ctx, weights):
    count, heads = p.shape[:2]
    pages = count // 2
    cols = q.shape[1]
    wide, d = wt.shape
    f = act.shape[2]
    rows = fl.shape[0]
    ways = lax.axis_size("dp")
    levels = ways.bit_length() - 1
    chunk = max(BLOCK, 16 * ways)
    per = chunk // BLOCK
    blocks = -(-((f + d) // BLOCK + 1) // per) * per
    chunks = blocks // per
    arows = 16 * ways
    achunks = -(-(wide + 1) // arows)
    turn = lambda i: lax.rem(i + pages, count)
    page = lambda n: pl.BlockSpec((PAGE, n), lambda i: (turn(i), 0))
    once = lambda a: pl.BlockSpec(a.shape, lambda i: (0,) * len(a.shape), pipeline_mode=pl.Buffered(1))
    return pl.pallas_call(
        partial(backward_kernel, pages=pages, ways=ways, blocks=blocks, per=per, arows=arows),
        out_shape=[S((blocks * BLOCK, d), BF), S((achunks * arows, d), BF), S((rows, d), F32)],
        grid=(count,),
        in_specs=[
            pl.BlockSpec((PAGE, d), lambda i: (page_of(turn(i), pages), 0)),
            once(wt), page(cols), page(cols), page(cols), page(POS),
            pl.BlockSpec((pl.Squeezed(), heads, PAGE, PAGE), lambda i: (turn(i), 0, 0, 0)),
            once(inv), once(vg), WHOLE,
        ]
        + [ANY] * 19,
        out_specs=[ANY] * 3,
        scratch_shapes=[
            V(act.shape, BF), V(ug.shape, BF), V((4, f, d), BF), V((4, cols, d), BF), V(fl.shape, BF), V(sl.shape, BF), V(fl.shape, BF), V(ctx.shape, BF),
            V((2, 2, BLOCK, d), BF), V((SLOTS, 2, BLOCK, d), BF), V((blocks, BLOCK, d), BF), V((blocks, BLOCK, d), BF),
            V((blocks * BLOCK, d), BF), V((blocks * BLOCK, d), BF), V((achunks * arows, d), BF), V((achunks * arows, d), BF),
            V((3, pages, HALF, cols), BF), V((4, pages, HALF, cols), BF), V((PAGE, cols), BF), V((wide, d), F32), V((8, wide), F32), V((PAGE, wide), BF),
            V((2, pages, HALF, d), BF), V((pages, HALF, d), BF), V((rows, d), F32), V((BLOCK, d), F32), V((8, d), F32), V((4, 8, f), F32),
            D((6,)), D((4, 4)), D((blocks,)), D((blocks,)), pltpu.SemaphoreType.REGULAR, D((blocks,)), D((blocks,)), D((4, chunks, levels + 1)), D((4, achunks, levels + 1)),
            D((3, pages)), D((3, pages)), D((2, pages)), D((2, pages)), D((pages,)), D((pages,)), D((pages,)),
        ],
        compiler_params=pltpu.CompilerParams(vmem_limit_bytes=67043328, collective_id=1, has_side_effects=True),
        name="backward",
    )(hidden, wt, q, k, v, geo, p, inv, vg, g1, act, ug, fl, sl, scaled, second, ctx, *weights)


def body(
    hidden_in, box_coords, page_lengths, query_weight, query_bias, key_weight, value_weight, value_bias, box_weight, box_bias, output_weight, output_bias,
    first_gain, first_shift, up_weight, up_bias, down_weight, down_bias, second_gain, second_shift, output_grad,
):
    rates = jnp.power(1000.0, -jnp.arange(FREQ, dtype=F32) / FREQ)
    rates = jnp.tile(rates, POS // FREQ).reshape(1, POS)
    q, k, v, geo, p, ctx, wt, ups, *gathered = run_forward(
        page_lengths, rates, hidden_in, box_coords, box_weight, query_bias, value_bias, box_bias, up_bias,
        query_weight.T, key_weight.T, value_weight.T, output_weight, up_weight, down_weight,
    )
    rows, d = output_grad.shape
    ctx = ctx.reshape(ctx.shape[0], rows, ctx.shape[3])
    weights = (output_weight, up_weight, down_weight, *gathered)
    layer_out, act, ug, fl, sl, scaled, second, inv, vg = run_middle(
        hidden_in, output_grad, ctx, weights, ups, (output_bias, first_gain, first_shift, down_bias, second_gain, second_shift), tile=384 if rows % 384 == 0 else BLOCK
    )
    fin, afin, input_grad = run_backward(hidden_in, wt, q, k, v, geo, p, inv, vg, first_gain, act, ug, fl, sl, scaled, second, ctx, weights)
    h = query_weight.shape[1]
    box = box_weight.shape[1]
    o = output_weight.shape[0]
    f = up_weight.shape[1]
    fin = fin.reshape(-1, d)
    afin = afin.reshape(-1, d)
    take = lambda a, n: afin[a : a + n].astype(F32).T
    tail = fin[f + d + o : f + d + o + 8].astype(F32)
    width = d // 4
    bias = afin[box + 3 * h].astype(F32)
    return (
        layer_out, input_grad,
        take(box, h), bias[box : box + h], take(box + h, h), take(box + 2 * h, h), bias[box + h : box + 2 * h], take(0, box), bias[:box],
        fin[f + d : f + d + o].astype(F32), tail[1, :width], tail[2, :width], tail[3, :width],
        fin[f : f + d].astype(F32), tail[0], fin[:f].astype(F32), tail[4, :width], tail[5, :width], tail[6, :width],
    )


def solution(mesh):
    shared = P()
    by_column = P(None, "tensor")
    by_row = P("tensor", None)
    vector = P("tensor")
    tokens = P(("dp", "tensor"), None)
    in_specs = (
        P("dp", None), P(None, "dp"), P("dp"), by_column, vector, by_column, by_column, vector, by_column, vector, by_row, shared,
        shared, shared, by_column, vector, by_row, shared, shared, shared, tokens,
    )
    out_specs = (
        tokens, tokens, by_column, vector, by_column, by_column, vector, by_column, vector, by_row, vector, vector, vector,
        by_column, vector, by_row, vector, vector, vector,
    )
    return jax.shard_map(body, mesh=mesh, in_specs=in_specs, out_specs=out_specs, check_vma=False)
```

time: 507 us -> 253 us (0.50)
  waiting for transfers between devices: 259 us -> 0 us
  Pallas kernels: 125 us -> 236 us
  local copies, waits for them, and re-layouts: 35.2 us -> 5.81 us
  other arithmetic: 35 us -> 9.56 us
  blocking collectives: 23.1 us -> 0 us
  starting transfers between devices: 13.8 us -> 0 us
  between operations: 14.5 us -> 0.7 us
    ppermute x23 -> x0, waiting for transfers between devices: 137 us -> none  [swap(): return lax.ppermute(x, 'tensor', [(i, i ^ by) for i in range(ways)])]
    psum x1 -> x0, waiting for transfers between devices: 122 us -> none  [body(): dw = lax.psum(dw, 'dp').astype(F32)]
    pallas_call x6 -> x3, Pallas kernels: 125 us -> 236 us  [the longest x1 155 us: run_backward(): pl.pallas_call(partial(backward_kernel, pages=pages, ways=ways, blocks=bl...]
    psum x1 -> x0, blocking collectives: 23.1 us -> none  [body(): db = lax.psum(db[0], 'dp')]
    ppermute x23 -> x0, starting transfers between devices: 13.7 us -> none  [swap(): return lax.ppermute(x, 'tensor', [(i, i ^ by) for i in range(ways)])]
    slice x11 -> x4, local copies, waits for them, and re-layouts: 13.4 us -> 2.43 us  [the longest x1 0.64 us: body(): bias[box + h:box + 2 * h]]
    convert_element_type x4 -> x3, other arithmetic: 14.5 us -> 5.74 us  [the longest x1 4.32 us: body(): fin[:f].astype(F32)]
    another operation x6 -> x0, other arithmetic: 7.34 us -> none
  transfers between devices with their start and end apart: 24 -> 0, of which waited for: 10 -> 0; matrix products, arithmetic and copies ran while one was open for 7% -> 0% of each run, Pallas kernels for 14% -> 0%
where the time goes in v3:
time: 253 us; the launch traced here: 252 us
  Pallas kernels  236 us (93%)
  other arithmetic  9.56 us (4%)
  local copies, waits for them, and re-layouts  5.81 us (2%)
    pallas_call x1, Pallas kernels, run_backward(): pl.pallas_call(partial(backward_kernel, pages=pages, ways=ways, blocks=bl...  155 us
    pallas_call x1, Pallas kernels, run_forward(): pl.pallas_call(partial(forward_kernel, pages=pages), out_shape=[S((rows,...  52.8 us
    pallas_call x1, Pallas kernels, run_middle(): pl.pallas_call(partial(middle_kernel, tile=tile), out_shape=[S((rows, d),...  28.1 us

profile of v3, /device:TPU:0, one launch (start us, length us, event | category | flops | bytes accessed | tf_op | source)
XLA Modules:
  0.0 252.4 jit_solution(13275681052755667510)
XLA Ops:
  0.7 0.6 reshape_tile.3.rates_ref
  1.3 52.8 %forward.1 = (bf16[3072,192]{1,0:T(8,128)(2,1)}, bf16[3072,192]{1,0:T(8,128)(2,1)}, bf16[3072,192]{1,0:T(8,128)(2,1)}, bf16[3072,128]{1,0:T(8,128)(2,1)}, bf16[6...) custom-call(s32[6]{0:T(128)} %len_ref.1, ...), custom_call_target="tpu_custom_call" | custom-call | tf_op jit(solution)/shard_map/forward/pallas_call | solution.py:289
  54.1 28.1 %middle.1 = (bf16[768,768]{1,0:T(8,128)(2,1)}, bf16[4,768,768]{2,1,0:T(8,128)(2,1)}, bf16[4,768,768]{2,1,0:T(8,128)(2,1)}, bf16[768,768]{1,0:T(8,128)(2,1)}, bf1...) custom-call(bf16[3072,768]{1,0:T(8,128)(2,1)} %h_ref.3, ...), custom_call_target="tpu_custom_call" | custom-call | tf_op jit(solution)/shard_map/middle/pallas_call | solution.py:409
  82.2 155.4 %backward.1 = (bf16[1792,768]{1,0:T(8,128)(2,1)}, bf16[1024,768]{1,0:T(8,128)(2,1)}, f32[768,768]{1,0:T(8,128)}) custom-call(bf16[3072,768]{1,0:T(8,128)(2,1)} %h_ref.3, bf16[960,768]{1,0:T(8,128)(2,1)} %get-tuple-element.60.wt_ref, bf16[3072,192]{1,0:T(8,128)(2,1)} %get-tuple-element.61.q_ref, bf16[3072,192]{1,0:T(8,128)(2,1)} %get-tuple-element.62.k_ref, ...), custom_call_target="tpu_custom_call" | custom-call | tf_op jit(solution)/shard_map/backward/pallas_call | solution.py:880
  237.6 2.7 %convert_bitcast_fusion.1 = (f32[768,192]{0,1:T(8,128)}, f32[768,192]{0,1:T(8,128)}, f32[768,192]{0,1:T(8,128)}, f32[192,768]{1,0:T(8,128)}) fusion(bf16[1024,768]{1,0:T(8,128)(2,1)} %get-tuple-element.75, bf16[1792,768]{1,0:T(8,128)(2,1)} %get-tuple-element.76), kind=kLoop, calls=%fused_computation.3 | loop fusion | flops 589824 | bytes 3538944 | tf_op jit(solution)/shard_map/transpose | solution.py:929
  240.3 0.7 slice_convert_fusion.4
  241.0 0.6 fusion.1
  241.7 1.1 convert_bitcast_fusion
  242.8 1.4 copy.40
  244.2 0.6 slice_reduce_fusion.1
  244.8 0.7 slice_convert_fusion.3
  245.5 0.6 fusion
  246.1 0.0 copy-start
  246.1 4.3 %slice_convert_fusion = (f32[768,768]{1,0:T(8,128)}, f32[768,768]{1,0:T(8,128)}) fusion(bf16[1792,768]{1,0:T(8,128)(2,1)} %get-tuple-element.76), kind=kLoop, calls=%fused_computation.1 | loop fusion | flops 1179648 | bytes 7077888 | tf_op jit(solution)/shard_map/convert_element_type | solution.py:937
  250.4 0.6 slice_reduce_fusion
  251.0 0.0 copy-done
  251.0 1.4 copy.42
  (2 shorter events, 0.0 us)
Async XLA Ops:
  246.1 4.9 %copy-start = (f32[768,768]{1,0:T(8,128)S(1)}, f32[768,768]{1,0:T(8,128)}, u32[]{:S(2)}) copy-start(f32[768,768]{1,0:T(8,128)} %get-tuple-element.130) | copy-start | bytes 7077892

commit v4 on v3

--- a/solution.py
+++ b/solution.py
@@ -117,43 +117,85 @@
     return jnp.where(i < pages, (1 - chip) * pages + i, chip * pages + i - pages)
 
 
+def weight_chunks(arrays):
+    chunks = []
+    for a, w in enumerate(arrays):
+        n = w.shape[0] // 4
+        step = n // 2 if n > PART // 2 else n
+        chunks += [(a, s, step) for s in range(0, n, step)]
+    return chunks
+
+
+def splits(chunk):
+    return chunk[2] % 32 == 0
+
+
 def forward_kernel(len_ref, rates_ref, h_ref, coords_ref, wb_ref, qb_ref, vb_ref, bb_ref, ub_ref, wq_any, wk_any, wv_any, wo_any, wu_any, wd_any,
                    q_ref, k_ref, v_ref, geo_ref, p_ref, ctx_any, wt_any, ua_any, no_any, nu_any, nd_any, fo_any, fu_any, fd_any, co_any, cu_any, cd_any,
-                   wt, cat_q, cat_k, cpage, ubs, l_s, x_s, x_r, y_s, y_r, n_s, n_r, c_s, c_r, u_s, u_r, t_s, t_r, *, pages):
+                   wt, cat_q, cat_k, cpage, ubs, l_s, x_s, x_r, y_s, y_r, z_s, z_r, n_s, n_r, c_s, c_r, u_s, u_r, t_s, t_r, *, pages):
     i = pl.program_id(0)
     cols = q_ref.shape[1]
     heads = cols // HEAD
     box = heads * POS
     group, place, core, chip, near, far, cross = seats()
-    side = lax.rem(group, 2)
-    beside = group + 1 - 2 * side
+    y = lax.rem(group, 2)
+    z = lax.rem(group // 2, 2)
+    beside = group + 1 - 2 * y
+    above = group + 2 - 4 * z
+    q = y + 2 * z
+    quarter = (q, q + 1 - 2 * y, q + 2 - 4 * z, q + 3 - 2 * y - 4 * z)
     own = (wo_any, wu_any, wd_any)
     nears = (no_any, nu_any, nd_any)
     fars = (fo_any, fu_any, fd_any)
     crosses = (co_any, cu_any, cd_any)
-    chunks = []
-    for a, w in enumerate(own):
-        half = w.shape[0] // 2
-        step = min(PART, half)
-        chunks += [(a, s, step) for s in range(0, half, step)]
-
-    def rows(c, other):
+    chunks = weight_chunks(own)
+
+    def rows(c, k, part=None):
         a, s, n = chunks[c]
-        half = own[a].shape[0] // 2
-        return a, pl.ds(pl.multiple_of(half * (1 - side if other else side) + s, 16), n)
+        start = quarter[k] * (own[a].shape[0] // 4) + s
+        if part is not None and splits(chunks[c]):
+            n //= 2
+            start += part * n
+        return pl.ds(pl.multiple_of(start, 16), n)
+
+    def hop(c, k, sems, to, part=None, source=fars):
+        a = chunks[c][0]
+        r = rows(c, k, part)
+        return remote(source[a].at[r], fars[a].at[r], sems[0], sems[1], to)
 
     def x_copy(c):
-        a, r = rows(c, False)
-        return remote(own[a].at[r], fars[a].at[r], x_s.at[c], x_r.at[c], (group, far))
-
-    def y_copy(c, other=False):
-        a, r = rows(c, other)
-        return remote(fars[a].at[r], fars[a].at[r], y_s.at[c], y_r.at[c], (beside, place))
-
-    def c_copy(c, other):
-        a, r = rows(c, other)
-        k = 1 if other else 0
+        return hop(c, 0, (x_s.at[c], x_r.at[c]), (group, far), source=own)
+
+    def y_copy(c, step, k):
+        return hop(c, k, (y_s.at[step, c], y_r.at[step, c]), (beside, place), None if step == 0 else 0)
+
+    def z_copy(c, step, k):
+        return hop(c, k, (z_s.at[step, c], z_r.at[step, c]), (above, place), None if step == 0 else 1)
+
+    def c_copy(c, k):
+        a = chunks[c][0]
+        r = rows(c, k)
         return remote(fars[a].at[r], crosses[a].at[r], c_s.at[k, c], c_r.at[k, c], (group, near))
+
+    def stage(n, c):
+        if n == 0:
+            x_copy(c).wait_recv()
+            y_copy(c, 0, 0).start()
+            z_copy(c, 0, 0).start()
+            c_copy(c, 0).start()
+        elif n == 1:
+            y_copy(c, 0, 1).wait_recv()
+            if splits(chunks[c]):
+                z_copy(c, 1, 1).start()
+            z_copy(c, 0, 2).wait_recv()
+            y_copy(c, 1, 2).start()
+            c_copy(c, 1).start()
+            c_copy(c, 2).start()
+        else:
+            y_copy(c, 1, 3).wait_recv()
+            if splits(chunks[c]):
+                z_copy(c, 1, 3).wait_recv()
+            c_copy(c, 3).start()
 
     n_copies = [remote(own[a], nears[a], n_s.at[a], n_r.at[a], (group, near)) for a in range(3)]
     u_copies = [remote(ubs.at[0], ubs.at[g], u_s.at[g - 1], u_r.at[g - 1], (group, d)) for g, d in ((1, near), (2, far), (3, cross))]
@@ -166,7 +208,7 @@
             c.start()
         ubs[0] = row(ub_ref)
         barrier = pltpu.get_barrier_semaphore()
-        peers = [(group, near), (group, far), (group, cross), (beside, place)]
+        peers = [(group, near), (group, far), (group, cross), (beside, place), (above, place)]
         for device in peers:
             pl.semaphore_signal(barrier, inc=1, device_id=device, device_id_type=MESH)
         pl.semaphore_wait(barrier, len(peers))
@@ -197,20 +239,37 @@
         cat_q[head, :, POS:] = q_ref[:, lanes]
         cat_k[head, :, :POS] = geo
         cat_k[head, :, POS:] = k_ref[:, lanes]
+    count = 2 * pages
+    plan = {0: [(0, 0)], 1: [(0, 1)], 2: [(1, 0)], 3: [(0, 2)], 4: [(1, 1)], 5: [(0, 3), (0, 4)], 7: [(1, 2), (2, 1)], 8: [(1, 3), (1, 4)], 10: [(2, 0), (2, 2)], 11: [(2, 3), (2, 4)]}
+
+    def tick(odd):
+        for at, todo in plan.items():
+            if at % 2 == odd:
+
+                @pl.when(i == at // 2)
+                def _():
+                    for n, c in todo:
+                        stage(n, c)
+
     valid = lax.broadcasted_iota(jnp.int32, (1, PAGE), 1) < length
     scale = LOG2E / math.sqrt(HEAD)
+    s = mm_nt(cat_q[0], cat_k[0])
     for head in range(heads):
         lanes = slice(head * HEAD, (head + 1) * HEAD)
-        s = mm_nt(cat_q[head], cat_k[head])
-        s = jnp.where(valid, s, -1e30)
-        top = jnp.max(s, axis=1, keepdims=True)
-        e = jnp.exp2((s - top) * scale)
+        now = s
+        if head + 1 < heads:
+            s = mm_nt(cat_q[head + 1], cat_k[head + 1])
+        now = jnp.where(valid, now, -1e30)
+        top = jnp.max(now, axis=1, keepdims=True)
+        e = jnp.exp2((now - top) * scale)
         total = jnp.sum(e, axis=1, keepdims=True)
         p = (e * (1.0 / total)).astype(BF)
         p_ref[head] = p
         c = mm(p, v_ref[:, lanes]).astype(BF)
         for k in range(2):
             cpage[2 * i + k, :, lanes] = c[k * HALF : (k + 1) * HALF]
+        if head == heads // 2:
+            tick(0)
     for k in range(2):
         piece = 2 * lax.rem(i, pages) + k
         oc = piece // pages
@@ -230,20 +289,7 @@
         def _():
             pltpu.make_async_copy(cpage.at[2 * i + k], ctx_any.at[0, slot], t_r.at[0, slot]).start()
 
-    count = 2 * pages
-
-    def forward_on(c):
-        x_copy(c).wait_recv()
-        y_copy(c).start()
-        c_copy(c, False).start()
-
-    plan = {0: [0], 1: [1], 3: [2], 4: [3], 5: [4]}
-    for at, todo in plan.items():
-
-        @pl.when(i == at)
-        def _():
-            for c in todo:
-                forward_on(c)
+    tick(1)
 
     @pl.when(i == count - 1)
     def _():
@@ -252,9 +298,6 @@
             u.wait()
         keep_ub = pltpu.make_async_copy(ubs, ua_any, u_s.at[3])
         keep_ub.start()
-        for c in range(len(chunks)):
-            y_copy(c, True).wait_recv()
-            c_copy(c, True).start()
         for n in n_copies:
             n.wait()
         keep_ub.wait()
@@ -272,9 +315,12 @@
 
         for c in range(len(chunks)):
             x_copy(c).wait_send()
-            y_copy(c).wait_send()
-            c_copy(c, False).wait()
-            c_copy(c, True).wait()
+            for step in range(2):
+                y_copy(c, step, 2 * step).wait_send()
+                if step == 0 or splits(chunks[c]):
+                    z_copy(c, step, step).wait_send()
+            for k in range(4):
+                c_copy(c, k).wait()
 
 
 def run_forward(lengths, rates, hidden, coords, wb, qb, vb, bb, ub, wq, wk, wv, wo, wu, wd):
@@ -283,7 +329,7 @@
     pages = lengths.shape[0] // 2
     wide = wb.shape[1] + 3 * cols
     own = (wo, wu, wd)
-    n = sum((x.shape[0] // 2) // min(PART, x.shape[0] // 2) for x in own)
+    n = len(weight_chunks(own))
     page_out = lambda w: pl.BlockSpec((PAGE, w), lambda i: (i, 0))
     rows = 2 * pages * PAGE
     return pl.pallas_call(
@@ -304,7 +350,7 @@
         + [page_out(POS), pl.BlockSpec((pl.Squeezed(), heads, PAGE, PAGE), lambda i: (i, 0, 0, 0))]
         + [ANY] * 12,
         scratch_shapes=[V((wide, d), BF), V((heads, PAGE, POS + HEAD), BF), V((heads, PAGE, POS + HEAD), BF), V((4 * pages, HALF, cols), BF), V((4, 1, ub.shape[0]), F32)]
-        + [D((4,)), D((n,)), D((n,)), D((n,)), D((n,)), D((3,)), D((3,)), D((2, n)), D((2, n)), D((4,)), D((3,)), D((4 * pages,)), D((4, pages))],
+        + [D((4,)), D((n,)), D((n,)), D((2, n)), D((2, n)), D((2, n)), D((2, n)), D((3,)), D((3,)), D((4, n)), D((4, n)), D((4,)), D((3,)), D((4 * pages,)), D((4, pages))],
         compiler_params=pltpu.CompilerParams(vmem_limit_bytes=56 << 20, collective_id=0, has_side_effects=True),
         name="forward",
     )(lengths, rates, hidden, coords, wb, qb, vb, bb, ub, wq, wk, wv, wo, wu, wd)
@@ -336,6 +382,10 @@
         c.wait()
     head_loads[1].wait()
     vg_ref[...] = jnp.zeros_like(vg_ref)
+    for g in range(groups):
+        loads[1][g].wait()
+        loads[2][g].wait()
+    head_loads[2].wait()
     steps = rows // tile
 
     def stores(i):
@@ -355,22 +405,15 @@
         scaled1[r] = scaled
         inv_ref[r] = inverse
         fl[r] = f.astype(BF)
+        x = mm(fl[r], wu[0])
         for g in range(groups):
-
-            @pl.when(i == 0)
-            def _():
-                loads[1][g].wait()
-
-            x = mm(fl[r], wu[g]) + ub_ref[g]
-            half = 0.5 + 0.5 * lax.erf(x * 0.7071067811865476)
-            a = (x * half).astype(BF)
+            now = x + ub_ref[g]
+            if g + 1 < groups:
+                x = mm(fl[r], wu[g + 1])
+            half = 0.5 + 0.5 * lax.erf(now * 0.7071067811865476)
+            a = (now * half).astype(BF)
             act[g, r] = a
-            ug[g, r] = (half + x * jnp.exp(-0.5 * x * x) * 0.3989422804014327).astype(BF)
-
-            @pl.when(i == 0)
-            def _():
-                loads[2][g].wait()
-
+            ug[g, r] = (half + now * jnp.exp(-0.5 * now * now) * 0.3989422804014327).astype(BF)
             part = mm(a, wd[g])
             if g == 0:
                 ffn[...] = part
@@ -379,10 +422,6 @@
 
         scaled, inverse = normal(ffn[...] + row(db_ref) + first[...])
         lo[r] = (scaled * row(g2_ref) + row(s2_ref)).astype(BF)
-
-        @pl.when(i == 0)
-        def _():
-            head_loads[2].wait()
 
         o = og[r].astype(F32)
         second = normal_back(o * row(g2_ref), scaled, inverse)
@@ -903,6 +942,70 @@
     )(hidden, wt, q, k, v, geo, p, inv, vg, g1, act, ug, fl, sl, scaled, second, ctx, *weights)
 
 
+def finish_kernel(fin_any, afin_any, down_any, up_any, out_any, q_any, k_any, v_any, box_any,
+                  ub_ref, qb_ref, vb_ref, bb_ref, n0_ref, n1_ref, n2_ref, n3_ref, n4_ref, n5_ref,
+                  low, alow, full, afull, boxt, l_s, o_s):
+    d = low.shape[1]
+    cols = q_any.shape[0]
+    box = box_any.shape[1]
+    wide = box + 3 * cols
+    f = down_any.shape[0]
+    up = up_any.shape[0]
+    rows = f + up + cols
+    pieces = [(low, fin_any, full, a, BLOCK, (down_any if a < f else up_any), a % f) for a in range(0, f + up, BLOCK)]
+    pieces += [(low, fin_any, full, f + up, cols + 16, out_any, 0)]
+    pieces += [(alow, afin_any, afull, a, min(cols, wide + 16 - a), None, 0) for a in range(0, box, cols)]
+    pieces += [(alow, afin_any, afull, box + n * cols, cols + (16 if n == 2 else 0), x, 0) for n, x in enumerate((q_any, k_any, v_any))]
+    loads = [pltpu.make_async_copy(src.at[pl.ds(a, n)], buf.at[pl.ds(a, n)], l_s.at[j]) for j, (buf, src, _, a, n, _, _) in enumerate(pieces)]
+    order = list(range(len(pieces) - 3 - box // cols, len(pieces))) + list(range(len(pieces) - 3 - box // cols))
+    for j in order:
+        loads[j].start()
+    stores = []
+    for j in order:
+        buf, _, wide_buf, a, n, dst, to = pieces[j]
+        loads[j].wait()
+        wide_buf[a : a + n, :] = buf[a : a + n, :].astype(F32)
+        if dst is not None:
+            n = min(n, dst.shape[0])
+            c = pltpu.make_async_copy(wide_buf.at[pl.ds(a, n)], dst.at[pl.ds(to, n)], o_s.at[len(stores)])
+            c.start()
+            stores.append(c)
+        elif a + n == box:
+            boxt[...] = afull[:box, :].T
+            c = pltpu.make_async_copy(boxt, box_any, o_s.at[len(stores)])
+            c.start()
+            stores.append(c)
+    tail = full[rows : rows + 8, :]
+    ub_ref[...] = tail[0]
+    width = d // 4
+    for n, ref in enumerate((n0_ref, n1_ref, n2_ref, n3_ref, n4_ref, n5_ref)):
+        ref[...] = tail[1 + n, :width]
+    bias = afull[wide : wide + 8, :][0]
+    bb_ref[...] = bias[:box]
+    qb_ref[...] = bias[box : box + cols]
+    vb_ref[...] = bias[box + cols : box + 2 * cols]
+    for c in stores:
+        c.wait()
+
+
+def run_finish(fin, afin, f, up, cols, box):
+    d = fin.shape[1]
+    rows = f + up + cols + 16
+    wide = box + 3 * cols + 16
+    width = d // 4
+    vectors = [S((f,), F32), S((cols,), F32), S((cols,), F32), S((box,), F32)] + [S((width,), F32)] * 6
+    n = (f + up) // BLOCK + 4 + box // cols
+    return pl.pallas_call(
+        finish_kernel,
+        out_shape=[S((f, d), F32), S((up, d), F32), S((cols, d), F32)] + [S((cols, d), F32)] * 3 + [S((d, box), F32)] + vectors,
+        in_specs=[ANY] * 2,
+        out_specs=[ANY] * 7 + [WHOLE] * 10,
+        scratch_shapes=[V((rows, d), BF), V((wide, d), BF), V((rows, d), F32), V((wide, d), F32), V((d, box), F32), D((n,)), D((n,))],
+        compiler_params=pltpu.CompilerParams(vmem_limit_bytes=62 << 20),
+        name="finish",
+    )(fin, afin)
+
+
 def body(
     hidden_in, box_coords, page_lengths, query_weight, query_bias, key_weight, value_weight, value_bias, box_weight, box_bias, output_weight, output_bias,
     first_gain, first_shift, up_weight, up_bias, down_weight, down_bias, second_gain, second_shift, output_grad,
@@ -920,21 +1023,10 @@
         hidden_in, output_grad, ctx, weights, ups, (output_bias, first_gain, first_shift, down_bias, second_gain, second_shift), tile=384 if rows % 384 == 0 else BLOCK
     )
     fin, afin, input_grad = run_backward(hidden_in, wt, q, k, v, geo, p, inv, vg, first_gain, act, ug, fl, sl, scaled, second, ctx, weights)
-    h = query_weight.shape[1]
-    box = box_weight.shape[1]
-    o = output_weight.shape[0]
-    f = up_weight.shape[1]
-    fin = fin.reshape(-1, d)
-    afin = afin.reshape(-1, d)
-    take = lambda a, n: afin[a : a + n].astype(F32).T
-    tail = fin[f + d + o : f + d + o + 8].astype(F32)
-    width = d // 4
-    bias = afin[box + 3 * h].astype(F32)
+    cols = query_weight.shape[1]
+    down, up, out, q, k, v, box, ub, qb, vb, bb, *norms = run_finish(fin, afin, up_weight.shape[1], d, cols, box_weight.shape[1])
     return (
-        layer_out, input_grad,
-        take(box, h), bias[box : box + h], take(box + h, h), take(box + 2 * h, h), bias[box + h : box + 2 * h], take(0, box), bias[:box],
-        fin[f + d : f + d + o].astype(F32), tail[1, :width], tail[2, :width], tail[3, :width],
-        fin[f : f + d].astype(F32), tail[0], fin[:f].astype(F32), tail[4, :width], tail[5, :width], tail[6, :width],
+        layer_out, input_grad, q.T, qb, k.T, v.T, vb, box, bb, out, norms[0], norms[1], norms[2], up, ub, down, norms[3], norms[4], norms[5],
     )
 
 

time: 253 us -> 229 us (0.905)
  Pallas kernels: 236 us -> 224 us
  other arithmetic: 9.56 us -> 0.01 us
    pallas_call x1, Pallas kernels: 52.8 us -> 41.2 us  [run_forward(): pl.pallas_call(partial(forward_kernel, pages=pages), out_shape=[S((rows,...]
    convert_element_type x3 -> x0, other arithmetic: 5.74 us -> none  [the longest x1 4.32 us: body(): fin[:f].astype(F32)]
    pallas_call x0 -> x1, Pallas kernels: none -> 5.49 us  [run_finish(): pl.pallas_call(finish_kernel, out_shape=[S((f, d), F32), S((up, d), F32),...]
    pallas_call x1, Pallas kernels: 28.1 us -> 22.6 us  [run_middle(): pl.pallas_call(partial(middle_kernel, tile=tile), out_shape=[S((rows, d),...]
    transpose x2 -> x0, other arithmetic: 3.81 us -> none  [body(): take = lambda a, n: afin[a:a + n].astype(F32).T]
where the time goes in v4:
time: 229 us
  Pallas kernels  224 us (98%)
  local copies, waits for them, and re-layouts  3.82 us (2%)
    pallas_call x1, Pallas kernels, run_backward(): pl.pallas_call(partial(backward_kernel, pages=pages, ways=ways, blocks=bl...  155 us
    pallas_call x1, Pallas kernels, run_forward(): pl.pallas_call(partial(forward_kernel, pages=pages), out_shape=[S((rows,...  41.2 us
    pallas_call x1, Pallas kernels, run_middle(): pl.pallas_call(partial(middle_kernel, tile=tile), out_shape=[S((rows, d),...  22.6 us
    pallas_call x1, Pallas kernels, run_finish(): pl.pallas_call(finish_kernel, out_shape=[S((f, d), F32), S((up, d), F32),...  5.49 us

profile of v4, /device:TPU:0, one launch (start us, length us, event | category | flops | bytes accessed | tf_op | source)
XLA Modules:
  0.0 228.6 jit_solution(18125541933169930326)
XLA Ops:
  0.7 0.6 reshape_tile.3.rates_ref
  1.3 41.2 %forward.1 = (bf16[3072,192]{1,0:T(8,128)(2,1)}, bf16[3072,192]{1,0:T(8,128)(2,1)}, bf16[3072,192]{1,0:T(8,128)(2,1)}, bf16[3072,128]{1,0:T(8,128)(2,1)}, bf16[6...) custom-call(s32[6]{0:T(128)} %len_ref.1, ...), custom_call_target="tpu_custom_call" | custom-call | tf_op jit(solution)/shard_map/forward/pallas_call | solution.py:335
  42.5 22.6 %middle.1 = (bf16[768,768]{1,0:T(8,128)(2,1)}, bf16[4,768,768]{2,1,0:T(8,128)(2,1)}, bf16[4,768,768]{2,1,0:T(8,128)(2,1)}, bf16[768,768]{1,0:T(8,128)(2,1)}, bf1...) custom-call(bf16[3072,768]{1,0:T(8,128)(2,1)} %h_ref.3, ...), custom_call_target="tpu_custom_call" | custom-call | tf_op jit(solution)/shard_map/middle/pallas_call | solution.py:448
  65.1 154.7 %backward.1 = (bf16[1792,768]{1,0:T(8,128)(2,1)}, bf16[1024,768]{1,0:T(8,128)(2,1)}, f32[768,768]{1,0:T(8,128)}) custom-call(bf16[3072,768]{1,0:T(8,128)(2,1)} %h_ref.3, bf16[960,768]{1,0:T(8,128)(2,1)} %get-tuple-element.77.wt_ref, bf16[3072,192]{1,0:T(8,128)(2,1)} %get-tuple-element.78.q_ref, bf16[3072,192]{1,0:T(8,128)(2,1)} %get-tuple-element.79.k_ref, ...), custom_call_target="tpu_custom_call" | custom-call | tf_op jit(solution)/shard_map/backward/pallas_call | solution.py:919
  219.9 5.5 %finish.1 = (f32[768,768]{1,0:T(8,128)}, f32[768,768]{1,0:T(8,128)}, f32[192,768]{1,0:T(8,128)}, f32[192,768]{1,0:T(8,128)}, f32[192,768]{1,0:T(8,128)}, /*index...) custom-call(bf16[1792,768]{1,0:T(8,128)(2,1)} %get-tuple-element.92., ...), custom_call_target="tpu_custom_call" | custom-call | tf_op jit(solution)/shard_map/finish/pallas_call | solution.py:998
  225.4 3.2 %copy.41 = f32[768,768]{1,0:T(8,128)} copy(f32[768,768]{1,0:T(8,128)} %get-tuple-element.131) | data formatting | bytes 4718592
  (2 shorter events, 0.0 us)

commit v5 on v4

--- a/solution.py
+++ b/solution.py
@@ -251,21 +251,21 @@
                     for n, c in todo:
                         stage(n, c)
 
-    valid = lax.broadcasted_iota(jnp.int32, (1, PAGE), 1) < length
+    valid = lax.broadcasted_iota(jnp.int32, (PAGE, 1), 0) < length
     scale = LOG2E / math.sqrt(HEAD)
-    s = mm_nt(cat_q[0], cat_k[0])
+    s = mm_nt(cat_k[0], cat_q[0])
     for head in range(heads):
         lanes = slice(head * HEAD, (head + 1) * HEAD)
         now = s
         if head + 1 < heads:
-            s = mm_nt(cat_q[head + 1], cat_k[head + 1])
+            s = mm_nt(cat_k[head + 1], cat_q[head + 1])
         now = jnp.where(valid, now, -1e30)
-        top = jnp.max(now, axis=1, keepdims=True)
+        top = jnp.max(now, axis=0, keepdims=True)
         e = jnp.exp2((now - top) * scale)
-        total = jnp.sum(e, axis=1, keepdims=True)
+        total = jnp.sum(e, axis=0, keepdims=True)
         p = (e * (1.0 / total)).astype(BF)
         p_ref[head] = p
-        c = mm(p, v_ref[:, lanes]).astype(BF)
+        c = mm_tn(p, v_ref[:, lanes]).astype(BF)
         for k in range(2):
             cpage[2 * i + k, :, lanes] = c[k * HALF : (k + 1) * HALF]
         if head == heads // 2:
@@ -466,17 +466,22 @@
         self.main, self.recv, self.out, self.sems = main, recv, out, sems
         self.group, self.place, self.rows, self.levels = group, place, rows, levels
         self.steps = 2 * levels - 1
-
-    def bit(self, j, s):
+        self.sides = [lax.rem(group // 2**n, 2) for n in range(levels)]
+        self.mates = [group + 2**n * (1 - 2 * side) for n, side in enumerate(self.sides)]
+
+    def pick(self, j, s, values):
         if s > 1:
-            return 2**s
-        return jnp.where(lax.rem(j, 4) == 3, 2 - s, 1 + s)
+            return values[s]
+        return jnp.where((j & 3) == 3, values[1 - s], values[s])
 
     def side(self, j, s):
-        return lax.rem(self.group // self.bit(j, s), 2)
+        return self.pick(j, s, self.sides)
 
     def partner(self, j, s):
-        return (self.group + self.bit(j, s) * (1 - 2 * self.side(j, s)), self.place)
+        return (self.pick(j, s, self.mates), self.place)
+
+    def got(self, n, sem, j, s):
+        arrived(self.recv.at[pl.ds(0, n)], self.sems.at[sem, j, s])
 
     def low(self, j, s):
         at = j * self.rows
@@ -508,8 +513,8 @@
     def step(self, k, j):
         last = self.levels - 1
         if k <= last:
-            self.r_copy(j, k).wait_recv()
             n = self.rows >> (k + 1)
+            self.got(n, 1, j, k)
             mine = self.span(self.low(j, k + 1), n)
             got = self.span(j * self.rows + self.rows - (self.rows >> k), n)
             self.main[mine] = self.main[mine] + self.recv[got]
@@ -520,16 +525,16 @@
                 self.g_copy(j, last).start()
         else:
             s = 2 * self.levels - 2 - k
-            self.g_copy(j, s + 1).wait_recv()
+            self.got(self.rows >> (s + 2), 3, j, s + 1)
             if s + 1 == last:
-                self.keep(j).wait()
+                self.got(self.rows >> self.levels, 0, j, self.levels)
             self.g_copy(j, s).start()
 
     def finish(self, j):
-        self.g_copy(j, 0).wait_recv()
+        self.got(self.rows >> 1, 3, j, 0)
         for s in range(self.levels):
-            self.r_copy(j, s).wait_send()
-            self.g_copy(j, s).wait_send()
+            self.got(self.rows >> (s + 1), 0, j, s)
+            self.got(self.rows >> (s + 1), 2, j, s)
 
 
 SLOTS = 3
@@ -705,8 +710,6 @@
         c_add(downs - 1)
         for c in wo_loads:
             c.wait()
-        for n in (1, 5):
-            loads[n].wait()
         vg[...] = vgin_ref[...]
         ubg[...] = jnp.zeros_like(ubg)
 
@@ -766,6 +769,8 @@
 
             return 0
 
+        for n in (1, 5):
+            loads[n].wait()
         lax.fori_loop(downs, ups, up_block, 0)
         block(ups, "out")
         c_add(ups - 1)
@@ -794,24 +799,21 @@
     geo = geo_ref[...]
     co, si = mixing(geo.astype(F32))
     factor = 1.0 / math.sqrt(HEAD)
+    lanes = [slice(head * HEAD, (head + 1) * HEAD) for head in range(heads)]
+    dp = mm_nt(v_ref[:, lanes[0]], dcp[:, lanes[0]])
     for head in range(heads):
-        lanes = slice(head * HEAD, (head + 1) * HEAD)
+        now = dp
+        if head + 1 < heads:
+            dp = mm_nt(v_ref[:, lanes[head + 1]], dcp[:, lanes[head + 1]])
         p = p_ref[head]
-        dcl = dcp[:, lanes]
-        mixed[:, box + 2 * cols + head * HEAD : box + 2 * cols + (head + 1) * HEAD] = mm_tn(p, dcl).astype(BF)
-        dp = mm_nt(dcl, v_ref[:, lanes])
+        mixed[:, box + 2 * cols + head * HEAD : box + 2 * cols + (head + 1) * HEAD] = mm(p, dcp[:, lanes[head]]).astype(BF)
         pf = p.astype(F32)
-        delta = jnp.sum(pf * dp, axis=1, keepdims=True)
-        ds = (pf * (dp - delta)).astype(BF)
-        both = mm(ds, jnp.concatenate([geo, k_ref[:, lanes]], axis=1)) * factor
+        delta = jnp.sum(pf * now, axis=0, keepdims=True)
+        ds = (pf * (now - delta)).astype(BF)
+        both = mm_tn(ds, jnp.concatenate([geo, k_ref[:, lanes[head]]], axis=1)) * factor
         mixed[:, box + head * HEAD : box + (head + 1) * HEAD] = both[:, POS:].astype(BF)
         mixed[:, head * POS : (head + 1) * POS] = mix(both[:, :POS], co, si).astype(BF)
-        mixed[:, box + cols + head * HEAD : box + cols + (head + 1) * HEAD] = (mm_tn(ds, q_ref[:, lanes]) * factor).astype(BF)
-        if head == heads // 2:
-
-            @pl.when(i < 2)
-            def _():
-                tick(4 + i, 0)
+        mixed[:, box + cols + head * HEAD : box + cols + (head + 1) * HEAD] = (mm(ds, q_ref[:, lanes[head]]) * factor).astype(BF)
 
     total[...] += mm_tn(mixed[...], h_ref[...])
     btotal[0:1, :] += columns(mixed[...].astype(F32))
@@ -823,10 +825,11 @@
         return remote(spare(0, slot), dxrecv.at[slot], f_s.at[slot], f_r.at[slot], (group, far))
 
     kind = jnp.where(i < pages, 1, 0)
+    dx = mm(mixed[...], wt_ref[...]).astype(BF)
     for k in range(2):
         piece = 2 * lax.rem(i, pages) + k
         slot = lax.rem(piece, pages)
-        value = mm(mixed[k * HALF : (k + 1) * HALF, :], wt_ref[...]).astype(BF)
+        value = dx[k * HALF : (k + 1) * HALF]
         mine = piece // pages == core
         r = pl.ds(pl.multiple_of(slot * HALF, HALF), HALF)
 
@@ -838,6 +841,10 @@
         def _():
             wd[2 + kind, r] = value
             remote(wd.at[2 + kind, r], drecv.at[kind, slot], d_s.at[kind, slot], d_r.at[kind, slot], (group, near)).start()
+
+    @pl.when(i < 2)
+    def _():
+        tick(4 + i, 0)
 
     @pl.when(i >= 1)
     def _():
@@ -942,9 +949,9 @@
     )(hidden, wt, q, k, v, geo, p, inv, vg, g1, act, ug, fl, sl, scaled, second, ctx, *weights)
 
 
-def finish_kernel(fin_any, afin_any, down_any, up_any, out_any, q_any, k_any, v_any, box_any,
+def finish_kernel(fin_any, afin_any, grad_any, down_any, up_any, out_any, q_any, k_any, v_any, box_any, ig_any,
                   ub_ref, qb_ref, vb_ref, bb_ref, n0_ref, n1_ref, n2_ref, n3_ref, n4_ref, n5_ref,
-                  low, alow, full, afull, boxt, l_s, o_s):
+                  low, alow, full, afull, boxt, grad, l_s, o_s):
     d = low.shape[1]
     cols = q_any.shape[0]
     box = box_any.shape[1]
@@ -960,6 +967,9 @@
     order = list(range(len(pieces) - 3 - box // cols, len(pieces))) + list(range(len(pieces) - 3 - box // cols))
     for j in order:
         loads[j].start()
+    grad_in = pltpu.make_async_copy(grad_any, grad, l_s.at[len(pieces)])
+    grad_out = pltpu.make_async_copy(grad, ig_any, o_s.at[len(pieces)])
+    grad_in.start()
     stores = []
     for j in order:
         buf, _, wide_buf, a, n, dst, to = pieces[j]
@@ -975,6 +985,9 @@
             c = pltpu.make_async_copy(boxt, box_any, o_s.at[len(stores)])
             c.start()
             stores.append(c)
+    grad_in.wait()
+    grad_out.start()
+    stores.append(grad_out)
     tail = full[rows : rows + 8, :]
     ub_ref[...] = tail[0]
     width = d // 4
@@ -988,22 +1001,22 @@
         c.wait()
 
 
-def run_finish(fin, afin, f, up, cols, box):
+def run_finish(fin, afin, grad, f, up, cols, box):
     d = fin.shape[1]
     rows = f + up + cols + 16
     wide = box + 3 * cols + 16
     width = d // 4
     vectors = [S((f,), F32), S((cols,), F32), S((cols,), F32), S((box,), F32)] + [S((width,), F32)] * 6
-    n = (f + up) // BLOCK + 4 + box // cols
+    n = (f + up) // BLOCK + 5 + box // cols
     return pl.pallas_call(
         finish_kernel,
-        out_shape=[S((f, d), F32), S((up, d), F32), S((cols, d), F32)] + [S((cols, d), F32)] * 3 + [S((d, box), F32)] + vectors,
-        in_specs=[ANY] * 2,
-        out_specs=[ANY] * 7 + [WHOLE] * 10,
-        scratch_shapes=[V((rows, d), BF), V((wide, d), BF), V((rows, d), F32), V((wide, d), F32), V((d, box), F32), D((n,)), D((n,))],
+        out_shape=[S((f, d), F32), S((up, d), F32), S((cols, d), F32)] + [S((cols, d), F32)] * 3 + [S((d, box), F32), S(grad.shape, F32)] + vectors,
+        in_specs=[ANY] * 3,
+        out_specs=[ANY] * 8 + [WHOLE] * 10,
+        scratch_shapes=[V((rows, d), BF), V((wide, d), BF), V((rows, d), F32), V((wide, d), F32), V((d, box), F32), V(grad.shape, F32), D((n,)), D((n,))],
         compiler_params=pltpu.CompilerParams(vmem_limit_bytes=62 << 20),
         name="finish",
-    )(fin, afin)
+    )(fin, afin, grad)
 
 
 def body(
@@ -1022,9 +1035,9 @@
     layer_out, act, ug, fl, sl, scaled, second, inv, vg = run_middle(
         hidden_in, output_grad, ctx, weights, ups, (output_bias, first_gain, first_shift, down_bias, second_gain, second_shift), tile=384 if rows % 384 == 0 else BLOCK
     )
-    fin, afin, input_grad = run_backward(hidden_in, wt, q, k, v, geo, p, inv, vg, first_gain, act, ug, fl, sl, scaled, second, ctx, weights)
+    fin, afin, grad = run_backward(hidden_in, wt, q, k, v, geo, p, inv, vg, first_gain, act, ug, fl, sl, scaled, second, ctx, weights)
     cols = query_weight.shape[1]
-    down, up, out, q, k, v, box, ub, qb, vb, bb, *norms = run_finish(fin, afin, up_weight.shape[1], d, cols, box_weight.shape[1])
+    down, up, out, q, k, v, box, input_grad, ub, qb, vb, bb, *norms = run_finish(fin, afin, grad, up_weight.shape[1], d, cols, box_weight.shape[1])
     return (
         layer_out, input_grad, q.T, qb, k.T, v.T, vb, box, bb, out, norms[0], norms[1], norms[2], up, ub, down, norms[3], norms[4], norms[5],
     )

time: 229 us -> 221 us (0.965)
  Pallas kernels: 224 us -> 219 us
  local copies, waits for them, and re-layouts: 3.82 us -> 0.59 us
    pallas_call x1, Pallas kernels: 155 us -> 150 us  [run_backward(): pl.pallas_call(partial(backward_kernel, pages=pages, ways=ways, blocks=bl...]
    unnamed x1 -> x0, local copies, waits for them, and re-layouts: 3.22 us -> none
where the time goes in v5:
time: 221 us
  Pallas kernels  219 us (99%)
    pallas_call x1, Pallas kernels, run_backward(): pl.pallas_call(partial(backward_kernel, pages=pages, ways=ways, blocks=bl...  150 us
    pallas_call x1, Pallas kernels, run_forward(): pl.pallas_call(partial(forward_kernel, pages=pages), out_shape=[S((rows,...  40.8 us
    pallas_call x1, Pallas kernels, run_middle(): pl.pallas_call(partial(middle_kernel, tile=tile), out_shape=[S((rows, d),...  22.6 us
    pallas_call x1, Pallas kernels, run_finish(): pl.pallas_call(finish_kernel, out_shape=[S((f, d), F32), S((up, d), F32),...  6.44 us

profile of v5, /device:TPU:0, one launch (start us, length us, event | category | flops | bytes accessed | tf_op | source)
XLA Modules:
  0.0 220.9 jit_solution(2058806607196686041)
XLA Ops:
  0.7 0.6 reshape_tile.3.rates_ref
  1.3 40.8 %forward.1 = (bf16[3072,192]{1,0:T(8,128)(2,1)}, bf16[3072,192]{1,0:T(8,128)(2,1)}, bf16[3072,192]{1,0:T(8,128)(2,1)}, bf16[3072,128]{1,0:T(8,128)(2,1)}, bf16[6...) custom-call(s32[6]{0:T(128)} %len_ref.1, ...), custom_call_target="tpu_custom_call" | custom-call | tf_op jit(solution)/shard_map/forward/pallas_call | solution.py:335
  42.1 22.6 %middle.1 = (bf16[768,768]{1,0:T(8,128)(2,1)}, bf16[4,768,768]{2,1,0:T(8,128)(2,1)}, bf16[4,768,768]{2,1,0:T(8,128)(2,1)}, bf16[768,768]{1,0:T(8,128)(2,1)}, bf1...) custom-call(bf16[3072,768]{1,0:T(8,128)(2,1)} %h_ref.3, ...), custom_call_target="tpu_custom_call" | custom-call | tf_op jit(solution)/shard_map/middle/pallas_call | solution.py:448
  64.7 149.6 %backward.1 = (bf16[1792,768]{1,0:T(8,128)(2,1)}, bf16[1024,768]{1,0:T(8,128)(2,1)}, f32[768,768]{1,0:T(8,128)}) custom-call(bf16[3072,768]{1,0:T(8,128)(2,1)} %h_ref.3, bf16[960,768]{1,0:T(8,128)(2,1)} %get-tuple-element.78.wt_ref, bf16[3072,192]{1,0:T(8,128)(2,1)} %get-tuple-element.79.q_ref, bf16[3072,192]{1,0:T(8,128)(2,1)} %get-tuple-element.80.k_ref, ...), custom_call_target="tpu_custom_call" | custom-call | tf_op jit(solution)/shard_map/backward/pallas_call | solution.py:926
  214.3 6.4 %finish.1 = (f32[768,768]{1,0:T(8,128)}, f32[768,768]{1,0:T(8,128)}, f32[192,768]{1,0:T(8,128)}, f32[192,768]{1,0:T(8,128)}, f32[192,768]{1,0:T(8,128)}, /*index...) custom-call(bf16[1792,768]{1,0:T(8,128)(2,1)} %get-tuple-element.92., ...), custom_call_target="tpu_custom_call" | custom-call | tf_op jit(solution)/shard_map/finish/pallas_call | solution.py:1011
  (2 shorter events, 0.0 us)

commit v6 on v5

--- a/solution.py
+++ b/solution.py
@@ -240,7 +240,7 @@
         cat_k[head, :, :POS] = geo
         cat_k[head, :, POS:] = k_ref[:, lanes]
     count = 2 * pages
-    plan = {0: [(0, 0)], 1: [(0, 1)], 2: [(1, 0)], 3: [(0, 2)], 4: [(1, 1)], 5: [(0, 3), (0, 4)], 7: [(1, 2), (2, 1)], 8: [(1, 3), (1, 4)], 10: [(2, 0), (2, 2)], 11: [(2, 3), (2, 4)]}
+    plan = {1: [(0, 0)], 3: [(0, 1), (0, 2), (1, 0)], 5: [(0, 3), (0, 4), (1, 1)], 7: [(1, 2)], 9: [(1, 3), (1, 4), (2, 0), (2, 1)], 11: [(2, 2), (2, 3), (2, 4)]}
 
     def tick(odd):
         for at, todo in plan.items():
@@ -872,7 +872,18 @@
         when += list(range(14, 14 + ticks - len(when)))
         waves = max(achunks + 2 * (att.steps - 1), when[-1] + 1)
 
+        outs = [pltpu.make_async_copy(ag.at[pl.ds(slot * HALF, HALF)], ig_any.at[pl.ds(slot * HALF, HALF)], o_sem.at[slot]) for slot in range(pages)]
+
         def wave(w, _):
+            @pl.when(w == 8)
+            def _():
+                for slot in range(pages):
+                    r = pl.ds(slot * HALF, HALF)
+                    d_copy(1, slot).wait_recv()
+                    f_copy(slot).wait_recv()
+                    ag[r] = ag[r] + wd[1, r].astype(F32) + drecv[1, slot].astype(F32) + dxrecv[slot].astype(F32)
+                    outs[slot].start()
+
             u = -100
             for n in range(ticks):
                 u = jnp.where(w == when[n], first + n, u)
@@ -886,13 +897,6 @@
             return 0
 
         lax.fori_loop(0, waves, wave, 0)
-        outs = [pltpu.make_async_copy(ag.at[pl.ds(slot * HALF, HALF)], ig_any.at[pl.ds(slot * HALF, HALF)], o_sem.at[slot]) for slot in range(pages)]
-        for slot in range(pages):
-            r = pl.ds(slot * HALF, HALF)
-            d_copy(1, slot).wait_recv()
-            f_copy(slot).wait_recv()
-            ag[r] = ag[r] + wd[1, r].astype(F32) + drecv[1, slot].astype(F32) + dxrecv[slot].astype(F32)
-            outs[slot].start()
         for slot in range(pages):
             outs[slot].wait()
             f_copy(slot).wait_send()

time: 221 us -> 222 us (level)
  no operation moved by 1% of the time
where the time goes in v6:
time: 222 us
  Pallas kernels  220 us (99%)
    pallas_call x1, Pallas kernels, run_backward(): pl.pallas_call(partial(backward_kernel, pages=pages, ways=ways, blocks=bl...  151 us
    pallas_call x1, Pallas kernels, run_forward(): pl.pallas_call(partial(forward_kernel, pages=pages), out_shape=[S((rows,...  39.9 us
    pallas_call x1, Pallas kernels, run_middle(): pl.pallas_call(partial(middle_kernel, tile=tile), out_shape=[S((rows, d),...  22.6 us
    pallas_call x1, Pallas kernels, run_finish(): pl.pallas_call(finish_kernel, out_shape=[S((f, d), F32), S((up, d), F32),...  6.44 us

profile of v6, /device:TPU:0, one launch (start us, length us, event | category | flops | bytes accessed | tf_op | source)
XLA Modules:
  0.0 221.6 jit_solution(9321658906547410937)
XLA Ops:
  0.7 0.6 reshape_tile.3.rates_ref
  1.3 39.9 %forward.1 = (bf16[3072,192]{1,0:T(8,128)(2,1)}, bf16[3072,192]{1,0:T(8,128)(2,1)}, bf16[3072,192]{1,0:T(8,128)(2,1)}, bf16[3072,128]{1,0:T(8,128)(2,1)}, bf16[6...) custom-call(s32[6]{0:T(128)} %len_ref.1, ...), custom_call_target="tpu_custom_call" | custom-call | tf_op jit(solution)/shard_map/forward/pallas_call | solution.py:335
  41.1 22.6 %middle.1 = (bf16[768,768]{1,0:T(8,128)(2,1)}, bf16[4,768,768]{2,1,0:T(8,128)(2,1)}, bf16[4,768,768]{2,1,0:T(8,128)(2,1)}, bf16[768,768]{1,0:T(8,128)(2,1)}, bf1...) custom-call(bf16[3072,768]{1,0:T(8,128)(2,1)} %h_ref.3, ...), custom_call_target="tpu_custom_call" | custom-call | tf_op jit(solution)/shard_map/middle/pallas_call | solution.py:448
  63.8 151.2 %backward.1 = (bf16[1792,768]{1,0:T(8,128)(2,1)}, bf16[1024,768]{1,0:T(8,128)(2,1)}, f32[768,768]{1,0:T(8,128)}) custom-call(bf16[3072,768]{1,0:T(8,128)(2,1)} %h_ref.3, bf16[960,768]{1,0:T(8,128)(2,1)} %get-tuple-element.78.wt_ref, bf16[3072,192]{1,0:T(8,128)(2,1)} %get-tuple-element.79.q_ref, bf16[3072,192]{1,0:T(8,128)(2,1)} %get-tuple-element.80.k_ref, ...), custom_call_target="tpu_custom_call" | custom-call | tf_op jit(solution)/shard_map/backward/pallas_call | solution.py:930
  215.0 6.4 %finish.1 = (f32[768,768]{1,0:T(8,128)}, f32[768,768]{1,0:T(8,128)}, f32[192,768]{1,0:T(8,128)}, f32[192,768]{1,0:T(8,128)}, f32[192,768]{1,0:T(8,128)}, /*index...) custom-call(bf16[1792,768]{1,0:T(8,128)(2,1)} %get-tuple-element.92., ...), custom_call_target="tpu_custom_call" | custom-call | tf_op jit(solution)/shard_map/finish/pallas_call | solution.py:1015
  (2 shorter events, 0.0 us)

commit v7 on v5

--- a/solution.py
+++ b/solution.py
@@ -2,6 +2,7 @@
 import math
 import jax
 import jax.numpy as jnp
+import numpy as np
 from jax import lax
 from jax.experimental import pallas as pl
 from jax.experimental.pallas import tpu as pltpu
@@ -240,7 +241,7 @@
         cat_k[head, :, :POS] = geo
         cat_k[head, :, POS:] = k_ref[:, lanes]
     count = 2 * pages
-    plan = {0: [(0, 0)], 1: [(0, 1)], 2: [(1, 0)], 3: [(0, 2)], 4: [(1, 1)], 5: [(0, 3), (0, 4)], 7: [(1, 2), (2, 1)], 8: [(1, 3), (1, 4)], 10: [(2, 0), (2, 2)], 11: [(2, 3), (2, 4)]}
+    plan = {1: [(0, 0)], 3: [(0, 1), (0, 2), (1, 0)], 5: [(0, 3), (0, 4), (1, 1)], 7: [(1, 2)], 9: [(1, 3), (1, 4), (2, 0), (2, 1)], 11: [(2, 2), (2, 3), (2, 4)]}
 
     def tick(odd):
         for at, todo in plan.items():
@@ -1023,8 +1024,8 @@
     hidden_in, box_coords, page_lengths, query_weight, query_bias, key_weight, value_weight, value_bias, box_weight, box_bias, output_weight, output_bias,
     first_gain, first_shift, up_weight, up_bias, down_weight, down_bias, second_gain, second_shift, output_grad,
 ):
-    rates = jnp.power(1000.0, -jnp.arange(FREQ, dtype=F32) / FREQ)
-    rates = jnp.tile(rates, POS // FREQ).reshape(1, POS)
+    rates = np.power(1000.0, -np.arange(FREQ) / FREQ).astype(np.float32)
+    rates = jnp.asarray(np.tile(rates, POS // FREQ).reshape(1, POS))
     q, k, v, geo, p, ctx, wt, ups, *gathered = run_forward(
         page_lengths, rates, hidden_in, box_coords, box_weight, query_bias, value_bias, box_bias, up_bias,
         query_weight.T, key_weight.T, value_weight.T, output_weight, up_weight, down_weight,

time: 221 us -> 221 us (level)
  no operation moved by 1% of the time
where the time goes in v7:
time: 221 us
  Pallas kernels  220 us (100%)
    pallas_call x1, Pallas kernels, run_backward(): pl.pallas_call(partial(backward_kernel, pages=pages, ways=ways, blocks=bl...  151 us
    pallas_call x1, Pallas kernels, run_forward(): pl.pallas_call(partial(forward_kernel, pages=pages), out_shape=[S((rows,...  39.9 us
    pallas_call x1, Pallas kernels, run_middle(): pl.pallas_call(partial(middle_kernel, tile=tile), out_shape=[S((rows, d),...  22.6 us
    pallas_call x1, Pallas kernels, run_finish(): pl.pallas_call(finish_kernel, out_shape=[S((f, d), F32), S((up, d), F32),...  6.43 us

profile of v7, /device:TPU:0, one launch (start us, length us, event | category | flops | bytes accessed | tf_op | source)
XLA Modules:
  0.0 220.7 jit_solution(8087050392340358668)
XLA Ops:
  0.7 39.9 %forward.1 = (bf16[3072,192]{1,0:T(8,128)(2,1)}, bf16[3072,192]{1,0:T(8,128)(2,1)}, bf16[3072,192]{1,0:T(8,128)(2,1)}, bf16[3072,128]{1,0:T(8,128)(2,1)}, bf16[6...) custom-call(s32[6]{0:T(128)} %len_ref.1, ...), custom_call_target="tpu_custom_call" | custom-call | tf_op jit(solution)/shard_map/forward/pallas_call | solution.py:336
  40.6 22.6 %middle.1 = (bf16[768,768]{1,0:T(8,128)(2,1)}, bf16[4,768,768]{2,1,0:T(8,128)(2,1)}, bf16[4,768,768]{2,1,0:T(8,128)(2,1)}, bf16[768,768]{1,0:T(8,128)(2,1)}, bf1...) custom-call(bf16[3072,768]{1,0:T(8,128)(2,1)} %h_ref.3, ...), custom_call_target="tpu_custom_call" | custom-call | tf_op jit(solution)/shard_map/middle/pallas_call | solution.py:449
  63.3 150.9 %backward.1 = (bf16[1792,768]{1,0:T(8,128)(2,1)}, bf16[1024,768]{1,0:T(8,128)(2,1)}, f32[768,768]{1,0:T(8,128)}) custom-call(bf16[3072,768]{1,0:T(8,128)(2,1)} %h_ref.3, bf16[960,768]{1,0:T(8,128)(2,1)} %get-tuple-element.78.wt_ref, bf16[3072,192]{1,0:T(8,128)(2,1)} %get-tuple-element.79.q_ref, bf16[3072,192]{1,0:T(8,128)(2,1)} %get-tuple-element.80.k_ref, ...), custom_call_target="tpu_custom_call" | custom-call | tf_op jit(solution)/shard_map/backward/pallas_call | solution.py:927
  214.1 6.4 %finish.1 = (f32[768,768]{1,0:T(8,128)}, f32[768,768]{1,0:T(8,128)}, f32[192,768]{1,0:T(8,128)}, f32[192,768]{1,0:T(8,128)}, f32[192,768]{1,0:T(8,128)}, /*index...) custom-call(bf16[1792,768]{1,0:T(8,128)(2,1)} %get-tuple-element.92., ...), custom_call_target="tpu_custom_call" | custom-call | tf_op jit(solution)/shard_map/finish/pallas_call | solution.py:1012
